TPU v7x, 32 devices: a whole 2x2x4 slice. The times are simulated.
32 devices in a mesh: gx: 16 (over z, y, x), gy: 2 (over core).
Axes of the slice: x: 2, y: 2, z: 4, core: 2. Of those that a mesh axis runs over, the one named last changes fastest.
Arguments:
- snapshot: bfloat16 [3, 128, 32, 1024], P(None, 'gx', 'gy'), may hold values from -6 to 6
- basis: bfloat16 [3, 16, 4, 128, 512], P(None, 'gx', 'gy'), may hold values from -3000 to 3000
- taps: bfloat16 [3, 17], replicated, may hold values from 0.099609375 to 1
Outputs:
- new_modes: bfloat16 [3, 16, 4, 128, 512], P(None, 'gx', 'gy')
- new_mode: float32 [3, 16, 4, 128], P(None, 'gx', 'gy')
- factor: float32 [513, 513], replicated
All inputs are finite; a program needn't handle non-finite values.
Results may differ from a plain program's by a relative error of at most 0.0012.
The roundings to bfloat16 on the way count: a program that leaves them out, or rounds other values in their place, can miss the bound.
Values sent between devices are 32-bit elements; how exact they have to be, the bound alone decides.
No kernel may reach another device: no remote copies, remote signals or barrier semaphores. Data moves between devices by JAX's collectives and lax.ppermute only.
A program may use at most 64 MiB of HBM per device.

v0:
```python
import jax
import jax.numpy as jnp
from jax import lax
from jax.sharding import PartitionSpec as P

STRIDE = 8


def padded(block, sides, width, periodic):
    for axis, dim in sides:
        count = lax.axis_size(axis)
        forward = [(i, i + 1) for i in range(count - 1)]
        if periodic:
            forward.append((count - 1, 0))
        backward = [(target, source) for source, target in forward]
        low = lax.ppermute(
            lax.slice_in_dim(block, block.shape[dim] - width, None, axis=dim), axis, forward
        )
        high = lax.ppermute(lax.slice_in_dim(block, 0, width, axis=dim), axis, backward)
        block = jnp.concatenate([low, block, high], axis=dim)
    return block


def band(taps_row, length, out_len, shift, wrap):
    rows = jnp.arange(length, dtype=jnp.int32)[:, None]
    cols = jnp.arange(out_len, dtype=jnp.int32)[None, :]
    lag = rows - STRIDE * cols + shift
    if wrap:
        lag = lag % length
    hits = lag[:, :, None] == jnp.arange(2 * STRIDE + 1, dtype=jnp.int32)[None, None, :]
    return jnp.sum(jnp.where(hits, taps_row[None, None, :], jnp.zeros((), taps_row.dtype)), axis=-1)


def local(snapshot, basis, taps):
    comps, cells_x, cells_y, cells_z = snapshot.shape
    modes = basis.shape[-1]
    flat_rows = basis.reshape(-1, modes)
    total = flat_rows.shape[0] * lax.axis_size("gx") * lax.axis_size("gy")
    mode_part = lax.psum(
        jnp.einsum("rk,rj->kj", flat_rows, flat_rows, preferred_element_type=jnp.float32),
        ("gx", "gy"),
    )
    matrix_z = band(taps[2], cells_z, cells_z // STRIDE, STRIDE, True)
    along_z = jnp.dot(snapshot.reshape(-1, cells_z), matrix_z, preferred_element_type=jnp.float32)
    along_z = along_z.reshape(comps, cells_x, cells_y, cells_z // STRIDE)
    padded_y = padded(along_z, (("gy", 2),), STRIDE, False)
    matrix_y = band(taps[1], cells_y + 2 * STRIDE, cells_y // STRIDE, 0, False).astype(jnp.float32)
    along_y = jnp.einsum("cxyz,yf->cxfz", padded_y, matrix_y, precision=lax.Precision.HIGHEST)
    padded_x = padded(along_y, (("gx", 1),), STRIDE, True)
    matrix_x = band(taps[0], cells_x + 2 * STRIDE, cells_x // STRIDE, 0, False).astype(jnp.float32)
    along_x = jnp.einsum("cxyz,xf->cfyz", padded_x, matrix_x, precision=lax.Precision.HIGHEST)
    filtered = along_x.astype(jnp.bfloat16).reshape(-1)
    stack = jnp.concatenate([flat_rows, filtered[:, None]], axis=1)
    fresh_wide = filtered.astype(jnp.float32)
    cross, square = lax.psum(
        (
            jnp.einsum("rk,r->k", flat_rows, filtered, preferred_element_type=jnp.float32),
            jnp.sum(fresh_wide * fresh_wide),
        ),
        ("gx", "gy"),
    )
    upper_rows = jnp.concatenate([mode_part, cross[:, None]], axis=1)
    last_row = jnp.concatenate([cross, square[None]])[None, :]
    gram = jnp.concatenate([upper_rows, last_row], axis=0)
    gram = gram / total
    lower = jnp.linalg.cholesky(gram)
    solved = lax.linalg.triangular_solve(
        lower, stack.astype(jnp.float32), left_side=False, lower=True, transpose_a=True
    )
    new_modes = solved[:, :modes].astype(jnp.bfloat16).reshape(basis.shape)
    new_mode = solved[:, modes].reshape(basis.shape[:-1])
    return (new_modes, new_mode, lower.T)


def solution(mesh):
    in_specs = (P(None, "gx", "gy", None), P(None, "gx", "gy", None, None), P())
    out_specs = (P(None, "gx", "gy", None, None), P(None, "gx", "gy", None), P())
    return jax.shard_map(local, mesh=mesh, in_specs=in_specs, out_specs=out_specs, check_vma=False)
```

profile of v0, /device:TPU:0, one launch (start us, length us, event | category | flops | bytes accessed | tf_op | source)
XLA Modules:
  0.0 347.1 jit_solution(4015166581742099439)
XLA Ops:
  9.8 2.4 collective-permute-start
  15.7 2.4 collective-permute-start.2
  18.1 4.1 %collective-permute-start.3 = (f32[3,8,2,128]{3,2,1,0:T(2,128)S(1)}, f32[3,8,2,128]{3,2,1,0:T(2,128)S(1)}, u32[]{:S(2)}, u32[]{:S(2)}) collective-permute-start(f32[3,8,2,128]{3,2,1,0:T(2,128)S(1)} %convolution_bitcast_fusion.2), channel_id=1, source_target_pairs={{2,0},{4,2},{6,4},{8,6},{10,8},{12,10},{14,12},{16,14},{18,16},{20... | collective-permute-start | bytes 73736 | tf_op jit(solution)/shard_map/ppermute | solution.py:19
  24.9 41.3 %all-reduce.3 = (f32[1]{0:T(128)}, f32[512]{0:T(512)S(1)}) all-reduce(f32[1]{0:T(128)} %bitcast.19, f32[512]{0:T(512)S(1)} %bitcast.151), channel_id=1, replica_groups=mesh['gx'=16,'gy'=2] {'gx','gy'}, use_global_device_ids=true, to_apply=%region_6.7 | all-reduce | flops 513 | bytes 4104 | tf_op jit(solution)/shard_map/psum | solution.py:55
  67.3 81.6 %all-reduce.6.cloned.1.call-done = f32[512,512]{0,1:T(8,128)} async-done(((f32[512,512]{0,1:T(8,128)}), f32[512,512]{0,1:T(8,128)}) %all-reduce.6.cloned.1.call-update) | async-done | bytes 1048592 | tf_op jit(solution)/shard_map/psum | solution.py:39
  148.9 2.4 maximum_multiply_fusion
  156.1 11.7 %cholesky.131 = f32[128,128]{1,0:T(8,128)S(1)} custom-call(f32[128,128]{1,0:T(8,128)S(1)} %cholesky.333), custom_call_target="Cholesky" | custom-call | tf_op jit(solution)/shard_map/jit(cholesky)/cholesky | solution.py:66
  168.0 9.8 %custom-call.35 = f32[1,128,128]{1,2,0:T(8,128)S(1)} custom-call(f32[1,128,128]{2,1,0:T(8,128)S(1)} %get-tuple-element.51), custom_call_target="InvertDiagBlocksLowerTriangular" | custom-call | tf_op jit(solution)/shard_map/jit(cholesky)/cholesky | solution.py:66
  180.6 11.7 %cholesky.264 = f32[128,128]{1,0:T(8,128)S(1)} custom-call(f32[128,128]{1,0:T(8,128)S(1)} %cholesky.337), custom_call_target="Cholesky" | custom-call | tf_op jit(solution)/shard_map/jit(cholesky)/cholesky | solution.py:66
  192.4 9.9 %custom-call.36 = f32[1,128,128]{1,2,0:T(8,128)S(1)} custom-call(f32[1,128,128]{2,1,0:T(8,128)S(1)} %get-tuple-element.48), custom_call_target="InvertDiagBlocksLowerTriangular" | custom-call | tf_op jit(solution)/shard_map/jit(cholesky)/cholesky | solution.py:66
  204.0 11.7 %cholesky.285 = f32[128,128]{1,0:T(8,128)S(1)} custom-call(f32[128,128]{1,0:T(8,128)S(1)} %cholesky.342), custom_call_target="Cholesky" | custom-call | tf_op jit(solution)/shard_map/jit(cholesky)/cholesky | solution.py:66
  215.8 9.8 %custom-call.37 = f32[1,128,128]{1,2,0:T(8,128)S(1)} custom-call(f32[1,128,128]{2,1,0:T(8,128)S(1)} %get-tuple-element.45), custom_call_target="InvertDiagBlocksLowerTriangular" | custom-call | tf_op jit(solution)/shard_map/jit(cholesky)/cholesky | solution.py:66
  227.1 11.9 %cholesky.304 = f32[128,128]{1,0:T(8,128)S(1)} custom-call(f32[128,128]{1,0:T(8,128)S(1)} %cholesky.347), custom_call_target="Cholesky" | custom-call | tf_op jit(solution)/shard_map/jit(cholesky)/cholesky | solution.py:66
  239.1 9.8 %custom-call.38 = f32[1,128,128]{1,2,0:T(8,128)S(1)} custom-call(f32[1,128,128]{2,1,0:T(8,128)S(1)} %get-tuple-element.42), custom_call_target="InvertDiagBlocksLowerTriangular" | custom-call | tf_op jit(solution)/shard_map/jit(cholesky)/cholesky | solution.py:66
  258.1 11.3 %while.1 = (s32[]{:T(128)}, f32[513,513]{1,0:T(8,128)}, s32[4,2]{0,1:T(2,128)S(1)}, f32[4,128,128]{2,1,0:T(8,128)S(1)}, s32[]{:T(128)}) while((s32[]{:T(128)}, f32[513,513]{1,0:T(8,128)}, s32[4,2]{0,1:T(2,128)S(1)}, f32[4,128,128]{2,1,0:T(8,128)S(1)}, s32[]{:T(128)}) %tuple.51), condition=%wide.while_cond, body=%wide.while_body.sunk | while | flops 2 | bytes 131181 | solution.py:67
  258.7 2.2 bitcast_dynamic-update-slice_fusion.2
  261.5 2.2 bitcast_dynamic-update-slice_fusion.2
  264.4 2.2 bitcast_dynamic-update-slice_fusion.2
  267.2 2.2 bitcast_dynamic-update-slice_fusion.2
  270.2 49.1 %custom-call.39 = f32[5,128,128]{1,2,0:T(8,128)S(1)} custom-call(f32[5,128,128]{2,1,0:T(8,128)S(1)} %pad_maximum_fusion.1), custom_call_target="InvertDiagBlocksLowerTriangular" | custom-call | tf_op jit(solution)/shard_map/triangular_solve | solution.py:67
  323.3 2.3 convolution_subtract_fusion.2
  326.9 3.0 convolution_subtract_fusion
  329.9 2.0 fusion.72
  332.8 1.9 fusion.17
  (101 shorter events, 40.7 us)
Async XLA Ops:
  7.2 2.1 copy-start
  7.2 141.7 %all-reduce.6.cloned.1.call-start = ((), (), s32[]{:S(2)}) async-start(), calls=%async_computation | async-start | bytes 2097152 | tf_op jit(solution)/shard_map/psum | solution.py:39
  8.3 5.2 %copy-start.1 = (bf16[3,1,2,128,512]{4,3,2,1,0:T(8,128)(2,1)S(1)}, bf16[3,1,2,128,512]{4,3,2,1,0:T(8,128)(2,1)}, u32[]{:S(2)}) copy-start(bf16[3,1,2,128,512]{4,3,2,1,0:T(8,128)(2,1)} %param.4) | copy-start | bytes 2359300
  9.8 5.7 %collective-permute-start = (f32[3,8,8,128]{3,2,1,0:T(8,128)S(1)}, f32[3,8,8,128]{3,2,1,0:T(8,128)S(1)}, u32[]{:S(2)}, u32[]{:S(2)}) collective-permute-start(f32[3,8,8,128]{3,2,1,0:T(8,128)S(1)} %get-tuple-element.39), channel_id=1, source_target_pairs={{0,1},{2,3},{4,5},{6,7},{8,9},{10,11},{12,13},{14,15},{16,17},{18,... | collective-permute-start | bytes 294920 | tf_op jit(solution)/shard_map/ppermute | solution.py:16
  12.2 3.3 collective-permute-start.1
  15.7 8.2 %collective-permute-start.2 = (f32[3,8,2,128]{3,2,1,0:T(2,128)S(1)}, f32[3,8,2,128]{3,2,1,0:T(2,128)S(1)}, u32[]{:S(2)}, u32[]{:S(2)}) collective-permute-start(f32[3,8,2,128]{3,2,1,0:T(2,128)S(1)} %convolution_bitcast_fusion.2), channel_id=1, source_target_pairs={{0,2},{2,4},{4,6},{6,8},{8,10},{10,12},{12,14},{14,16},{16,18},{18... | collective-permute-start | bytes 73736 | tf_op jit(solution)/shard_map/ppermute | solution.py:16
  18.1 5.8 %collective-permute-start.3 = (f32[3,8,2,128]{3,2,1,0:T(2,128)S(1)}, f32[3,8,2,128]{3,2,1,0:T(2,128)S(1)}, u32[]{:S(2)}, u32[]{:S(2)}) collective-permute-start(f32[3,8,2,128]{3,2,1,0:T(2,128)S(1)} %convolution_bitcast_fusion.2), channel_id=1, source_target_pairs={{2,0},{4,2},{6,4},{8,6},{10,8},{12,10},{14,12},{16,14},{18,16},{20... | collective-permute-start | bytes 73736 | tf_op jit(solution)/shard_map/ppermute | solution.py:19
  154.5 1.1 copy-start.4
  255.8 2.3 copy-start.7
  257.0 1.1 copy-start.3
  319.4 6.2 %copy-start.8 = (f32[5,128,128]{1,2,0:T(8,128)}, f32[5,128,128]{1,2,0:T(8,128)S(1)}, u32[]{:S(2)}) copy-start(f32[5,128,128]{1,2,0:T(8,128)S(1)} %custom-call.39) | copy-start | bytes 983044
  334.7 2.7 copy-start.2
  337.5 1.6 copy-start.5
  337.5 1.6 copy-start.6
Sparse Core Ops, SparseCore 0:
  15.2 133.6 all-reduce.5
where the time goes:
time: 351 us; the launch traced here: 347 us
  other arithmetic  149 us (42%)
  waiting for transfers between devices  83.3 us (24%)
  blocking collectives  41.3 us (12%)
  local copies, waits for them, and re-layouts  22.5 us (6%)
  matrix products  22.2 us (6%)
  between operations  18.6 us (5%)
  starting transfers between devices  10.2 us (3%)
    another operation x16, other arithmetic, local(): lower = jnp.linalg.cholesky(gram)  89.1 us
    psum x1, waiting for transfers between devices, local(): lax.psum(jnp.einsum('rk,rj->kj', flat_rows, flat_rows, preferred_element_...  81.6 us
    another operation x8, other arithmetic, local(): lax.linalg.triangular_solve(lower, stack.astype(jnp.float32), left_side=F...  52 us
    psum x1, blocking collectives, local(): lax.psum((jnp.einsum('rk,r->k', flat_rows, filtered, preferred_element_ty...  41.3 us
    another operation x8, matrix products, local(): lax.linalg.triangular_solve(lower, stack.astype(jnp.float32), left_side=F...  13.5 us
    another operation x12, local copies, waits for them, and re-layouts  11.3 us
  transfers between devices with their start and end apart: 5, of which 2 were waited for; matrix products, arithmetic and copies ran while one was open for 1% of the time, Pallas kernels for 0%

commit v1 on v0

v1 whole, which is shorter than its diff:
```python
import jax
import jax.numpy as jnp
from jax import lax
from jax.experimental import pallas as pl
from jax.experimental.pallas import tpu as pltpu
from jax.sharding import PartitionSpec as P

STRIDE = 8
TILE = 128
PIVOTS = 32
F32 = jnp.float32
BF16 = jnp.bfloat16
HIGHEST = lax.Precision.HIGHEST


def padded(block, sides, width, periodic):
    for axis, dim in sides:
        count = lax.axis_size(axis)
        forward = [(i, i + 1) for i in range(count - 1)]
        if periodic:
            forward.append((count - 1, 0))
        backward = [(target, source) for source, target in forward]
        low = lax.ppermute(
            lax.slice_in_dim(block, block.shape[dim] - width, None, axis=dim), axis, forward
        )
        high = lax.ppermute(lax.slice_in_dim(block, 0, width, axis=dim), axis, backward)
        block = jnp.concatenate([low, block, high], axis=dim)
    return block


def band(taps_row, length, out_len, shift, wrap):
    rows = jnp.arange(length, dtype=jnp.int32)[:, None]
    cols = jnp.arange(out_len, dtype=jnp.int32)[None, :]
    lag = rows - STRIDE * cols + shift
    if wrap:
        lag = lag % length
    hits = lag[:, :, None] == jnp.arange(2 * STRIDE + 1, dtype=jnp.int32)[None, None, :]
    return jnp.sum(jnp.where(hits, taps_row[None, None, :], jnp.zeros((), taps_row.dtype)), axis=-1)


def hops(axes):
    found = []
    for axis in axes:
        size = lax.axis_size(axis)
        if size & (size - 1):
            return None
        bit = 1
        while bit < size:
            pairs = [(i, i ^ bit) for i in range(size)]
            upper = (lax.axis_index(axis) & bit) != 0
            found.append((axis, pairs, upper))
            bit *= 2
    return found


def total_of(block, axes):
    exchanges = hops(axes)
    if exchanges is None:
        return lax.psum(block, axes)
    halved = []
    for axis, pairs, upper in exchanges:
        rows = block.shape[0]
        if rows % 16 == 0:
            low, high = block[: rows // 2], block[rows // 2 :]
            sent = jnp.where(upper, low, high)
            kept = jnp.where(upper, high, low)
            block = kept + lax.ppermute(sent, axis, pairs)
            halved.append((axis, pairs, upper))
        else:
            block = block + lax.ppermute(block, axis, pairs)
    for axis, pairs, upper in reversed(halved):
        other = lax.ppermute(block, axis, pairs)
        block = jnp.concatenate(
            [jnp.where(upper, other, block), jnp.where(upper, block, other)], axis=0
        )
    return block


def small_total(block, axes):
    exchanges = hops(axes)
    if exchanges is None:
        return lax.psum(block, axes)
    for axis, pairs, _ in exchanges:
        block = block + lax.ppermute(block, axis, pairs)
    return block


def contract_rows(a, b, precision=None):
    return lax.dot_general(
        a, b, (((0,), (0,)), ((), ())), precision=precision, preferred_element_type=F32
    )


def contract_lanes(a, b, precision=None):
    return lax.dot_general(
        a, b, (((1,), (1,)), ((), ())), precision=precision, preferred_element_type=F32
    )


def gram_kernel(rows_ref, out_ref):
    modes = rows_ref.shape[1]
    at = 0
    for p in range(modes // TILE):
        left = rows_ref[:, TILE * p : TILE * (p + 1)]
        part = contract_rows(left, rows_ref[:, TILE * p :])
        for c in range(modes // TILE - p):
            out_ref[at : at + TILE, :] = part[:, TILE * c : TILE * (c + 1)]
            at += TILE


def local_gram(rows):
    count, modes = rows.shape
    chunks = modes // TILE
    blocks = chunks * (chunks + 1) // 2
    return pl.pallas_call(
        gram_kernel,
        out_shape=jax.ShapeDtypeStruct((blocks * TILE, TILE), F32),
        cost_estimate=pl.CostEstimate(
            flops=2 * count * modes * modes, bytes_accessed=4 * blocks * TILE * TILE, transcendentals=0
        ),
        name="gram",
    )(rows)


def factor_blocks(work, scaled, upper):
    modes = work.shape[0]
    chunks = modes // TILE
    groups = PIVOTS // 8
    lane = lax.broadcasted_iota(jnp.int32, (8, TILE), 1)
    row = lax.broadcasted_iota(jnp.int32, (8, TILE), 0)
    scale_blocks = []
    for p in range(chunks):
        base = p * TILE
        for j in range(TILE // PIVOTS):
            first = PIVOTS * j
            top = base + first
            rows = [
                [work[top + 8 * g : top + 8 * g + 8, TILE * c : TILE * (c + 1)] for c in range(chunks)]
                for g in range(groups)
            ]
            cols = [
                [
                    jnp.broadcast_to(rows[g][p][:, first + k : first + k + 1], (8, TILE))
                    if g >= k // 8
                    else None
                    for g in range(groups)
                ]
                for k in range(PIVOTS)
            ]
            unit = [jnp.where(lane == first + 8 * g + row, 1.0, 0.0).astype(F32) for g in range(groups)]
            inverse = [jnp.zeros((8, TILE), F32) for _ in range(groups)]
            scale = [jnp.zeros((8, TILE), F32) for _ in range(groups)]
            for k in range(PIVOTS):
                own, sub = k // 8, k % 8
                pivot = cols[k][own][sub : sub + 1, :]
                recip = 1.0 / pivot
                inverse[own] = jnp.where(row == sub, recip, inverse[own])
                scale[own] = jnp.where(row == sub, lax.rsqrt(pivot), scale[own])
                mult = {g: cols[k][g] * recip for g in range(own, groups)}
                for later in range(k + 1, PIVOTS):
                    factor = cols[k][later // 8][later % 8 : later % 8 + 1, :]
                    for g in range(later // 8, groups):
                        cols[later][g] = cols[later][g] - mult[g] * factor
                mult[own] = jnp.where(row > sub, mult[own], 0.0)
                for c in range(chunks):
                    pivot_row = rows[own][c][sub : sub + 1, :]
                    for g in range(own, groups):
                        rows[g][c] = rows[g][c] - mult[g] * pivot_row
                pivot_row = unit[own][sub : sub + 1, :]
                for g in range(own, groups):
                    unit[g] = unit[g] - mult[g] * pivot_row
            inside = (lane >= first) & (lane < first + PIVOTS)
            for g in range(groups):
                where = slice(top + 8 * g, top + 8 * g + 8)
                for c in range(chunks):
                    cut = slice(TILE * c, TILE * (c + 1))
                    if c < p:
                        upper[where, cut] = jnp.zeros((8, TILE), F32)
                    elif c == p:
                        upper[where, cut] = jnp.where(
                            lane >= first + 8 * g + row, rows[g][c] * scale[g], 0.0
                        )
                    else:
                        upper[where, cut] = rows[g][c] * scale[g]
                    if c >= p:
                        scaled[first + 8 * g : first + 8 * g + 8, cut] = rows[g][c] * inverse[g]
                    work[where, cut] = jnp.where(inside, unit[g], rows[g][c]) if c == p else rows[g][c]
                scale_blocks.append(scale[g])
            end = first + PIVOTS
            if end < TILE:
                change = contract_rows(
                    scaled[first:end, base : base + TILE], work[top : top + PIVOTS, :], HIGHEST
                )
                wide = lax.broadcasted_iota(jnp.int32, (TILE - end, TILE), 1)
                for c in range(chunks):
                    cut = slice(TILE * c, TILE * (c + 1))
                    old = work[base + end : base + TILE, cut]
                    if c == p:
                        old = jnp.where((wide >= first) & (wide < end), 0.0, old)
                    work[base + end : base + TILE, cut] = old - change[end:, cut]
        block_lane = lax.broadcasted_iota(jnp.int32, (TILE, TILE), 1)
        block_row = lax.broadcasted_iota(jnp.int32, (TILE, TILE), 0)
        own = slice(base, base + TILE)
        work[own, own] = jnp.where(block_lane <= block_row, work[own, own], 0.0)
        for i in range(p + 1, chunks):
            below = slice(TILE * i, TILE * (i + 1))
            left = scaled[:, below]
            inverse_part = contract_rows(left, work[own, : base + TILE], HIGHEST)
            if p:
                work[below, :base] = work[below, :base] - inverse_part[:, :base]
            work[below, own] = -inverse_part[:, base:]
            gram_part = contract_rows(left, work[own, TILE * i :], HIGHEST)
            work[below, TILE * i :] = work[below, TILE * i :] - gram_part
    return scale_blocks


def solve_kernel(
    total_ref, cross_ref, fresh_ref, rows_ref, modes_ref, mode_ref, factor_ref, work, scaled, *, total
):
    modes = work.shape[0]
    chunks = modes // TILE
    at = 0
    for p in range(chunks):
        for c in range(p, chunks):
            work[TILE * p : TILE * (p + 1), TILE * c : TILE * (c + 1)] = (
                total_ref[at : at + TILE, :] * (1.0 / total)
            )
            at += TILE
    scales = factor_blocks(work, scaled, factor_ref)
    for g, scale in enumerate(scales):
        where = slice(8 * g, 8 * g + 8)
        for c in range(8 * g // TILE + 1):
            work[where, TILE * c : TILE * (c + 1)] = work[where, TILE * c : TILE * (c + 1)] * scale
    cross = [cross_ref[c : c + 1, :] * (1.0 / total) for c in range(chunks)]
    square = cross_ref[chunks : chunks + 1, :] * (1.0 / total)
    projected = []
    for p in range(chunks):
        own = slice(TILE * p, TILE * (p + 1))
        width = TILE * (p + 1)
        known = work[own, :width]
        first = known.astype(BF16)
        second = (known - first.astype(F32)).astype(BF16)
        left = rows_ref[:, :width]
        solved = contract_lanes(left, first) + contract_lanes(left, second)
        modes_ref[:, own] = solved.astype(BF16)
        line = jnp.concatenate(cross[: p + 1], axis=1)
        projected.append(contract_lanes(jnp.broadcast_to(line, (8, width)), known, HIGHEST))
        column = sum(known[:, TILE * c : TILE * (c + 1)] * cross[c] for c in range(p + 1))
        factor_ref[own, modes : modes + 1] = jnp.sum(column, axis=1, keepdims=True)
    norm = sum(jnp.sum(part * part, axis=1, keepdims=True) for part in projected)
    gap = square[:, :1] - norm[:1, :]
    last = jnp.sqrt(gap)
    share = jnp.zeros((8, modes), F32)
    back = []
    for c in range(chunks):
        own = slice(TILE * c, TILE * (c + 1))
        part = jnp.zeros((8, TILE), F32)
        for p in range(c, chunks):
            part = part + jnp.dot(
                projected[p],
                work[TILE * p : TILE * (p + 1), own],
                precision=HIGHEST,
                preferred_element_type=F32,
            )
        back.append(part)
    share = jnp.concatenate(back, axis=1)
    first = share.astype(BF16)
    second = (share - first.astype(F32)).astype(BF16)
    covered = contract_lanes(first, rows_ref[...]) + contract_lanes(second, rows_ref[...])
    mode_ref[...] = (fresh_ref[...] - covered[:1, :]) / last
    factor_ref[modes : modes + 1, :modes] = jnp.zeros((1, modes), F32)
    factor_ref[modes : modes + 1, modes : modes + 1] = last


def solve(total_gram, total_cross, fresh, rows, total):
    count, modes = rows.shape
    return pl.pallas_call(
        lambda *refs: solve_kernel(*refs, total=total),
        out_shape=(
            jax.ShapeDtypeStruct((count, modes), BF16),
            jax.ShapeDtypeStruct((1, count), F32),
            jax.ShapeDtypeStruct((modes + 1, modes + 1), F32),
        ),
        scratch_shapes=[pltpu.VMEM((modes, modes), F32), pltpu.VMEM((TILE, modes), F32)],
        cost_estimate=pl.CostEstimate(
            flops=4 * count * modes * modes, bytes_accessed=8 * modes * modes, transcendentals=modes
        ),
        name="solve",
    )(total_gram, total_cross, fresh, rows)


def local(snapshot, basis, taps):
    comps, cells_x, cells_y, cells_z = snapshot.shape
    modes = basis.shape[-1]
    axes = ("gy", "gx")
    flat_rows = basis.reshape(-1, modes)
    total = flat_rows.shape[0] * lax.axis_size("gx") * lax.axis_size("gy")
    gram = total_of(local_gram(flat_rows), axes)
    matrix_z = band(taps[2], cells_z, cells_z // STRIDE, STRIDE, True)
    along_z = jnp.dot(snapshot.reshape(-1, cells_z), matrix_z, preferred_element_type=F32)
    along_z = along_z.reshape(comps, cells_x, cells_y, cells_z // STRIDE)
    padded_y = padded(along_z, (("gy", 2),), STRIDE, False)
    matrix_y = band(taps[1], cells_y + 2 * STRIDE, cells_y // STRIDE, 0, False).astype(F32)
    along_y = jnp.einsum("cxyz,yf->cxfz", padded_y, matrix_y, precision=HIGHEST)
    padded_x = padded(along_y, (("gx", 1),), STRIDE, True)
    matrix_x = band(taps[0], cells_x + 2 * STRIDE, cells_x // STRIDE, 0, False).astype(F32)
    along_x = jnp.einsum("cxyz,xf->cfyz", padded_x, matrix_x, precision=HIGHEST)
    fresh = lax.reduce_precision(along_x, exponent_bits=8, mantissa_bits=7).reshape(-1)
    filtered = fresh.astype(BF16)
    cross = jnp.einsum("rk,r->k", flat_rows, filtered, preferred_element_type=F32)
    square = jnp.full((TILE,), jnp.sum(fresh * fresh), F32)
    sums = jnp.concatenate([cross, square]).reshape(-1, TILE)
    sums = small_total(sums, axes)
    new_modes, new_mode, factor = solve(gram, sums, fresh.reshape(1, -1), flat_rows, total)
    return (new_modes.reshape(basis.shape), new_mode.reshape(basis.shape[:-1]), factor)


def solution(mesh):
    in_specs = (P(None, "gx", "gy", None), P(None, "gx", "gy", None, None), P())
    out_specs = (P(None, "gx", "gy", None, None), P(None, "gx", "gy", None), P())
    return jax.shard_map(local, mesh=mesh, in_specs=in_specs, out_specs=out_specs, check_vma=False)
```

time: 351 us -> 95.6 us (0.27); the launches traced: 347 us -> 95.4 us
  other arithmetic: 149 us -> 6.88 us
  waiting for transfers between devices: 83.3 us -> 41.8 us
  blocking collectives: 41.3 us -> 0 us
  Pallas kernels: 0 us -> 24.5 us
  local copies, waits for them, and re-layouts: 22.5 us -> 0.83 us
  matrix products: 22.2 us -> 0.99 us
  between operations: 18.6 us -> 1.01 us
  starting transfers between devices: 10.2 us -> 19.5 us
    another operation x24 -> x0, other arithmetic: 141 us -> none  [the longest x16 89.1 us: local(): lower = jnp.linalg.cholesky(gram)]
    psum x1 -> x0, waiting for transfers between devices: 81.6 us -> none  [local(): lax.psum(jnp.einsum('rk,rj->kj', flat_rows, flat_rows, preferred_element_...]
    psum x1 -> x0, blocking collectives: 41.3 us -> none  [local(): lax.psum((jnp.einsum('rk,r->k', flat_rows, filtered, preferred_element_ty...]
    ppermute x0 -> x15, waiting for transfers between devices: none -> 36 us  [the longest x5 15.3 us: small_total(): block = block + lax.ppermute(block, axis, pairs)]
    pallas_call x0 -> x2, Pallas kernels: none -> 24.5 us  [the longest x1 21.9 us: solve(): pl.pallas_call(lambda *refs: solve_kernel(*refs, total=total), out_shape=...]
    another operation x15 -> x0, matrix products: 19.7 us -> none  [the longest x8 13.5 us: local(): lax.linalg.triangular_solve(lower, stack.astype(jnp.float32), left_side=F...]
    another operation x30 -> x0, local copies, waits for them, and re-layouts: 16.5 us -> none
    ppermute x0 -> x15, starting transfers between devices: none -> 12.9 us  [the longest x5 10.7 us: total_of(): block = kept + lax.ppermute(sent, axis, pairs)]
  transfers between devices with their start and end apart: 5 -> 19, of which waited for: 2 -> 11; matrix products, arithmetic and copies ran while one was open for 1% -> 7% of each run, Pallas kernels for 0% -> 0%
where the time goes in v1:
time: 95.6 us; the launch traced here: 95.4 us
  waiting for transfers between devices  41.8 us (44%)
  Pallas kernels  24.5 us (26%)
  starting transfers between devices  19.5 us (20%)
  other arithmetic  6.88 us (7%)
  between operations  1.01 us (1%)
  matrix products  0.99 us (1%)
    pallas_call x1, Pallas kernels, solve(): pl.pallas_call(lambda *refs: solve_kernel(*refs, total=total), out_shape=...  21.9 us
    ppermute x5, waiting for transfers between devices, small_total(): block = block + lax.ppermute(block, axis, pairs)  15.3 us
    ppermute x5, waiting for transfers between devices, total_of(): other = lax.ppermute(block, axis, pairs)  11.4 us
    ppermute x5, starting transfers between devices, total_of(): block = kept + lax.ppermute(sent, axis, pairs)  10.7 us
    ppermute x5, waiting for transfers between devices, total_of(): block = kept + lax.ppermute(sent, axis, pairs)  9.29 us
    ppermute x2, waiting for transfers between devices, padded(): lax.ppermute(lax.slice_in_dim(block, block.shape[dim] - width, None, axis...  5.75 us
    ppermute x2, starting transfers between devices, padded(): lax.ppermute(lax.slice_in_dim(block, 0, width, axis=dim), axis, backward)  4.57 us
    pallas_call x1, Pallas kernels, local_gram(): pl.pallas_call(gram_kernel, out_shape=jax.ShapeDtypeStruct((blocks * TILE...  2.55 us
  transfers between devices with their start and end apart: 19, of which 11 were waited for; matrix products, arithmetic and copies ran while one was open for 7% of the time, Pallas kernels for 0%

profile of v1, /device:TPU:0, one launch (start us, length us, event | category | flops | bytes accessed | tf_op | source)
XLA Modules:
  0.0 95.4 jit_solution(2680784852072318774)
XLA Ops:
  0.7 2.5 %gram.1 = f32[1280,128]{1,0:T(8,128)} custom-call(bf16[768,512]{1,0:T(8,128)(2,1)} %bitcast.49), custom_call_target="tpu_custom_call" | custom-call | flops 402653184 | bytes 655360 | tf_op jit(solution)/shard_map/gram/pallas_call | solution.py:115
  3.2 1.1 %slice_select_fusion = f32[640,128]{1,0:T(8,128)S(1)} fusion(f32[1280,128]{1,0:T(8,128)} %gram.1, pred[]{:T(512)S(6)} %ne.31), kind=kLoop, calls=%fused_computation.19 | loop fusion | flops 81920 | bytes 983041 | tf_op jit(solution)/shard_map/jit(_where)/select_n | solution.py:65
  5.2 0.9 fusion.1
  6.6 1.9 %collective-permute-start.10 = (f32[3,8,8,128]{3,2,1,0:T(8,128)S(1)}, f32[3,8,8,128]{3,2,1,0:T(8,128)S(1)}, u32[]{:S(2)}, u32[]{:S(2)}) collective-permute-start(f32[3,8,8,128]{3,2,1,0:T(8,128)S(1)} %get-tuple-element.22), channel_id=1, source_target_pairs={{0,1},{2,3},{4,5},{6,7},{8,9},{10,11},{12,13},{14,15},{16,17},{18,... | collective-permute-start | bytes 294920 | tf_op jit(solution)/shard_map/ppermute | solution.py:23
  8.6 1.3 %collective-permute-start.11 = (f32[3,8,8,128]{3,2,1,0:T(8,128)S(1)}, f32[3,8,8,128]{3,2,1,0:T(8,128)S(1)}, u32[]{:S(2)}, u32[]{:S(2)}) collective-permute-start(f32[3,8,8,128]{3,2,1,0:T(8,128)S(1)} %get-tuple-element.23), channel_id=1, source_target_pairs={{1,0},{3,2},{5,4},{7,6},{9,8},{11,10},{13,12},{15,14},{17,16},{19,... | collective-permute-start | bytes 294920 | tf_op jit(solution)/shard_map/ppermute | solution.py:26
  10.0 3.0 %collective-permute-start.1 = (f32[320,128]{1,0:T(8,128)S(1)}, f32[320,128]{1,0:T(8,128)S(1)}, u32[]{:S(2)}, u32[]{:S(2)}) collective-permute-start(f32[320,128]{1,0:T(8,128)S(1)} %slice_select_fusion.1), channel_id=1, source_target_pairs={{0,2},{2,0},{4,6},{6,4},{8,10},{10,8},{12,14},{14,12},{16,18},{18,... | collective-permute-start | bytes 491528 | tf_op jit(solution)/shard_map/ppermute | solution.py:67
  13.1 4.5 %collective-permute-done.1 = f32[320,128]{1,0:T(8,128)S(1)} collective-permute-done((f32[320,128]{1,0:T(8,128)S(1)}, f32[320,128]{1,0:T(8,128)S(1)}, u32[]{:S(2)}, u32[]{:S(2)}) %collective-permute-start.1) | collective-permute-done | bytes 163872 | tf_op jit(solution)/shard_map/ppermute | solution.py:67
  17.7 2.4 %collective-permute-start.2 = (f32[160,128]{1,0:T(8,128)S(1)}, f32[160,128]{1,0:T(8,128)S(1)}, u32[]{:S(2)}, u32[]{:S(2)}) collective-permute-start(f32[160,128]{1,0:T(8,128)S(1)} %slice_select_fusion.2), channel_id=1, source_target_pairs={{0,4},{2,6},{4,0},{6,2},{8,12},{10,14},{12,8},{14,10},{16,20},{18,... | collective-permute-start | bytes 245768 | tf_op jit(solution)/shard_map/ppermute | solution.py:67
  20.2 2.6 %collective-permute-done.2 = f32[160,128]{1,0:T(8,128)S(1)} collective-permute-done((f32[160,128]{1,0:T(8,128)S(1)}, f32[160,128]{1,0:T(8,128)S(1)}, u32[]{:S(2)}, u32[]{:S(2)}) %collective-permute-start.2) | collective-permute-done | bytes 81952 | tf_op jit(solution)/shard_map/ppermute | solution.py:67
  22.9 1.8 %collective-permute-start.3 = (f32[80,128]{1,0:T(8,128)S(1)}, f32[80,128]{1,0:T(8,128)S(1)}, u32[]{:S(2)}, u32[]{:S(2)}) collective-permute-start(f32[80,128]{1,0:T(8,128)S(1)} %slice_select_fusion.3), channel_id=1, source_target_pairs={{0,8},{2,10},{4,12},{6,14},{8,0},{10,2},{12,4},{14,6},{16,24},{18,... | collective-permute-start | bytes 122888 | tf_op jit(solution)/shard_map/ppermute | solution.py:67
  24.8 2.1 %collective-permute-done.3 = f32[80,128]{1,0:T(8,128)S(1)} collective-permute-done((f32[80,128]{1,0:T(8,128)S(1)}, f32[80,128]{1,0:T(8,128)S(1)}, u32[]{:S(2)}, u32[]{:S(2)}) %collective-permute-start.3) | collective-permute-done | bytes 40992 | tf_op jit(solution)/shard_map/ppermute | solution.py:67
  27.0 2.9 %collective-permute-start.4 = (f32[40,128]{1,0:T(8,128)S(1)}, f32[40,128]{1,0:T(8,128)S(1)}, u32[]{:S(2)}, u32[]{:S(2)}) collective-permute-start(f32[40,128]{1,0:T(8,128)S(1)} %slice_select_fusion.4), channel_id=1, source_target_pairs={{0,16},{2,18},{4,20},{6,22},{8,24},{10,26},{12,28},{14,30},{16,0},... | collective-permute-start | bytes 61448 | tf_op jit(solution)/shard_map/ppermute | solution.py:67
  30.1 3.3 %collective-permute-start.13 = (f32[3,8,2,128]{3,2,1,0:T(2,128)S(1)}, f32[3,8,2,128]{3,2,1,0:T(2,128)S(1)}, u32[]{:S(2)}, u32[]{:S(2)}) collective-permute-start(f32[3,8,2,128]{3,2,1,0:T(2,128)S(1)} %convolution_bitcast_fusion.1), channel_id=1, source_target_pairs={{2,0},{4,2},{6,4},{8,6},{10,8},{12,10},{14,12},{16,14},{18,16},{20... | collective-permute-start | bytes 73736 | tf_op jit(solution)/shard_map/ppermute | solution.py:26
  33.4 1.8 %collective-permute-start.5 = (f32[40,128]{1,0:T(8,128)S(1)}, f32[40,128]{1,0:T(8,128)S(1)}, u32[]{:S(2)}, u32[]{:S(2)}) collective-permute-start(f32[40,128]{1,0:T(8,128)S(1)} %select_add_fusion.4), channel_id=1, source_target_pairs={{0,16},{2,18},{4,20},{6,22},{8,24},{10,26},{12,28},{14,30},{16,0},... | collective-permute-start | bytes 61448 | tf_op jit(solution)/shard_map/ppermute | solution.py:72
  35.2 5.7 %collective-permute-done.12 = f32[3,8,2,128]{3,2,1,0:T(2,128)S(1)} collective-permute-done((f32[3,8,2,128]{3,2,1,0:T(2,128)S(1)}, f32[3,8,2,128]{3,2,1,0:T(2,128)S(1)}, u32[]{:S(2)}, u32[]{:S(2)}) %collective-permute-start.12) | collective-permute-done | bytes 24608 | tf_op jit(solution)/shard_map/ppermute | solution.py:23
  41.2 3.8 %collective-permute-done.6 = f32[80,128]{1,0:T(8,128)S(1)} collective-permute-done((f32[80,128]{1,0:T(8,128)S(1)}, f32[80,128]{1,0:T(8,128)S(1)}, u32[]{:S(2)}, u32[]{:S(2)}) %collective-permute-start.6) | collective-permute-done | bytes 40992 | tf_op jit(solution)/shard_map/ppermute | solution.py:72
  45.2 1.2 %fusion.21 = (f32[3,2,128]{2,1,0:T(2,128)}, bf16[3,2,128,1]{2,1,0,3:T(2,128)(2,1)S(1)}, f32[]{:T(128)}) fusion(f32[3,2,128]{2,1,0:T(2,128)S(1)} %bitcast.56), kind=kLoop, calls=%fused_computation.64 | loop fusion | flops 3071 | bytes 7684 | tf_op jit(solution)/shard_map/reduce_precision | solution.py:308
  46.4 3.2 %collective-permute-done.7 = f32[160,128]{1,0:T(8,128)S(1)} collective-permute-done((f32[160,128]{1,0:T(8,128)S(1)}, f32[160,128]{1,0:T(8,128)S(1)}, u32[]{:S(2)}, u32[]{:S(2)}) %collective-permute-start.7) | collective-permute-done | bytes 81952 | tf_op jit(solution)/shard_map/ppermute | solution.py:72
  50.7 4.3 %collective-permute-done.8 = f32[320,128]{1,0:T(8,128)S(1)} collective-permute-done((f32[320,128]{1,0:T(8,128)S(1)}, f32[320,128]{1,0:T(8,128)S(1)}, u32[]{:S(2)}, u32[]{:S(2)}) %collective-permute-start.8) | collective-permute-done | bytes 163872 | tf_op jit(solution)/shard_map/ppermute | solution.py:72
  55.9 3.6 %collective-permute-done.15 = f32[5,128]{1,0:T(8,128)S(1)} collective-permute-done((f32[5,128]{1,0:T(8,128)S(1)}, f32[5,128]{1,0:T(8,128)S(1)}, u32[]{:S(2)}, u32[]{:S(2)}) %collective-permute-start.15) | collective-permute-done | bytes 2592 | tf_op jit(solution)/shard_map/ppermute | solution.py:84
  60.2 3.6 %collective-permute-done.16 = f32[5,128]{1,0:T(8,128)S(1)} collective-permute-done((f32[5,128]{1,0:T(8,128)S(1)}, f32[5,128]{1,0:T(8,128)S(1)}, u32[]{:S(2)}, u32[]{:S(2)}) %collective-permute-start.16) | collective-permute-done | bytes 2592 | tf_op jit(solution)/shard_map/ppermute | solution.py:84
  63.8 3.6 %collective-permute-done.17 = f32[5,128]{1,0:T(8,128)S(1)} collective-permute-done((f32[5,128]{1,0:T(8,128)S(1)}, f32[5,128]{1,0:T(8,128)S(1)}, u32[]{:S(2)}, u32[]{:S(2)}) %collective-permute-start.17) | collective-permute-done | bytes 2592 | tf_op jit(solution)/shard_map/ppermute | solution.py:84
  67.4 4.5 %collective-permute-done.18 = f32[5,128]{1,0:T(8,128)S(1)} collective-permute-done((f32[5,128]{1,0:T(8,128)S(1)}, f32[5,128]{1,0:T(8,128)S(1)}, u32[]{:S(2)}, u32[]{:S(2)}) %collective-permute-start.18) | collective-permute-done | bytes 2592 | tf_op jit(solution)/shard_map/ppermute | solution.py:84
  73.5 21.9 %solve.1 = (bf16[768,512]{1,0:T(8,128)(2,1)}, f32[1,768]{1,0:T(1,128)}, f32[513,513]{1,0:T(8,128)}) custom-call(f32[1280,128]{1,0:T(8,128)} %pad_maximum_fusion.refs_0_, f32[5,128]{1,0:T(8,128)} %add.64.refs_1_, f32[1,768]{1,0:T(1,128)} %bitcast.57, bf16[768,512]{1,0:T(8,128)(2,1)} %bitcast.50), custom_call_target="tpu_custom_call" | custom-call | flops 805306368 | bytes 2097152 | tf_op jit(solution)/shard_map/solve/pallas_call | solution.py:277
  (66 shorter events, 6.6 us)
Async XLA Ops:
  0.6 5.5 %copy-start = (bf16[3,8,16,1024]{3,2,1,0:T(8,128)(2,1)S(1)}, bf16[3,8,16,1024]{3,2,1,0:T(8,128)(2,1)}, u32[]{:S(2)}) copy-start(bf16[3,8,16,1024]{3,2,1,0:T(8,128)(2,1)} %param.3) | copy-start | bytes 2359300
  0.6 4.2 %copy-start.3 = (bf16[3,17]{1,0:T(4,128)(2,1)S(1)}, bf16[3,17]{1,0:T(4,128)(2,1)}, u32[]{:S(2)}) copy-start(bf16[3,17]{1,0:T(4,128)(2,1)} %param.5) | copy-start | bytes 310
  4.3 5.6 %collective-permute-start = (f32[640,128]{1,0:T(8,128)S(1)}, f32[640,128]{1,0:T(8,128)S(1)}, u32[]{:S(2)}, u32[]{:S(2)}) collective-permute-start(f32[640,128]{1,0:T(8,128)S(1)} %slice_select_fusion), channel_id=1, source_target_pairs={{0,1},{1,0},{2,3},{3,2},{4,5},{5,4},{6,7},{7,6},{8,9},{9,8},{10,11... | collective-permute-start | bytes 983048 | tf_op jit(solution)/shard_map/ppermute | solution.py:67
  5.1 4.8 %copy-start.1 = (f32[1280,128]{1,0:T(8,128)S(1)}, f32[1280,128]{1,0:T(8,128)}, u32[]{:S(2)}) copy-start(f32[1280,128]{1,0:T(8,128)} %gram.1) | copy-start | bytes 1966084
  6.6 23.2 %collective-permute-start.10 = (f32[3,8,8,128]{3,2,1,0:T(8,128)S(1)}, f32[3,8,8,128]{3,2,1,0:T(8,128)S(1)}, u32[]{:S(2)}, u32[]{:S(2)}) collective-permute-start(f32[3,8,8,128]{3,2,1,0:T(8,128)S(1)} %get-tuple-element.22), channel_id=1, source_target_pairs={{0,1},{2,3},{4,5},{6,7},{8,9},{10,11},{12,13},{14,15},{16,17},{18,... | collective-permute-start | bytes 294920 | tf_op jit(solution)/shard_map/ppermute | solution.py:23
  8.6 21.2 %collective-permute-start.11 = (f32[3,8,8,128]{3,2,1,0:T(8,128)S(1)}, f32[3,8,8,128]{3,2,1,0:T(8,128)S(1)}, u32[]{:S(2)}, u32[]{:S(2)}) collective-permute-start(f32[3,8,8,128]{3,2,1,0:T(8,128)S(1)} %get-tuple-element.23), channel_id=1, source_target_pairs={{1,0},{3,2},{5,4},{7,6},{9,8},{11,10},{13,12},{15,14},{17,16},{19,... | collective-permute-start | bytes 294920 | tf_op jit(solution)/shard_map/ppermute | solution.py:26
  10.0 7.6 %collective-permute-start.1 = (f32[320,128]{1,0:T(8,128)S(1)}, f32[320,128]{1,0:T(8,128)S(1)}, u32[]{:S(2)}, u32[]{:S(2)}) collective-permute-start(f32[320,128]{1,0:T(8,128)S(1)} %slice_select_fusion.1), channel_id=1, source_target_pairs={{0,2},{2,0},{4,6},{6,4},{8,10},{10,8},{12,14},{14,12},{16,18},{18,... | collective-permute-start | bytes 491528 | tf_op jit(solution)/shard_map/ppermute | solution.py:67
  17.7 32.0 %copy-start.2 = (bf16[3,1,2,128,512]{4,3,2,1,0:T(8,128)(2,1)S(1)}, bf16[3,1,2,128,512]{4,3,2,1,0:T(8,128)(2,1)}, u32[]{:S(2)}) copy-start(bf16[3,1,2,128,512]{4,3,2,1,0:T(8,128)(2,1)} %param.4) | copy-start | bytes 2359300
  17.7 5.1 %collective-permute-start.2 = (f32[160,128]{1,0:T(8,128)S(1)}, f32[160,128]{1,0:T(8,128)S(1)}, u32[]{:S(2)}, u32[]{:S(2)}) collective-permute-start(f32[160,128]{1,0:T(8,128)S(1)} %slice_select_fusion.2), channel_id=1, source_target_pairs={{0,4},{2,6},{4,0},{6,2},{8,12},{10,14},{12,8},{14,10},{16,20},{18,... | collective-permute-start | bytes 245768 | tf_op jit(solution)/shard_map/ppermute | solution.py:67
  22.9 4.1 %collective-permute-start.3 = (f32[80,128]{1,0:T(8,128)S(1)}, f32[80,128]{1,0:T(8,128)S(1)}, u32[]{:S(2)}, u32[]{:S(2)}) collective-permute-start(f32[80,128]{1,0:T(8,128)S(1)} %slice_select_fusion.3), channel_id=1, source_target_pairs={{0,8},{2,10},{4,12},{6,14},{8,0},{10,2},{12,4},{14,6},{16,24},{18,... | collective-permute-start | bytes 122888 | tf_op jit(solution)/shard_map/ppermute | solution.py:67
  27.0 6.4 %collective-permute-start.4 = (f32[40,128]{1,0:T(8,128)S(1)}, f32[40,128]{1,0:T(8,128)S(1)}, u32[]{:S(2)}, u32[]{:S(2)}) collective-permute-start(f32[40,128]{1,0:T(8,128)S(1)} %slice_select_fusion.4), channel_id=1, source_target_pairs={{0,16},{2,18},{4,20},{6,22},{8,24},{10,26},{12,28},{14,30},{16,0},... | collective-permute-start | bytes 61448 | tf_op jit(solution)/shard_map/ppermute | solution.py:67
  30.1 5.1 %collective-permute-start.13 = (f32[3,8,2,128]{3,2,1,0:T(2,128)S(1)}, f32[3,8,2,128]{3,2,1,0:T(2,128)S(1)}, u32[]{:S(2)}, u32[]{:S(2)}) collective-permute-start(f32[3,8,2,128]{3,2,1,0:T(2,128)S(1)} %convolution_bitcast_fusion.1), channel_id=1, source_target_pairs={{2,0},{4,2},{6,4},{8,6},{10,8},{12,10},{14,12},{16,14},{18,16},{20... | collective-permute-start | bytes 73736 | tf_op jit(solution)/shard_map/ppermute | solution.py:26
  33.4 7.5 %collective-permute-start.12 = (f32[3,8,2,128]{3,2,1,0:T(2,128)S(1)}, f32[3,8,2,128]{3,2,1,0:T(2,128)S(1)}, u32[]{:S(2)}, u32[]{:S(2)}) collective-permute-start(f32[3,8,2,128]{3,2,1,0:T(2,128)S(1)} %convolution_bitcast_fusion.1), channel_id=1, source_target_pairs={{0,2},{2,4},{4,6},{6,8},{8,10},{10,12},{12,14},{14,16},{16,18},{18... | collective-permute-start | bytes 73736 | tf_op jit(solution)/shard_map/ppermute | solution.py:23
  33.4 7.5 %collective-permute-start.5 = (f32[40,128]{1,0:T(8,128)S(1)}, f32[40,128]{1,0:T(8,128)S(1)}, u32[]{:S(2)}, u32[]{:S(2)}) collective-permute-start(f32[40,128]{1,0:T(8,128)S(1)} %select_add_fusion.4), channel_id=1, source_target_pairs={{0,16},{2,18},{4,20},{6,22},{8,24},{10,26},{12,28},{14,30},{16,0},... | collective-permute-start | bytes 61448 | tf_op jit(solution)/shard_map/ppermute | solution.py:72
  41.0 4.1 %collective-permute-start.6 = (f32[80,128]{1,0:T(8,128)S(1)}, f32[80,128]{1,0:T(8,128)S(1)}, u32[]{:S(2)}, u32[]{:S(2)}) collective-permute-start(f32[80,128]{1,0:T(8,128)S(1)} %pad_maximum_fusion.5), channel_id=1, source_target_pairs={{0,8},{2,10},{4,12},{6,14},{8,0},{10,2},{12,4},{14,6},{16,24},{18,... | collective-permute-start | bytes 122888 | tf_op jit(solution)/shard_map/ppermute | solution.py:72
  45.1 4.5 %collective-permute-start.7 = (f32[160,128]{1,0:T(8,128)S(1)}, f32[160,128]{1,0:T(8,128)S(1)}, u32[]{:S(2)}, u32[]{:S(2)}) collective-permute-start(f32[160,128]{1,0:T(8,128)S(1)} %pad_maximum_fusion.3), channel_id=1, source_target_pairs={{0,4},{2,6},{4,0},{6,2},{8,12},{10,14},{12,8},{14,10},{16,20},{18,... | collective-permute-start | bytes 245768 | tf_op jit(solution)/shard_map/ppermute | solution.py:72
  49.6 5.4 %collective-permute-start.8 = (f32[320,128]{1,0:T(8,128)S(1)}, f32[320,128]{1,0:T(8,128)S(1)}, u32[]{:S(2)}, u32[]{:S(2)}) collective-permute-start(f32[320,128]{1,0:T(8,128)S(1)} %pad_maximum_fusion.2), channel_id=1, source_target_pairs={{0,2},{2,0},{4,6},{6,4},{8,10},{10,8},{12,14},{14,12},{16,18},{18,... | collective-permute-start | bytes 491528 | tf_op jit(solution)/shard_map/ppermute | solution.py:72
  50.6 4.6 %collective-permute-start.14 = (f32[5,128]{1,0:T(8,128)S(1)}, f32[5,128]{1,0:T(8,128)S(1)}, u32[]{:S(2)}, u32[]{:S(2)}) collective-permute-start(f32[5,128]{1,0:T(8,128)S(1)} %pad_bitcast_fusion), channel_id=1, source_target_pairs={{0,1},{1,0},{2,3},{3,2},{4,5},{5,4},{6,7},{7,6},{8,9},{9,8},{10,11... | collective-permute-start | bytes 7688 | tf_op jit(solution)/shard_map/ppermute | solution.py:84
  55.1 17.5 %collective-permute-start.9 = (f32[640,128]{1,0:T(8,128)S(1)}, f32[640,128]{1,0:T(8,128)S(1)}, u32[]{:S(2)}, u32[]{:S(2)}) collective-permute-start(f32[640,128]{1,0:T(8,128)S(1)} %pad_maximum_fusion.1), channel_id=1, source_target_pairs={{0,1},{1,0},{2,3},{3,2},{4,5},{5,4},{6,7},{7,6},{8,9},{9,8},{10,11... | collective-permute-start | bytes 983048 | tf_op jit(solution)/shard_map/ppermute | solution.py:72
  55.8 3.7 %collective-permute-start.15 = (f32[5,128]{1,0:T(8,128)S(1)}, f32[5,128]{1,0:T(8,128)S(1)}, u32[]{:S(2)}, u32[]{:S(2)}) collective-permute-start(f32[5,128]{1,0:T(8,128)S(1)} %fusion.18), channel_id=1, source_target_pairs={{0,2},{2,0},{4,6},{6,4},{8,10},{10,8},{12,14},{14,12},{16,18},{18,... | collective-permute-start | bytes 7688 | tf_op jit(solution)/shard_map/ppermute | solution.py:84
  60.1 3.7 %collective-permute-start.16 = (f32[5,128]{1,0:T(8,128)S(1)}, f32[5,128]{1,0:T(8,128)S(1)}, u32[]{:S(2)}, u32[]{:S(2)}) collective-permute-start(f32[5,128]{1,0:T(8,128)S(1)} %fusion.24), channel_id=1, source_target_pairs={{0,4},{2,6},{4,0},{6,2},{8,12},{10,14},{12,8},{14,10},{16,20},{18,... | collective-permute-start | bytes 7688 | tf_op jit(solution)/shard_map/ppermute | solution.py:84
  63.8 3.6 %collective-permute-start.17 = (f32[5,128]{1,0:T(8,128)S(1)}, f32[5,128]{1,0:T(8,128)S(1)}, u32[]{:S(2)}, u32[]{:S(2)}) collective-permute-start(f32[5,128]{1,0:T(8,128)S(1)} %add.62), channel_id=1, source_target_pairs={{0,8},{2,10},{4,12},{6,14},{8,0},{10,2},{12,4},{14,6},{16,24},{18,... | collective-permute-start | bytes 7688 | tf_op jit(solution)/shard_map/ppermute | solution.py:84
  67.4 4.5 %collective-permute-start.18 = (f32[5,128]{1,0:T(8,128)S(1)}, f32[5,128]{1,0:T(8,128)S(1)}, u32[]{:S(2)}, u32[]{:S(2)}) collective-permute-start(f32[5,128]{1,0:T(8,128)S(1)} %add.63), channel_id=1, source_target_pairs={{0,16},{2,18},{4,20},{6,22},{8,24},{10,26},{12,28},{14,30},{16,0},... | collective-permute-start | bytes 7688 | tf_op jit(solution)/shard_map/ppermute | solution.py:84

commit v2 on v1

--- a/solution.py
+++ b/solution.py
@@ -13,76 +13,16 @@
 HIGHEST = lax.Precision.HIGHEST
 
 
-def padded(block, sides, width, periodic):
-    for axis, dim in sides:
-        count = lax.axis_size(axis)
-        forward = [(i, i + 1) for i in range(count - 1)]
-        if periodic:
-            forward.append((count - 1, 0))
-        backward = [(target, source) for source, target in forward]
-        low = lax.ppermute(
-            lax.slice_in_dim(block, block.shape[dim] - width, None, axis=dim), axis, forward
-        )
-        high = lax.ppermute(lax.slice_in_dim(block, 0, width, axis=dim), axis, backward)
-        block = jnp.concatenate([low, block, high], axis=dim)
-    return block
-
-
-def band(taps_row, length, out_len, shift, wrap):
-    rows = jnp.arange(length, dtype=jnp.int32)[:, None]
-    cols = jnp.arange(out_len, dtype=jnp.int32)[None, :]
-    lag = rows - STRIDE * cols + shift
-    if wrap:
-        lag = lag % length
-    hits = lag[:, :, None] == jnp.arange(2 * STRIDE + 1, dtype=jnp.int32)[None, None, :]
-    return jnp.sum(jnp.where(hits, taps_row[None, None, :], jnp.zeros((), taps_row.dtype)), axis=-1)
-
-
-def hops(axes):
-    found = []
-    for axis in axes:
-        size = lax.axis_size(axis)
-        if size & (size - 1):
-            return None
-        bit = 1
-        while bit < size:
-            pairs = [(i, i ^ bit) for i in range(size)]
-            upper = (lax.axis_index(axis) & bit) != 0
-            found.append((axis, pairs, upper))
-            bit *= 2
-    return found
-
-
-def total_of(block, axes):
-    exchanges = hops(axes)
-    if exchanges is None:
-        return lax.psum(block, axes)
-    halved = []
-    for axis, pairs, upper in exchanges:
-        rows = block.shape[0]
-        if rows % 16 == 0:
-            low, high = block[: rows // 2], block[rows // 2 :]
-            sent = jnp.where(upper, low, high)
-            kept = jnp.where(upper, high, low)
-            block = kept + lax.ppermute(sent, axis, pairs)
-            halved.append((axis, pairs, upper))
-        else:
-            block = block + lax.ppermute(block, axis, pairs)
-    for axis, pairs, upper in reversed(halved):
-        other = lax.ppermute(block, axis, pairs)
-        block = jnp.concatenate(
-            [jnp.where(upper, other, block), jnp.where(upper, block, other)], axis=0
-        )
-    return block
-
-
-def small_total(block, axes):
-    exchanges = hops(axes)
-    if exchanges is None:
-        return lax.psum(block, axes)
-    for axis, pairs, _ in exchanges:
-        block = block + lax.ppermute(block, axis, pairs)
-    return block
+def swap(block, axis, step):
+    return lax.ppermute(block, axis, [(i, i ^ step) for i in range(lax.axis_size(axis))])
+
+
+def bit_groups(size):
+    groups, bit = [], 1
+    while bit < size:
+        groups.append((bit, 2 * bit, 3 * bit) if 4 * bit <= size else (bit,))
+        bit *= 4 if 4 * bit <= size else 2
+    return groups
 
 
 def contract_rows(a, b, precision=None):
@@ -97,29 +37,142 @@
     )
 
 
-def gram_kernel(rows_ref, out_ref):
-    modes = rows_ref.shape[1]
-    at = 0
-    for p in range(modes // TILE):
-        left = rows_ref[:, TILE * p : TILE * (p + 1)]
-        part = contract_rows(left, rows_ref[:, TILE * p :])
-        for c in range(modes // TILE - p):
-            out_ref[at : at + TILE, :] = part[:, TILE * c : TILE * (c + 1)]
-            at += TILE
-
-
-def local_gram(rows):
+def upper_blocks(chunks):
+    return [(p, c) for p in range(chunks) for c in range(p, chunks)]
+
+
+def gram_kernel(side_ref, rows_ref, out_ref):
+    blocks = upper_blocks(rows_ref.shape[1] // TILE)
+    half = len(blocks) // 2
+    for side in range(2):
+
+        @pl.when(side_ref[0] == side)
+        def _():
+            mine = blocks[half * side : half * (side + 1)]
+            for p in sorted({p for p, _ in mine}):
+                cols = [c for q, c in mine if q == p]
+                part = contract_rows(
+                    rows_ref[:, TILE * p : TILE * (p + 1)],
+                    rows_ref[:, TILE * cols[0] : TILE * (cols[-1] + 1)],
+                )
+                for c in cols:
+                    at = TILE * mine.index((p, c))
+                    out_ref[at : at + TILE, :] = part[:, TILE * (c - cols[0]) : TILE * (c - cols[0] + 1)]
+
+
+def half_gram(side, rows):
     count, modes = rows.shape
-    chunks = modes // TILE
-    blocks = chunks * (chunks + 1) // 2
+    height = TILE * len(upper_blocks(modes // TILE)) // 2
     return pl.pallas_call(
         gram_kernel,
-        out_shape=jax.ShapeDtypeStruct((blocks * TILE, TILE), F32),
+        out_shape=jax.ShapeDtypeStruct((height, TILE), F32),
+        in_specs=[pl.BlockSpec(memory_space=pltpu.SMEM), pl.BlockSpec(memory_space=pltpu.VMEM)],
         cost_estimate=pl.CostEstimate(
-            flops=2 * count * modes * modes, bytes_accessed=4 * blocks * TILE * TILE, transcendentals=0
+            flops=2 * count * height * TILE, bytes_accessed=4 * height * TILE, transcendentals=0
         ),
         name="gram",
-    )(rows)
+    )(side.reshape(1), rows)
+
+
+def weights(taps_ref, direction, lag):
+    found = jnp.zeros(lag.shape, F32)
+    for tap in range(2 * STRIDE + 1):
+        found = jnp.where(lag == tap, taps_ref[direction, tap], found)
+    return found
+
+
+def filter_kernel(taps_ref, cells_ref, out_ref, band, *, comps, cells_x, cells_y):
+    depth, points = band.shape
+    height = out_ref.shape[0]
+    step = TILE // STRIDE
+    z = lax.broadcasted_iota(jnp.int32, (TILE, points), 0)
+    p = lax.broadcasted_iota(jnp.int32, (TILE, points), 1)
+    for block in range(depth // TILE):
+        lag = z + TILE * block - STRIDE * p + STRIDE
+        lag = jnp.where(lag < 0, lag + depth, lag)
+        lag = jnp.where(lag >= depth, lag - depth, lag)
+        if block == 0:
+            pattern = weights(taps_ref, 2, lag)
+            band[:TILE, :] = pattern.astype(BF16)
+        else:
+            band[TILE * block : TILE * (block + 1), :] = pltpu.roll(pattern, step * block, 1).astype(BF16)
+    along_z = jnp.dot(cells_ref[...], band[...], preferred_element_type=F32)
+    count = cells_ref.shape[0]
+    wide_r = cells_x // STRIDE + 2
+    out = lax.broadcasted_iota(jnp.int32, (height, count), 0)
+    cell = lax.broadcasted_iota(jnp.int32, (height, count), 1)
+    comp, r, q = out % comps, out // comps % wide_r, out // (comps * wide_r)
+    x, y = cell // cells_y % cells_x, cell % cells_y
+    weight = weights(taps_ref, 0, x - STRIDE * (r - 1) + STRIDE)
+    weight = weight * weights(taps_ref, 1, y - STRIDE * (q - 1) + STRIDE)
+    weight = jnp.where(cell // (cells_x * cells_y) == comp, weight, 0.0)
+    out_ref[...] = jnp.dot(weight, along_z, precision=HIGHEST, preferred_element_type=F32)
+
+
+def local_filter(taps, snapshot):
+    comps, cells_x, cells_y, cells_z = snapshot.shape
+    wide_r, wide_q = cells_x // STRIDE + 2, cells_y // STRIDE + 2
+    points = cells_z // STRIDE
+    used = comps * wide_r * wide_q
+    height = -(-used // 8) * 8
+    cells = snapshot.reshape(-1, cells_z)
+    sums = pl.pallas_call(
+        lambda *refs: filter_kernel(*refs, comps=comps, cells_x=cells_x, cells_y=cells_y),
+        out_shape=jax.ShapeDtypeStruct((height, points), F32),
+        in_specs=[pl.BlockSpec(memory_space=pltpu.SMEM), pl.BlockSpec(memory_space=pltpu.VMEM)],
+        scratch_shapes=[pltpu.VMEM((cells_z, points), BF16)],
+        cost_estimate=pl.CostEstimate(
+            flops=4 * cells.size * points, bytes_accessed=2 * cells.size, transcendentals=0
+        ),
+        name="filter",
+    )(taps.astype(F32), cells)
+    return sums[:used].reshape(wide_q, wide_r, comps, points)
+
+
+def fold_neighbours(parts, axis, periodic):
+    count = lax.axis_size(axis)
+    own = parts[1:-1]
+    if count == 2 and not periodic:
+        upper = lax.axis_index(axis) == 1
+        other = swap(jnp.where(upper, parts[0], parts[-1]), axis, 1)
+        zero = jnp.zeros_like(other)
+        low, high = jnp.where(upper, other, zero), jnp.where(upper, zero, other)
+    else:
+        forward = [(i, i + 1) for i in range(count - 1)] + ([(count - 1, 0)] if periodic else [])
+        low = lax.ppermute(parts[-1], axis, forward)
+        high = lax.ppermute(parts[0], axis, [(target, source) for source, target in forward])
+    inner = own.shape[0]
+    if inner == 1:
+        return own + (low + high)[None]
+    return jnp.concatenate([(own[0] + low)[None], own[1:-1], (own[-1] + high)[None]])
+
+
+def cross_kernel(fresh_ref, rows_ref, out_ref):
+    lines, points = fresh_ref.shape
+    modes = rows_ref.shape[1]
+    total = jnp.zeros((8, modes), F32)
+    square = jnp.zeros((1, 1), F32)
+    for i in range(lines):
+        line = fresh_ref[i : i + 1, :]
+        square = square + jnp.sum(line * line, axis=1, keepdims=True)
+        left = jnp.broadcast_to(line, (8, points)).astype(BF16)
+        total = total + jnp.dot(
+            left, rows_ref[points * i : points * (i + 1), :], preferred_element_type=F32
+        )
+    out_ref[...] = jnp.zeros(out_ref.shape, F32)
+    for c in range(modes // TILE):
+        out_ref[c : c + 1, :] = total[:1, TILE * c : TILE * (c + 1)]
+    out_ref[modes // TILE : modes // TILE + 1, :] = jnp.broadcast_to(square, (1, TILE))
+
+
+def local_cross(fresh, rows):
+    height = -(-(rows.shape[1] // TILE + 1) // 8) * 8
+    return pl.pallas_call(
+        cross_kernel,
+        out_shape=jax.ShapeDtypeStruct((height, TILE), F32),
+        cost_estimate=pl.CostEstimate(flops=16 * rows.size, bytes_accessed=2 * rows.size, transcendentals=0),
+        name="cross",
+    )(fresh, rows)
 
 
 def factor_blocks(work, scaled, upper):
@@ -215,24 +268,27 @@
 
 
 def solve_kernel(
-    total_ref, cross_ref, fresh_ref, rows_ref, modes_ref, mode_ref, factor_ref, work, scaled, *, total
+    place_ref, mine_ref, other_ref, fresh_ref, rows_ref, modes_ref, mode_ref, factor_ref,
+    work, scaled, blocks, *, total,
 ):
     modes = work.shape[0]
     chunks = modes // TILE
-    at = 0
-    for p in range(chunks):
-        for c in range(p, chunks):
-            work[TILE * p : TILE * (p + 1), TILE * c : TILE * (c + 1)] = (
-                total_ref[at : at + TILE, :] * (1.0 / total)
-            )
-            at += TILE
+    half = blocks.shape[0] // 2
+    piece = half // 4
+    for part_ref, side in ((mine_ref, place_ref[0]), (other_ref, 1 - place_ref[0])):
+        for step in range(4):
+            at = pl.multiple_of(half * side + piece * (place_ref[1] ^ step), 8)
+            blocks[pl.ds(at, piece), :] = part_ref[piece * step : piece * (step + 1), :] * (1.0 / total)
+    for at, (p, c) in enumerate(upper_blocks(chunks)):
+        work[TILE * p : TILE * (p + 1), TILE * c : TILE * (c + 1)] = blocks[TILE * at : TILE * (at + 1), :]
     scales = factor_blocks(work, scaled, factor_ref)
     for g, scale in enumerate(scales):
         where = slice(8 * g, 8 * g + 8)
         for c in range(8 * g // TILE + 1):
             work[where, TILE * c : TILE * (c + 1)] = work[where, TILE * c : TILE * (c + 1)] * scale
-    cross = [cross_ref[c : c + 1, :] * (1.0 / total) for c in range(chunks)]
-    square = cross_ref[chunks : chunks + 1, :] * (1.0 / total)
+    sums = (mine_ref[half : half + chunks + 1, :] + other_ref[half : half + chunks + 1, :]) * (1.0 / total)
+    cross = [sums[c : c + 1, :] for c in range(chunks)]
+    square = sums[chunks : chunks + 1, :]
     projected = []
     for p in range(chunks):
         own = slice(TILE * p, TILE * (p + 1))
@@ -272,8 +328,10 @@
     factor_ref[modes : modes + 1, modes : modes + 1] = last
 
 
-def solve(total_gram, total_cross, fresh, rows, total):
+def solve(place, mine, other, fresh, rows, total):
     count, modes = rows.shape
+    height = TILE * len(upper_blocks(modes // TILE))
+    vmem = pl.BlockSpec(memory_space=pltpu.VMEM)
     return pl.pallas_call(
         lambda *refs: solve_kernel(*refs, total=total),
         out_shape=(
@@ -281,37 +339,61 @@
             jax.ShapeDtypeStruct((1, count), F32),
             jax.ShapeDtypeStruct((modes + 1, modes + 1), F32),
         ),
-        scratch_shapes=[pltpu.VMEM((modes, modes), F32), pltpu.VMEM((TILE, modes), F32)],
+        in_specs=[pl.BlockSpec(memory_space=pltpu.SMEM)] + [vmem] * 4,
+        scratch_shapes=[
+            pltpu.VMEM((modes, modes), F32),
+            pltpu.VMEM((TILE, modes), F32),
+            pltpu.VMEM((height, TILE), F32),
+        ],
         cost_estimate=pl.CostEstimate(
             flops=4 * count * modes * modes, bytes_accessed=8 * modes * modes, transcendentals=modes
         ),
         name="solve",
-    )(total_gram, total_cross, fresh, rows)
+    )(place, mine, other, fresh, rows)
 
 
 def local(snapshot, basis, taps):
-    comps, cells_x, cells_y, cells_z = snapshot.shape
     modes = basis.shape[-1]
-    axes = ("gy", "gx")
-    flat_rows = basis.reshape(-1, modes)
-    total = flat_rows.shape[0] * lax.axis_size("gx") * lax.axis_size("gy")
-    gram = total_of(local_gram(flat_rows), axes)
-    matrix_z = band(taps[2], cells_z, cells_z // STRIDE, STRIDE, True)
-    along_z = jnp.dot(snapshot.reshape(-1, cells_z), matrix_z, preferred_element_type=F32)
-    along_z = along_z.reshape(comps, cells_x, cells_y, cells_z // STRIDE)
-    padded_y = padded(along_z, (("gy", 2),), STRIDE, False)
-    matrix_y = band(taps[1], cells_y + 2 * STRIDE, cells_y // STRIDE, 0, False).astype(F32)
-    along_y = jnp.einsum("cxyz,yf->cxfz", padded_y, matrix_y, precision=HIGHEST)
-    padded_x = padded(along_y, (("gx", 1),), STRIDE, True)
-    matrix_x = band(taps[0], cells_x + 2 * STRIDE, cells_x // STRIDE, 0, False).astype(F32)
-    along_x = jnp.einsum("cxyz,xf->cfyz", padded_x, matrix_x, precision=HIGHEST)
-    fresh = lax.reduce_precision(along_x, exponent_bits=8, mantissa_bits=7).reshape(-1)
-    filtered = fresh.astype(BF16)
-    cross = jnp.einsum("rk,r->k", flat_rows, filtered, preferred_element_type=F32)
-    square = jnp.full((TILE,), jnp.sum(fresh * fresh), F32)
-    sums = jnp.concatenate([cross, square]).reshape(-1, TILE)
-    sums = small_total(sums, axes)
-    new_modes, new_mode, factor = solve(gram, sums, fresh.reshape(1, -1), flat_rows, total)
+    rows = basis.reshape(-1, modes)
+    total = rows.shape[0] * lax.axis_size("gx") * lax.axis_size("gy")
+    side = lax.axis_index("gy") & 1
+    member = lax.axis_index("gx") & 3
+    first, *others = bit_groups(lax.axis_size("gx"))
+
+    away = swap(half_gram(1 - side, rows), "gy", 1)
+    half = half_gram(side, rows) + away
+    bit = 2
+    while bit < lax.axis_size("gy"):
+        half = half + swap(half, "gy", bit)
+        bit *= 2
+    piece = half.shape[0] // 4
+    quarters = half.reshape(4, piece, TILE)
+    quarter = lax.dynamic_index_in_dim(quarters, member, 0, keepdims=False)
+    arrived = [
+        swap(lax.dynamic_index_in_dim(quarters, member ^ step, 0, keepdims=False), "gx", step)
+        for step in first
+    ]
+    quarter = quarter + arrived[0] + arrived[1] + arrived[2]
+
+    parts = fold_neighbours(local_filter(taps, snapshot), "gy", False)
+    parts = fold_neighbours(jnp.swapaxes(parts, 0, 1), "gx", True)
+    fresh = lax.reduce_precision(jnp.transpose(parts, (2, 0, 1, 3)), exponent_bits=8, mantissa_bits=7)
+    fresh = fresh.reshape(-1, fresh.shape[-1])
+    cross = local_cross(fresh, rows)
+    bit = 2
+    while bit < lax.axis_size("gy"):
+        cross = cross + swap(cross, "gy", bit)
+        bit *= 2
+
+    block = jnp.concatenate([quarter, cross])
+    for steps in others:
+        block = sum([swap(block, "gx", step) for step in steps], block)
+    gathered = [block] + [swap(block, "gx", step) for step in first]
+    sums = sum([got[piece:] for got in gathered[1:]], block[piece:])
+    mine = jnp.concatenate([got[:piece] for got in gathered] + [sums])
+    other = swap(mine, "gy", 1)
+    place = jnp.stack([side, member]).astype(jnp.int32)
+    new_modes, new_mode, factor = solve(place, mine, other, fresh.reshape(1, -1), rows, total)
     return (new_modes.reshape(basis.shape), new_mode.reshape(basis.shape[:-1]), factor)
 
 

time: 95.6 us -> 69.2 us (0.72)
  waiting for transfers between devices: 41.8 us -> 11.9 us
  Pallas kernels: 24.5 us -> 31.2 us
  other arithmetic: 6.88 us -> 5.15 us
  starting transfers between devices: 19.5 us -> 18.3 us
  matrix products: 0.99 us -> 0 us
    ppermute x19 -> x14, waiting for transfers between devices: 41.8 us -> 11.9 us  [the longest x12 9.2 us: swap(): lax.ppermute(block, axis, [(i, i ^ step) for i in range(lax.axis_size(axi...]
    pallas_call x1 -> x4, Pallas kernels: 2.55 us -> 9.18 us  [the longest x2 4.43 us: half_gram(): pl.pallas_call(gram_kernel, out_shape=jax.ShapeDtypeStruct((height, TILE)...]
    select_n x11 -> x0, other arithmetic: 1.5 us -> none  [the longest x5 1.15 us: total_of(): sent = jnp.where(upper, low, high)]
    convert_element_type x0 -> x1, other arithmetic: none -> 1.26 us  [local_filter(): taps.astype(F32)]
    ppermute x19 -> x14, starting transfers between devices: 19.5 us -> 18.3 us  [the longest x12 11.2 us: swap(): lax.ppermute(block, axis, [(i, i ^ step) for i in range(lax.axis_size(axi...]
    reduce_precision x1, other arithmetic: 1.2 us -> 0.01 us  [local(): lax.reduce_precision(jnp.transpose(parts, (2, 0, 1, 3)), exponent_bits=8,...]
    reduce_sum x3 -> x0, other arithmetic: 1.13 us -> none  [band(): jnp.sum(jnp.where(hits, taps_row[None, None, :], jnp.zeros((), taps_row.d...]
    dot_general x4 -> x0, matrix products: 0.99 us -> none  [the longest x1 0.38 us: local(): jnp.dot(snapshot.reshape(-1, cells_z), matrix_z, preferred_element_type=F32)]
  transfers between devices with their start and end apart: 19 -> 14, of which waited for: 11 -> 5; matrix products, arithmetic and copies ran while one was open for 7% -> 3% of each run, Pallas kernels for 0% -> 9%
where the time goes in v2:
time: 69.2 us; the launch traced here: 68.7 us
  Pallas kernels  31.2 us (45%)
  starting transfers between devices  18.3 us (26%)
  waiting for transfers between devices  11.9 us (17%)
  other arithmetic  5.15 us (7%)
  local copies, waits for them, and re-layouts  1.44 us (2%)
  between operations  0.8 us (1%)
    pallas_call x1, Pallas kernels, solve(): pl.pallas_call(lambda *refs: solve_kernel(*refs, total=total), out_shape=...  22 us
    ppermute x12, starting transfers between devices, swap(): lax.ppermute(block, axis, [(i, i ^ step) for i in range(lax.axis_size(axi...  11.2 us
    ppermute x12, waiting for transfers between devices, swap(): lax.ppermute(block, axis, [(i, i ^ step) for i in range(lax.axis_size(axi...  9.2 us
    ppermute x1, starting transfers between devices, fold_neighbours(): lax.ppermute(parts[0], axis, [(target, source) for source, target in forw...  7.01 us
    pallas_call x2, Pallas kernels, half_gram(): pl.pallas_call(gram_kernel, out_shape=jax.ShapeDtypeStruct((height, TILE)...  4.43 us
    pallas_call x1, Pallas kernels, local_filter(): pl.pallas_call(lambda *refs: filter_kernel(*refs, comps=comps, cells_x=ce...  2.79 us
    ppermute x1, waiting for transfers between devices, fold_neighbours(): low = lax.ppermute(parts[-1], axis, forward)  2.68 us
    pallas_call x1, Pallas kernels, local_cross(): pl.pallas_call(cross_kernel, out_shape=jax.ShapeDtypeStruct((height, TILE...  1.96 us
  transfers between devices with their start and end apart: 14, of which 5 were waited for; matrix products, arithmetic and copies ran while one was open for 3% of the time, Pallas kernels for 9%

profile of v2, /device:TPU:0, one launch (start us, length us, event | category | flops | bytes accessed | tf_op | source)
XLA Modules:
  0.0 68.7 jit_solution(9727392441842235)
XLA Ops:
  0.6 1.3 %convert_element_type.3.refs_0_ = f32[3,17]{1,0:T(4,128)} convert(bf16[3,17]{1,0:T(4,128)(2,1)} %param.5) | non-fusion elementwise | flops 51 | bytes 306 | tf_op jit(solution)/shard_map/convert_element_type | solution.py:128
  1.9 2.8 %filter.1 = f32[40,128]{1,0:T(8,128)} custom-call(f32[3,17]{1,0:T(4,128)} %convert_element_type.3.refs_0_, bf16[384,1024]{1,0:T(8,128)(2,1)} %bitcast.45), custom_call_target="tpu_custom_call" | custom-call | flops 201326592 | bytes 786432 | tf_op jit(solution)/shard_map/filter/pallas_call | solution.py:119
  4.7 0.8 %fusion.3 = (f32[9,128]{1,0:T(8,128)S(1)}, f32[9,128]{1,0:T(8,128)S(1)}, f32[9,128]{1,0:T(8,128)S(1)}) fusion(f32[40,128]{1,0:T(8,128)} %filter.1, pred[]{:T(512)S(6)} %eq.3), kind=kLoop, calls=%fused_computation.25 | loop fusion | flops 1152 | bytes 32257 | tf_op jit(solution)/shard_map/slice | solution.py:147
  6.1 2.2 %gram.3 = f32[640,128]{1,0:T(8,128)} custom-call(s32[1]{0:T(128)} %bitcast.3.side_ref, bf16[768,512]{1,0:T(8,128)(2,1)} %bitcast.39), custom_call_target="tpu_custom_call" | custom-call | flops 125829120 | bytes 327680 | tf_op jit(solution)/shard_map/gram/pallas_call | solution.py:66
  8.3 2.2 %gram.2 = f32[640,128]{1,0:T(8,128)} custom-call(s32[1]{0:T(128)} %bitcast.side_ref, bf16[768,512]{1,0:T(8,128)(2,1)} %bitcast.40), custom_call_target="tpu_custom_call" | custom-call | flops 125829120 | bytes 327680 | tf_op jit(solution)/shard_map/gram/pallas_call | solution.py:66
  10.6 7.0 %collective-permute-start.6 = (f32[2,3,128]{2,0,1:T(2,128)S(1)}, f32[2,3,128]{2,0,1:T(2,128)S(1)}, u32[]{:S(2)}, u32[]{:S(2)}) collective-permute-start(f32[2,3,128]{2,0,1:T(2,128)S(1)} %get-tuple-element.18), channel_id=1, source_target_pairs={{2,0},{4,2},{6,4},{8,6},{10,8},{12,10},{14,12},{16,14},{18,16},{20... | collective-permute-start | bytes 9224 | tf_op jit(solution)/shard_map/ppermute | solution.py:143
  17.7 1.0 %add.55 = f32[640,128]{1,0:T(8,128)S(1)} add(f32[640,128]{1,0:T(8,128)} %gram.2, f32[640,128]{1,0:T(8,128)S(1)} %collective-permute-done) | non-fusion elementwise | flops 81920 | bytes 983040 | tf_op jit(solution)/shard_map/add | solution.py:364
  18.8 0.9 %collective-permute-start.3 = (f32[160,128]{1,0:T(8,128)S(1)}, f32[160,128]{1,0:T(8,128)S(1)}, u32[]{:S(2)}, u32[]{:S(2)}) collective-permute-start(f32[160,128]{1,0:T(8,128)S(1)} %get-tuple-element.13), channel_id=1, source_target_pairs={{0,6},{2,4},{4,2},{6,0},{8,14},{10,12},{12,10},{14,8},{16,22},{18,... | collective-permute-start | bytes 245768 | tf_op jit(solution)/shard_map/ppermute | solution.py:17
  19.6 2.6 %collective-permute-start.2 = (f32[160,128]{1,0:T(8,128)S(1)}, f32[160,128]{1,0:T(8,128)S(1)}, u32[]{:S(2)}, u32[]{:S(2)}) collective-permute-start(f32[160,128]{1,0:T(8,128)S(1)} %get-tuple-element.14), channel_id=1, source_target_pairs={{0,4},{2,6},{4,0},{6,2},{8,12},{10,14},{12,8},{14,10},{16,20},{18,... | collective-permute-start | bytes 245768 | tf_op jit(solution)/shard_map/ppermute | solution.py:17
  22.3 2.7 %collective-permute-done.5 = f32[2,3,128]{2,0,1:T(2,128)S(1)} collective-permute-done((f32[2,3,128]{2,0,1:T(2,128)S(1)}, f32[2,3,128]{2,0,1:T(2,128)S(1)}, u32[]{:S(2)}, u32[]{:S(2)}) %collective-permute-start.5) | collective-permute-done | bytes 3104 | tf_op jit(solution)/shard_map/ppermute | solution.py:142
  25.0 0.6 reshape.44.fresh_ref
  25.6 2.0 %cross.1 = f32[8,128]{1,0:T(8,128)} custom-call(f32[6,128]{1,0:T(8,128)} %reshape.44.fresh_ref, bf16[768,512]{1,0:T(8,128)(2,1)} %bitcast.41), custom_call_target="tpu_custom_call" | custom-call | flops 6291456 | bytes 786432 | tf_op jit(solution)/shard_map/cross/pallas_call | solution.py:170
  27.6 0.7 %pad_maximum_fusion = f32[168,128]{1,0:T(8,128)S(1)} fusion(f32[8,128]{1,0:T(8,128)} %cross.1, f32[160,128]{1,0:T(8,128)S(1)} %fusion.1), kind=kLoop, calls=%fused_computation | loop fusion | flops 21504 | bytes 172032 | tf_op jit(solution)/shard_map/concatenate | solution.py:388
  28.3 2.3 %collective-permute-start.9 = (f32[168,128]{1,0:T(8,128)S(1)}, f32[168,128]{1,0:T(8,128)S(1)}, u32[]{:S(2)}, u32[]{:S(2)}) collective-permute-start(f32[168,128]{1,0:T(8,128)S(1)} %pad_maximum_fusion), channel_id=1, source_target_pairs={{0,24},{2,26},{4,28},{6,30},{8,16},{10,18},{12,20},{14,22},{16,8},... | collective-permute-start | bytes 258056 | tf_op jit(solution)/shard_map/ppermute | solution.py:17
  30.6 1.2 %collective-permute-start.7 = (f32[168,128]{1,0:T(8,128)S(1)}, f32[168,128]{1,0:T(8,128)S(1)}, u32[]{:S(2)}, u32[]{:S(2)}) collective-permute-start(f32[168,128]{1,0:T(8,128)S(1)} %pad_maximum_fusion), channel_id=1, source_target_pairs={{0,8},{2,10},{4,12},{6,14},{8,0},{10,2},{12,4},{14,6},{16,24},{18,... | collective-permute-start | bytes 258056 | tf_op jit(solution)/shard_map/ppermute | solution.py:17
  31.8 4.5 %collective-permute-done.8 = f32[168,128]{1,0:T(8,128)S(1)} collective-permute-done((f32[168,128]{1,0:T(8,128)S(1)}, f32[168,128]{1,0:T(8,128)S(1)}, u32[]{:S(2)}, u32[]{:S(2)}) %collective-permute-start.8) | collective-permute-done | bytes 86048 | tf_op jit(solution)/shard_map/ppermute | solution.py:17
  36.8 0.7 %add_add_fusion = f32[168,128]{1,0:T(8,128)S(1)} fusion(f32[168,128]{1,0:T(8,128)S(1)} %collective-permute-done.9, f32[168,128]{1,0:T(8,128)S(1)} %collective-permute-done.8, f32[168,128]{1,0:T(8,128)S(1)} %collective-permute-done.7, f32[8,128]{1,0:T(8,128)} %cross.1, f32[160,128]{1,0:T(8,128)S(1)} %fusion.1), kind=kLoop, calls=%fused_computation.1 | loop fusion | flops 86016 | bytes 430080 | tf_op jit(solution)/shard_map/add | solution.py:390
  37.5 1.1 %collective-permute-start.12 = (f32[168,128]{1,0:T(8,128)S(1)}, f32[168,128]{1,0:T(8,128)S(1)}, u32[]{:S(2)}, u32[]{:S(2)}) collective-permute-start(f32[168,128]{1,0:T(8,128)S(1)} %add_add_fusion), channel_id=1, source_target_pairs={{0,6},{2,4},{4,2},{6,0},{8,14},{10,12},{12,10},{14,8},{16,22},{18,... | collective-permute-start | bytes 258056 | tf_op jit(solution)/shard_map/ppermute | solution.py:17
  38.6 1.1 %collective-permute-start.11 = (f32[168,128]{1,0:T(8,128)S(1)}, f32[168,128]{1,0:T(8,128)S(1)}, u32[]{:S(2)}, u32[]{:S(2)}) collective-permute-start(f32[168,128]{1,0:T(8,128)S(1)} %add_add_fusion), channel_id=1, source_target_pairs={{0,4},{2,6},{4,0},{6,2},{8,12},{10,14},{12,8},{14,10},{16,20},{18,... | collective-permute-start | bytes 258056 | tf_op jit(solution)/shard_map/ppermute | solution.py:17
  39.7 1.4 %collective-permute-start.10 = (f32[168,128]{1,0:T(8,128)S(1)}, f32[168,128]{1,0:T(8,128)S(1)}, u32[]{:S(2)}, u32[]{:S(2)}) collective-permute-start(f32[168,128]{1,0:T(8,128)S(1)} %add_add_fusion), channel_id=1, source_target_pairs={{0,2},{2,0},{4,6},{6,4},{8,10},{10,8},{12,14},{14,12},{16,18},{18,... | collective-permute-start | bytes 258056 | tf_op jit(solution)/shard_map/ppermute | solution.py:17
  41.1 3.1 %collective-permute-done.10 = f32[168,128]{1,0:T(8,128)S(1)} collective-permute-done((f32[168,128]{1,0:T(8,128)S(1)}, f32[168,128]{1,0:T(8,128)S(1)}, u32[]{:S(2)}, u32[]{:S(2)}) %collective-permute-start.10) | collective-permute-done | bytes 86048 | tf_op jit(solution)/shard_map/ppermute | solution.py:17
  44.9 1.0 %collective-permute-done.13.refs_2_ = f32[648,128]{1,0:T(8,128)S(1)} collective-permute-done((f32[648,128]{1,0:T(8,128)S(1)}, f32[648,128]{1,0:T(8,128)S(1)}, u32[]{:S(2)}, u32[]{:S(2)}) %collective-permute-start.13) | collective-permute-done | bytes 331808 | tf_op jit(solution)/shard_map/ppermute | solution.py:17
  46.0 0.7 %copy-done.2 = f32[648,128]{1,0:T(8,128)} copy-done((f32[648,128]{1,0:T(8,128)}, f32[648,128]{1,0:T(8,128)S(1)}, u32[]{:S(2)}) %copy-start.2) | copy-done | bytes 331800
  46.7 22.0 %solve.1 = (bf16[768,512]{1,0:T(8,128)(2,1)}, f32[1,768]{1,0:T(1,128)}, f32[513,513]{1,0:T(8,128)}) custom-call(s32[2]{0:T(128)} %pad_add_fusion.refs_0_, f32[648,128]{1,0:T(8,128)} %copy-done, f32[648,128]{1,0:T(8,128)} %copy-done.2, f32[1,768]{1,0:T(1,128)} %bitcast.47, bf16[768,512]{1,0:T(8,128)(2,1)} %bitcast.42), custom_call_target="tpu_custom_call" | custom-call | flops 805306368 | bytes 2097152 | tf_op jit(solution)/shard_map/solve/pallas_call | solution.py:335
  (38 shorter events, 2.0 us)
Async XLA Ops:
  5.5 5.0 %collective-permute-start.4 = (f32[3,3,128]{2,1,0:T(4,128)S(1)}, f32[3,3,128]{2,1,0:T(4,128)S(1)}, u32[]{:S(2)}, u32[]{:S(2)}) collective-permute-start(f32[3,3,128]{2,1,0:T(4,128)S(1)} %select_n.41), channel_id=1, source_target_pairs={{0,1},{1,0},{2,3},{3,2},{4,5},{5,4},{6,7},{7,6},{8,9},{9,8},{10,11... | collective-permute-start | bytes 13832 | tf_op jit(solution)/shard_map/ppermute | solution.py:17
  8.3 9.4 %collective-permute-start = (f32[640,128]{1,0:T(8,128)}, f32[640,128]{1,0:T(8,128)S(1)}, u32[]{:S(2)}, u32[]{:S(2)}) collective-permute-start(f32[640,128]{1,0:T(8,128)} %gram.3), channel_id=1, source_target_pairs={{0,1},{1,0},{2,3},{3,2},{4,5},{5,4},{6,7},{7,6},{8,9},{9,8},{10,11... | collective-permute-start | bytes 983048 | tf_op jit(solution)/shard_map/ppermute | solution.py:17
  10.6 11.6 %collective-permute-start.6 = (f32[2,3,128]{2,0,1:T(2,128)S(1)}, f32[2,3,128]{2,0,1:T(2,128)S(1)}, u32[]{:S(2)}, u32[]{:S(2)}) collective-permute-start(f32[2,3,128]{2,0,1:T(2,128)S(1)} %get-tuple-element.18), channel_id=1, source_target_pairs={{2,0},{4,2},{6,4},{8,6},{10,8},{12,10},{14,12},{16,14},{18,16},{20... | collective-permute-start | bytes 9224 | tf_op jit(solution)/shard_map/ppermute | solution.py:143
  17.7 7.3 %collective-permute-start.5 = (f32[2,3,128]{2,0,1:T(2,128)S(1)}, f32[2,3,128]{2,0,1:T(2,128)S(1)}, u32[]{:S(2)}, u32[]{:S(2)}) collective-permute-start(f32[2,3,128]{2,0,1:T(2,128)S(1)} %get-tuple-element.19), channel_id=1, source_target_pairs={{0,2},{2,4},{4,6},{6,8},{8,10},{10,12},{12,14},{14,16},{16,18},{18... | collective-permute-start | bytes 9224 | tf_op jit(solution)/shard_map/ppermute | solution.py:142
  18.7 8.8 %collective-permute-start.1 = (f32[160,128]{1,0:T(8,128)S(1)}, f32[160,128]{1,0:T(8,128)S(1)}, u32[]{:S(2)}, u32[]{:S(2)}) collective-permute-start(f32[160,128]{1,0:T(8,128)S(1)} %get-tuple-element.12), channel_id=1, source_target_pairs={{0,2},{2,0},{4,6},{6,4},{8,10},{10,8},{12,14},{14,12},{16,18},{18,... | collective-permute-start | bytes 245768 | tf_op jit(solution)/shard_map/ppermute | solution.py:17
  18.8 8.7 %collective-permute-start.3 = (f32[160,128]{1,0:T(8,128)S(1)}, f32[160,128]{1,0:T(8,128)S(1)}, u32[]{:S(2)}, u32[]{:S(2)}) collective-permute-start(f32[160,128]{1,0:T(8,128)S(1)} %get-tuple-element.13), channel_id=1, source_target_pairs={{0,6},{2,4},{4,2},{6,0},{8,14},{10,12},{12,10},{14,8},{16,22},{18,... | collective-permute-start | bytes 245768 | tf_op jit(solution)/shard_map/ppermute | solution.py:17
  19.6 7.9 %collective-permute-start.2 = (f32[160,128]{1,0:T(8,128)S(1)}, f32[160,128]{1,0:T(8,128)S(1)}, u32[]{:S(2)}, u32[]{:S(2)}) collective-permute-start(f32[160,128]{1,0:T(8,128)S(1)} %get-tuple-element.14), channel_id=1, source_target_pairs={{0,4},{2,6},{4,0},{6,2},{8,12},{10,14},{12,8},{14,10},{16,20},{18,... | collective-permute-start | bytes 245768 | tf_op jit(solution)/shard_map/ppermute | solution.py:17
  25.0 21.0 %copy-start.1 = (f32[1,2,3,128]{3,1,2,0:T(2,128)}, f32[1,2,3,128]{3,1,2,0:T(2,128)S(1)}, u32[]{:S(2)}) copy-start(f32[1,2,3,128]{3,1,2,0:T(2,128)S(1)} %fusion.2) | copy-start | bytes 9220
  28.3 8.0 %collective-permute-start.8 = (f32[168,128]{1,0:T(8,128)S(1)}, f32[168,128]{1,0:T(8,128)S(1)}, u32[]{:S(2)}, u32[]{:S(2)}) collective-permute-start(f32[168,128]{1,0:T(8,128)S(1)} %pad_maximum_fusion), channel_id=1, source_target_pairs={{0,16},{2,18},{4,20},{6,22},{8,24},{10,26},{12,28},{14,30},{16,0},... | collective-permute-start | bytes 258056 | tf_op jit(solution)/shard_map/ppermute | solution.py:17
  28.3 8.0 %collective-permute-start.9 = (f32[168,128]{1,0:T(8,128)S(1)}, f32[168,128]{1,0:T(8,128)S(1)}, u32[]{:S(2)}, u32[]{:S(2)}) collective-permute-start(f32[168,128]{1,0:T(8,128)S(1)} %pad_maximum_fusion), channel_id=1, source_target_pairs={{0,24},{2,26},{4,28},{6,30},{8,16},{10,18},{12,20},{14,22},{16,8},... | collective-permute-start | bytes 258056 | tf_op jit(solution)/shard_map/ppermute | solution.py:17
  30.6 6.2 %collective-permute-start.7 = (f32[168,128]{1,0:T(8,128)S(1)}, f32[168,128]{1,0:T(8,128)S(1)}, u32[]{:S(2)}, u32[]{:S(2)}) collective-permute-start(f32[168,128]{1,0:T(8,128)S(1)} %pad_maximum_fusion), channel_id=1, source_target_pairs={{0,8},{2,10},{4,12},{6,14},{8,0},{10,2},{12,4},{14,6},{16,24},{18,... | collective-permute-start | bytes 258056 | tf_op jit(solution)/shard_map/ppermute | solution.py:17
  37.5 6.7 %collective-permute-start.12 = (f32[168,128]{1,0:T(8,128)S(1)}, f32[168,128]{1,0:T(8,128)S(1)}, u32[]{:S(2)}, u32[]{:S(2)}) collective-permute-start(f32[168,128]{1,0:T(8,128)S(1)} %add_add_fusion), channel_id=1, source_target_pairs={{0,6},{2,4},{4,2},{6,0},{8,14},{10,12},{12,10},{14,8},{16,22},{18,... | collective-permute-start | bytes 258056 | tf_op jit(solution)/shard_map/ppermute | solution.py:17
  38.6 5.6 %collective-permute-start.11 = (f32[168,128]{1,0:T(8,128)S(1)}, f32[168,128]{1,0:T(8,128)S(1)}, u32[]{:S(2)}, u32[]{:S(2)}) collective-permute-start(f32[168,128]{1,0:T(8,128)S(1)} %add_add_fusion), channel_id=1, source_target_pairs={{0,4},{2,6},{4,0},{6,2},{8,12},{10,14},{12,8},{14,10},{16,20},{18,... | collective-permute-start | bytes 258056 | tf_op jit(solution)/shard_map/ppermute | solution.py:17
  39.7 4.5 %collective-permute-start.10 = (f32[168,128]{1,0:T(8,128)S(1)}, f32[168,128]{1,0:T(8,128)S(1)}, u32[]{:S(2)}, u32[]{:S(2)}) collective-permute-start(f32[168,128]{1,0:T(8,128)S(1)} %add_add_fusion), channel_id=1, source_target_pairs={{0,2},{2,0},{4,6},{6,4},{8,10},{10,8},{12,14},{14,12},{16,18},{18,... | collective-permute-start | bytes 258056 | tf_op jit(solution)/shard_map/ppermute | solution.py:17
  44.3 1.7 %copy-start = (f32[648,128]{1,0:T(8,128)}, f32[648,128]{1,0:T(8,128)S(1)}, u32[]{:S(2)}) copy-start(f32[648,128]{1,0:T(8,128)S(1)} %constant_dynamic-update-slice_fusion.refs_1_) | copy-start | bytes 995332
  44.3 1.7 %collective-permute-start.13 = (f32[648,128]{1,0:T(8,128)S(1)}, f32[648,128]{1,0:T(8,128)S(1)}, u32[]{:S(2)}, u32[]{:S(2)}) collective-permute-start(f32[648,128]{1,0:T(8,128)S(1)} %constant_dynamic-update-slice_fusion.refs_1_), channel_id=1, source_target_pairs={{0,1},{1,0},{2,3},{3,2},{4,5},{5,4},{6,7},{7,6},{8,9},{9,8},{10,11... | collective-permute-start | bytes 995336 | tf_op jit(solution)/shard_map/ppermute | solution.py:17
  46.0 0.7 %copy-start.2 = (f32[648,128]{1,0:T(8,128)}, f32[648,128]{1,0:T(8,128)S(1)}, u32[]{:S(2)}) copy-start(f32[648,128]{1,0:T(8,128)S(1)} %collective-permute-done.13.refs_2_) | copy-start | bytes 995332

commit v3 on v2

v3 whole, which is shorter than its diff:
```python
import jax
import jax.numpy as jnp
from jax import lax
from jax.experimental import pallas as pl
from jax.experimental.pallas import tpu as pltpu
from jax.sharding import PartitionSpec as P

STRIDE = 8
TILE = 128
PIVOTS = 32
F32 = jnp.float32
BF16 = jnp.bfloat16
HIGHEST = lax.Precision.HIGHEST


def swap(block, axis, step):
    return lax.ppermute(block, axis, [(i, i ^ step) for i in range(lax.axis_size(axis))])


def bit_groups(size):
    groups, bit = [], 1
    while bit < size:
        groups.append((bit, 2 * bit, 3 * bit) if 4 * bit <= size else (bit,))
        bit *= 4 if 4 * bit <= size else 2
    return groups


def contract_rows(a, b, precision=None):
    return lax.dot_general(
        a, b, (((0,), (0,)), ((), ())), precision=precision, preferred_element_type=F32
    )


def contract_lanes(a, b, precision=None):
    return lax.dot_general(
        a, b, (((1,), (1,)), ((), ())), precision=precision, preferred_element_type=F32
    )


def upper_blocks(chunks):
    return [(p, c) for p in range(chunks) for c in range(p, chunks)]


def gram_kernel(side_ref, rows_ref, out_ref):
    blocks = upper_blocks(rows_ref.shape[1] // TILE)
    half = len(blocks) // 2
    for side in range(2):

        @pl.when(side_ref[0] == side)
        def _():
            mine = blocks[half * side : half * (side + 1)]
            for p in sorted({p for p, _ in mine}):
                cols = [c for q, c in mine if q == p]
                part = contract_rows(
                    rows_ref[:, TILE * p : TILE * (p + 1)],
                    rows_ref[:, TILE * cols[0] : TILE * (cols[-1] + 1)],
                )
                for c in cols:
                    at = TILE * mine.index((p, c))
                    out_ref[at : at + TILE, :] = part[:, TILE * (c - cols[0]) : TILE * (c - cols[0] + 1)]


def half_gram(side, rows):
    count, modes = rows.shape
    height = TILE * len(upper_blocks(modes // TILE)) // 2
    return pl.pallas_call(
        gram_kernel,
        out_shape=jax.ShapeDtypeStruct((height, TILE), F32),
        in_specs=[pl.BlockSpec(memory_space=pltpu.SMEM), pl.BlockSpec(memory_space=pltpu.VMEM)],
        cost_estimate=pl.CostEstimate(
            flops=2 * count * height * TILE, bytes_accessed=4 * height * TILE, transcendentals=0
        ),
        compiler_params=pltpu.CompilerParams(vmem_limit_bytes=4 << 20),
        name="gram",
    )(side.reshape(1), rows)


def weights(taps_ref, direction, lag):
    line = taps_ref[...].astype(F32)[direction : direction + 1, :]
    found = jnp.zeros(lag.shape, F32)
    for tap in range(2 * STRIDE + 1):
        value = jnp.broadcast_to(line[:, tap : tap + 1], (1, lag.shape[1]))
        found = jnp.where(lag == tap, value, found)
    return found


def parted(index, size, bound):
    if size & (size - 1) == 0:
        return index >> (size.bit_length() - 1), index & (size - 1)
    scale = -(-(1 << 16) // size)
    assert all((i * scale) >> 16 == i // size for i in range(bound))
    quotient = (index * scale) >> 16
    return quotient, index - size * quotient


def filter_kernel(taps_ref, cells_ref, out_ref, band, *, comps, cells_x, cells_y):
    depth, points = band.shape
    height = out_ref.shape[0]
    z = lax.broadcasted_iota(jnp.int32, (TILE, points), 0)
    p = lax.broadcasted_iota(jnp.int32, (TILE, points), 1)
    lag = z - STRIDE * p + STRIDE
    pattern = weights(taps_ref, 2, jnp.where(lag < 0, lag + depth, lag))
    for block in range(depth // TILE):
        turned = pltpu.roll(pattern, TILE // STRIDE * block, 1) if block else pattern
        band[TILE * block : TILE * (block + 1), :] = turned.astype(BF16)
    along_z = jnp.dot(cells_ref[...], band[...], preferred_element_type=F32)
    count = cells_ref.shape[0]
    per_y = cells_y // STRIDE
    out = lax.broadcasted_iota(jnp.int32, (height, count), 0)
    cell = lax.broadcasted_iota(jnp.int32, (height, count), 1)
    slot, within = parted(out, height // 9, height)
    kind, r = parted(slot, 3, 9)
    comp, q = parted(within, per_y, height // 9)
    rest, y = parted(cell, cells_y, count)
    cell_comp, x = parted(rest, cells_x, count)
    y = y + jnp.where(kind == 1, -cells_y, jnp.where(kind == 2, cells_y, 0))
    weight = weights(taps_ref, 0, x - STRIDE * (r - 1) + STRIDE)
    weight = weight * weights(taps_ref, 1, y - STRIDE * q + STRIDE)
    weight = jnp.where(cell_comp == comp, weight, 0.0)
    out_ref[...] = jnp.dot(weight, along_z, precision=HIGHEST, preferred_element_type=F32)


def local_filter(taps, snapshot):
    comps, cells_x, cells_y, cells_z = snapshot.shape
    assert cells_x == STRIDE
    points = cells_z // STRIDE
    height = 9 * padded_rows(comps * cells_y // STRIDE)
    cells = snapshot.reshape(-1, cells_z)
    return pl.pallas_call(
        lambda *refs: filter_kernel(*refs, comps=comps, cells_x=cells_x, cells_y=cells_y),
        out_shape=jax.ShapeDtypeStruct((height, points), F32),
        scratch_shapes=[pltpu.VMEM((cells_z, points), BF16)],
        cost_estimate=pl.CostEstimate(
            flops=4 * cells.size * points, bytes_accessed=2 * cells.size, transcendentals=0
        ),
        compiler_params=pltpu.CompilerParams(vmem_limit_bytes=4 << 20),
        name="filter",
    )(taps, cells)


def padded_rows(rows):
    return -(-rows // 8) * 8


def along_slabs_y(parts):
    height = parts.shape[0] // 3
    own, up, down = parts[:height], parts[height : 2 * height], parts[2 * height :]
    count = lax.axis_size("gy")
    if count == 2:
        return own + swap(jnp.where(lax.axis_index("gy") == 1, down, up), "gy", 1)
    pairs = [(i, i + 1) for i in range(count - 1)]
    low = lax.ppermute(up, "gy", pairs)
    return own + low + lax.ppermute(down, "gy", [(j, i) for i, j in pairs])


def cross_kernel(own_ref, low_ref, high_ref, rows_ref, fresh_ref, out_ref):
    lines, points = fresh_ref.shape
    modes = rows_ref.shape[1]
    fresh = (own_ref[...] + low_ref[...] + high_ref[...]).astype(BF16).astype(F32)
    fresh_ref[...] = fresh[:lines, :]
    total = jnp.zeros((8, modes), F32)
    square = jnp.zeros((1, 1), F32)
    for i in range(lines):
        line = fresh[i : i + 1, :]
        square = square + jnp.sum(line * line, axis=1, keepdims=True)
        left = jnp.broadcast_to(line, (8, points)).astype(BF16)
        total = total + jnp.dot(
            left, rows_ref[points * i : points * (i + 1), :], preferred_element_type=F32
        )
    out_ref[...] = jnp.zeros(out_ref.shape, F32)
    for c in range(modes // TILE):
        out_ref[c : c + 1, :] = total[:1, TILE * c : TILE * (c + 1)]
    out_ref[modes // TILE : modes // TILE + 1, :] = jnp.broadcast_to(square, (1, TILE))


def local_cross(own, low, high, rows):
    points = own.shape[1]
    return pl.pallas_call(
        cross_kernel,
        out_shape=(
            jax.ShapeDtypeStruct((rows.shape[0] // points, points), F32),
            jax.ShapeDtypeStruct((padded_rows(rows.shape[1] // TILE + 1), TILE), F32),
        ),
        cost_estimate=pl.CostEstimate(flops=16 * rows.size, bytes_accessed=2 * rows.size, transcendentals=0),
        compiler_params=pltpu.CompilerParams(vmem_limit_bytes=4 << 20),
        name="cross",
    )(own, low, high, rows)


def split(value):
    parts = []
    for _ in range(3):
        parts.append(value.astype(BF16))
        value = value - parts[-1].astype(F32)
    return parts


def left_parts(value):
    a, b, c = split(value)
    return jnp.concatenate([a, a, b, b, a, c])


def right_parts(value):
    a, b, c = split(value)
    return jnp.concatenate([a, b, a, b, c, a])


def factor_blocks(work, scaled, upper):
    modes = work.shape[0]
    chunks = modes // TILE
    groups = PIVOTS // 8
    lane = lax.broadcasted_iota(jnp.int32, (8, TILE), 1)
    row = lax.broadcasted_iota(jnp.int32, (8, TILE), 0)
    scale_blocks = []
    for p in range(chunks):
        base = p * TILE
        for j in range(TILE // PIVOTS):
            first = PIVOTS * j
            top = base + first
            rows = [
                [work[top + 8 * g : top + 8 * g + 8, TILE * c : TILE * (c + 1)] for c in range(chunks)]
                for g in range(groups)
            ]
            cols = [
                [
                    jnp.broadcast_to(rows[g][p][:, first + k : first + k + 1], (8, TILE))
                    if g >= k // 8
                    else None
                    for g in range(groups)
                ]
                for k in range(PIVOTS)
            ]
            unit = [jnp.where(lane == first + 8 * g + row, 1.0, 0.0).astype(F32) for g in range(groups)]
            inverse = [jnp.zeros((8, TILE), F32) for _ in range(groups)]
            scale = [jnp.zeros((8, TILE), F32) for _ in range(groups)]
            for k in range(PIVOTS):
                own, sub = k // 8, k % 8
                pivot = cols[k][own][sub : sub + 1, :]
                recip = 1.0 / pivot
                inverse[own] = jnp.where(row == sub, recip, inverse[own])
                scale[own] = jnp.where(row == sub, lax.rsqrt(pivot), scale[own])
                mult = {g: cols[k][g] * recip for g in range(own, groups)}
                for later in range(k + 1, PIVOTS):
                    factor = cols[k][later // 8][later % 8 : later % 8 + 1, :]
                    for g in range(later // 8, groups):
                        cols[later][g] = cols[later][g] - mult[g] * factor
                mult[own] = jnp.where(row > sub, mult[own], 0.0)
                for c in range(chunks):
                    pivot_row = rows[own][c][sub : sub + 1, :]
                    for g in range(own, groups):
                        rows[g][c] = rows[g][c] - mult[g] * pivot_row
                pivot_row = unit[own][sub : sub + 1, :]
                for g in range(own, groups):
                    unit[g] = unit[g] - mult[g] * pivot_row
            inside = (lane >= first) & (lane < first + PIVOTS)
            for g in range(groups):
                where = slice(top + 8 * g, top + 8 * g + 8)
                for c in range(chunks):
                    cut = slice(TILE * c, TILE * (c + 1))
                    if c < p:
                        upper[where, cut] = jnp.zeros((8, TILE), F32)
                    elif c == p:
                        upper[where, cut] = jnp.where(
                            lane >= first + 8 * g + row, rows[g][c] * scale[g], 0.0
                        )
                    else:
                        upper[where, cut] = rows[g][c] * scale[g]
                    if c >= p:
                        scaled[first + 8 * g : first + 8 * g + 8, cut] = rows[g][c] * inverse[g]
                    work[where, cut] = jnp.where(inside, unit[g], rows[g][c]) if c == p else rows[g][c]
                scale_blocks.append(scale[g])
            end = first + PIVOTS
            if end < TILE:
                left = left_parts(jnp.concatenate([rows[g][p] * inverse[g] for g in range(groups)]))
                wide = lax.broadcasted_iota(jnp.int32, (TILE - end, TILE), 1)
                for cuts in ([p], [c for c in range(chunks) if c != p]):
                    right = [work[top : top + PIVOTS, TILE * c : TILE * (c + 1)] for c in cuts]
                    change = contract_rows(left, right_parts(jnp.concatenate(right, axis=1)))
                    for at, c in enumerate(cuts):
                        cut = slice(TILE * c, TILE * (c + 1))
                        old = work[base + end : base + TILE, cut]
                        if c == p:
                            old = jnp.where((wide >= first) & (wide < end), 0.0, old)
                        work[base + end : base + TILE, cut] = old - change[end:, TILE * at : TILE * (at + 1)]
        block_lane = lax.broadcasted_iota(jnp.int32, (TILE, TILE), 1)
        block_row = lax.broadcasted_iota(jnp.int32, (TILE, TILE), 0)
        own = slice(base, base + TILE)
        work[own, own] = jnp.where(block_lane <= block_row, work[own, own], 0.0)
        if p + 1 < chunks:
            left = left_parts(scaled[:, base + TILE :])
            right = right_parts(work[own, :])
        for i in range(p + 1, chunks):
            below = slice(TILE * i, TILE * (i + 1))
            part = left[:, TILE * (i - p - 1) : TILE * (i - p)]
            inverse_part = contract_rows(part, right[:, : base + TILE])
            if p:
                work[below, :base] = work[below, :base] - inverse_part[:, :base]
            work[below, own] = -inverse_part[:, base:]
            gram_part = contract_rows(part, right[:, TILE * i :])
            work[below, TILE * i :] = work[below, TILE * i :] - gram_part
    return scale_blocks


def factor_kernel(side_ref, member_ref, mine_ref, other_ref, inverse_ref, factor_ref, scaled, blocks, *, total):
    work = inverse_ref
    modes = work.shape[0]
    chunks = modes // TILE
    half = blocks.shape[0] // 2
    piece = half // 4
    for part_ref, side in ((mine_ref, side_ref[0]), (other_ref, 1 - side_ref[0])):
        for step in range(4):
            at = pl.multiple_of(half * side + piece * (member_ref[0] ^ step), 8)
            blocks[pl.ds(at, piece), :] = part_ref[piece * step : piece * (step + 1), :] * (1.0 / total)
    for at, (p, c) in enumerate(upper_blocks(chunks)):
        work[TILE * p : TILE * (p + 1), TILE * c : TILE * (c + 1)] = blocks[TILE * at : TILE * (at + 1), :]
    scales = factor_blocks(work, scaled, factor_ref)
    for g, scale in enumerate(scales):
        where = slice(8 * g, 8 * g + 8)
        for c in range(8 * g // TILE + 1):
            work[where, TILE * c : TILE * (c + 1)] = work[where, TILE * c : TILE * (c + 1)] * scale


def factored(side, member, mine, other, modes, total):
    height = TILE * len(upper_blocks(modes // TILE))
    smem, vmem = (pl.BlockSpec(memory_space=space) for space in (pltpu.SMEM, pltpu.VMEM))
    return pl.pallas_call(
        lambda *refs: factor_kernel(*refs, total=total),
        out_shape=(jax.ShapeDtypeStruct((modes, modes), F32),) * 2,
        in_specs=[smem, smem, vmem, vmem],
        scratch_shapes=[pltpu.VMEM((TILE, modes), F32), pltpu.VMEM((height, TILE), F32)],
        cost_estimate=pl.CostEstimate(
            flops=16 * modes**3, bytes_accessed=8 * modes * modes, transcendentals=modes
        ),
        compiler_params=pltpu.CompilerParams(vmem_limit_bytes=10 << 20),
        name="factor",
    )(side.reshape(1), member.reshape(1), mine, other)


def modes_kernel(inverse_ref, rows_ref, modes_ref):
    for p in range(inverse_ref.shape[0] // TILE):
        own = slice(TILE * p, TILE * (p + 1))
        width = TILE * (p + 1)
        known = inverse_ref[own, :width]
        first = known.astype(BF16)
        second = (known - first.astype(F32)).astype(BF16)
        left = rows_ref[:, :width]
        solved = contract_lanes(left, first) + contract_lanes(left, second)
        modes_ref[:, own] = solved.astype(BF16)


def solved_modes(inverse, rows):
    count, modes = rows.shape
    return pl.pallas_call(
        modes_kernel,
        out_shape=jax.ShapeDtypeStruct((count, modes), BF16),
        cost_estimate=pl.CostEstimate(
            flops=4 * count * modes * modes, bytes_accessed=4 * modes * modes, transcendentals=0
        ),
        compiler_params=pltpu.CompilerParams(vmem_limit_bytes=8 << 20),
        name="modes",
    )(inverse, rows)


def finish_kernel(inverse_ref, upper_ref, sums_ref, fresh_ref, rows_ref, mode_ref, factor_ref, *, total):
    modes = inverse_ref.shape[0]
    chunks = modes // TILE
    sums = sums_ref[...] * (1.0 / total)
    cross = [sums[c : c + 1, :] for c in range(chunks)]
    square = sums[chunks : chunks + 1, :]
    projected = []
    for p in range(chunks):
        own = slice(TILE * p, TILE * (p + 1))
        width = TILE * (p + 1)
        known = inverse_ref[own, :width]
        line = jnp.concatenate(cross[: p + 1], axis=1)
        projected.append(contract_lanes(jnp.broadcast_to(line, (8, width)), known, HIGHEST))
        column = sum(known[:, TILE * c : TILE * (c + 1)] * cross[c] for c in range(p + 1))
        factor_ref[own, :modes] = upper_ref[own, :]
        factor_ref[own, modes : modes + 1] = jnp.sum(column, axis=1, keepdims=True)
    norm = sum(jnp.sum(part * part, axis=1, keepdims=True) for part in projected)
    last = jnp.sqrt(square[:, :1] - norm[:1, :])
    back = []
    for c in range(chunks):
        own = slice(TILE * c, TILE * (c + 1))
        part = jnp.zeros((8, TILE), F32)
        for p in range(c, chunks):
            part = part + jnp.dot(
                projected[p],
                inverse_ref[TILE * p : TILE * (p + 1), own],
                precision=HIGHEST,
                preferred_element_type=F32,
            )
        back.append(part)
    share = jnp.concatenate(back, axis=1)
    first = share.astype(BF16)
    second = (share - first.astype(F32)).astype(BF16)
    points = fresh_ref.shape[1]
    for i in range(fresh_ref.shape[0]):
        left = rows_ref[points * i : points * (i + 1), :]
        covered = contract_lanes(first, left) + contract_lanes(second, left)
        mode_ref[:, points * i : points * (i + 1)] = (fresh_ref[i : i + 1, :] - covered[:1, :]) / last
    factor_ref[modes : modes + 1, :modes] = jnp.zeros((1, modes), F32)
    factor_ref[modes : modes + 1, modes : modes + 1] = last


def finish(inverse, upper, sums, fresh, rows, total):
    count, modes = rows.shape
    return pl.pallas_call(
        lambda *refs: finish_kernel(*refs, total=total),
        out_shape=(
            jax.ShapeDtypeStruct((1, count), F32),
            jax.ShapeDtypeStruct((modes + 1, modes + 1), F32),
        ),
        cost_estimate=pl.CostEstimate(
            flops=64 * modes * modes, bytes_accessed=8 * modes * modes, transcendentals=0
        ),
        compiler_params=pltpu.CompilerParams(vmem_limit_bytes=8 << 20),
        name="finish",
    )(inverse, upper, sums, fresh, rows)


def local(snapshot, basis, taps):
    modes = basis.shape[-1]
    rows = basis.reshape(-1, modes)
    total = rows.shape[0] * lax.axis_size("gx") * lax.axis_size("gy")
    side = lax.axis_index("gy") & 1
    place = lax.axis_index("gx")
    member = place & 3
    slabs = lax.axis_size("gx")
    first, *others = bit_groups(slabs)

    parts = local_filter(taps, snapshot)
    side, parts = lax.optimization_barrier((side, parts))
    parts = along_slabs_y(parts)
    away = swap(half_gram(1 - side, rows), "gy", 1)
    half = half_gram(side, rows) + away
    bit = 2
    while bit < lax.axis_size("gy"):
        half = half + swap(half, "gy", bit)
        bit *= 2

    piece = half.shape[0] // 4
    height = parts.shape[0] // 3
    quarters = half.reshape(4, piece, TILE)

    def quarter_of(index):
        return lax.dynamic_index_in_dim(quarters, index, 0, keepdims=False)

    before, own, after = parts[:height], parts[height : 2 * height], parts[2 * height :]
    odd = (member & 1) == 1
    riders = {1: jnp.where(odd, before, after), 3: jnp.where(odd, after, before)}
    got = {}
    for step in first:
        block = quarter_of(member ^ step)
        got[step] = swap(jnp.concatenate([block, riders[step]]) if step in riders else block, "gx", step)
    quarter = sum([got[step][:piece] for step in first], quarter_of(member))
    near, far = got[1][piece:], got[3][piece:]

    if slabs == 16:
        got = {}
        for step in others[0]:
            block = jnp.concatenate([quarter, far]) if step != 8 else quarter
            got[step] = swap(block, "gx", step)
        quarter = sum([block[:piece] for block in got.values()], quarter)
        group = place >> 2
        wanted = jnp.where(member == 0, group - 1, group + 1) & 3
        outer = jnp.where((group ^ wanted) == 1, got[4][piece:], got[12][piece:])
        far = jnp.where((member == 0) | (member == 3), outer, far)
    else:
        for steps in others:
            quarter = sum([swap(quarter, "gx", step) for step in steps], quarter)
        forward = [(i, (i + 1) % slabs) for i in range(slabs)]
        near = lax.ppermute(after, "gx", forward)
        far = lax.ppermute(before, "gx", [(j, i) for i, j in forward])

    fresh, cross = local_cross(own, near, far, rows)
    block = jnp.concatenate([quarter, cross])
    gathered = [block] + [swap(block, "gx", step) for step in first]
    sums = sum([got[piece:] for got in gathered[1:]], block[piece:])
    mine = jnp.concatenate([got[:piece] for got in gathered] + [sums])
    other = swap(mine, "gy", 1)
    sums = mine[4 * piece :] + other[4 * piece :]
    bit = 2
    while bit < lax.axis_size("gy"):
        sums = sums + swap(sums, "gy", bit)
        bit *= 2
    bit = 4
    while 2 * bit < slabs:
        sums = sums + swap(sums, "gx", bit)
        bit *= 2
    inverse, upper = factored(side, member, mine, other, modes, total)
    sums, inverse = lax.optimization_barrier((sums, inverse))
    if bit < slabs:
        sums = sums + swap(sums, "gx", bit)
    new_modes = solved_modes(inverse, rows)
    new_mode, factor = finish(inverse, upper, sums, fresh, rows, total)
    return (new_modes.reshape(basis.shape), new_mode.reshape(basis.shape[:-1]), factor)


def solution(mesh):
    in_specs = (P(None, "gx", "gy", None), P(None, "gx", "gy", None, None), P())
    out_specs = (P(None, "gx", "gy", None, None), P(None, "gx", "gy", None), P())
    return jax.shard_map(local, mesh=mesh, in_specs=in_specs, out_specs=out_specs, check_vma=False)
```

time: 69.2 us -> 58.3 us (0.84)
  Pallas kernels: 31.2 us -> 21.8 us
  waiting for transfers between devices: 11.9 us -> 17 us
  other arithmetic: 5.15 us -> 0.16 us
  starting transfers between devices: 18.3 us -> 16.3 us
    ppermute x12 -> x14, waiting for transfers between devices: 9.2 us -> 17 us  [swap(): lax.ppermute(block, axis, [(i, i ^ step) for i in range(lax.axis_size(axi...]
    ppermute x2 -> x0, starting transfers between devices: 7.01 us -> none  [the longest x1 7.01 us: fold_neighbours(): lax.ppermute(parts[0], axis, [(target, source) for source, target in forw...]
    ppermute x12 -> x14, starting transfers between devices: 11.2 us -> 16.3 us  [swap(): lax.ppermute(block, axis, [(i, i ^ step) for i in range(lax.axis_size(axi...]
    pallas_call x2 -> x4, Pallas kernels: 24 us -> 19.7 us  [the longest x1 14.6 us: factored(): pl.pallas_call(lambda *refs: factor_kernel(*refs, total=total), out_shape...]
    pallas_call x2, Pallas kernels: 4.43 us -> 0.89 us  [half_gram(): pl.pallas_call(gram_kernel, out_shape=jax.ShapeDtypeStruct((height, TILE)...]
    ppermute x2 -> x0, waiting for transfers between devices: 2.69 us -> none  [the longest x1 2.68 us: fold_neighbours(): low = lax.ppermute(parts[-1], axis, forward)]
    pallas_call x1, Pallas kernels: 2.79 us -> 1.25 us  [local_filter(): pl.pallas_call(lambda *refs: filter_kernel(*refs, comps=comps, cells_x=ce...]
    convert_element_type x1 -> x0, other arithmetic: 1.26 us -> none  [local_filter(): taps.astype(F32)]
  transfers between devices with their start and end apart: 14 -> 14, of which waited for: 5 -> 9; matrix products, arithmetic and copies ran while one was open for 3% -> 0% of each run, Pallas kernels for 9% -> 31%
where the time goes in v3:
time: 58.3 us; the launch traced here: 58.1 us
  Pallas kernels  21.8 us (37%)
  waiting for transfers between devices  17 us (29%)
  starting transfers between devices  16.3 us (28%)
  local copies, waits for them, and re-layouts  1.93 us (3%)
  between operations  0.81 us (1%)
    ppermute x14, waiting for transfers between devices, swap(): lax.ppermute(block, axis, [(i, i ^ step) for i in range(lax.axis_size(axi...  17 us
    ppermute x14, starting transfers between devices, swap(): lax.ppermute(block, axis, [(i, i ^ step) for i in range(lax.axis_size(axi...  16.3 us
    pallas_call x1, Pallas kernels, factored(): pl.pallas_call(lambda *refs: factor_kernel(*refs, total=total), out_shape...  14.6 us
    pallas_call x1, Pallas kernels, finish(): pl.pallas_call(lambda *refs: finish_kernel(*refs, total=total), out_shape...  2.82 us
    pallas_call x1, Pallas kernels, solved_modes(): pl.pallas_call(modes_kernel, out_shape=jax.ShapeDtypeStruct((count, modes...  2.07 us
    unnamed x9, local copies, waits for them, and re-layouts  1.9 us
    pallas_call x1, Pallas kernels, local_filter(): pl.pallas_call(lambda *refs: filter_kernel(*refs, comps=comps, cells_x=ce...  1.25 us
  transfers between devices with their start and end apart: 14, of which 9 were waited for; matrix products, arithmetic and copies ran while one was open for 0% of the time, Pallas kernels for 31%

profile of v3, /device:TPU:0, one launch (start us, length us, event | category | flops | bytes accessed | tf_op | source)
XLA Modules:
  0.0 58.1 jit_solution(17635483914449619666)
XLA Ops:
  0.7 1.2 %copy-done.1 = bf16[3,8,16,1024]{3,2,1,0:T(8,128)(2,1)S(1)} copy-done((bf16[3,8,16,1024]{3,2,1,0:T(8,128)(2,1)S(1)}, bf16[3,8,16,1024]{3,2,1,0:T(8,128)(2,1)}, u32[]{:S(2)}) %copy-start.1) | copy-done | bytes 786456
  1.9 0.7 %copy-done.2 = bf16[3,17]{1,0:T(4,128)(2,1)S(1)} copy-done((bf16[3,17]{1,0:T(4,128)(2,1)S(1)}, bf16[3,17]{1,0:T(4,128)(2,1)}, u32[]{:S(2)}) %copy-start.2) | copy-done | bytes 126
  2.5 1.2 %filter.1 = f32[72,128]{1,0:T(8,128)S(1)} custom-call(bf16[3,17]{1,0:T(4,128)(2,1)S(1)} %copy-done.2, bf16[384,1024]{1,0:T(8,128)(2,1)S(1)} %bitcast.25), custom_call_target="tpu_custom_call" | custom-call | flops 201326592 | bytes 786432 | tf_op jit(solution)/shard_map/filter/pallas_call | solution.py:129
  3.8 0.6 collective-permute-start
  4.8 0.5 gram.2
  5.4 1.0 %collective-permute-done.1 = f32[640,128]{1,0:T(8,128)S(1)} collective-permute-done((f32[640,128]{1,0:T(8,128)S(1)}, f32[640,128]{1,0:T(8,128)S(1)}, u32[]{:S(2)}, u32[]{:S(2)}) %collective-permute-start.1) | collective-permute-done | bytes 327712 | tf_op jit(solution)/shard_map/ppermute | solution.py:17
  6.5 3.6 %collective-permute-start.4 = (f32[168,128]{1,0:T(8,128)S(1)}, f32[168,128]{1,0:T(8,128)S(1)}, u32[]{:S(2)}, u32[]{:S(2)}) collective-permute-start(f32[168,128]{1,0:T(8,128)S(1)} %pad_maximum_fusion.1), channel_id=1, source_target_pairs={{0,6},{2,4},{4,2},{6,0},{8,14},{10,12},{12,10},{14,8},{16,22},{18,... | collective-permute-start | bytes 258056 | tf_op jit(solution)/shard_map/ppermute | solution.py:17
  10.1 0.5 collective-permute-start.2
  10.8 2.7 %collective-permute-done.4 = f32[168,128]{1,0:T(8,128)S(1)} collective-permute-done((f32[168,128]{1,0:T(8,128)S(1)}, f32[168,128]{1,0:T(8,128)S(1)}, u32[]{:S(2)}, u32[]{:S(2)}) %collective-permute-start.4) | collective-permute-done | bytes 86048 | tf_op jit(solution)/shard_map/ppermute | solution.py:17
  13.5 1.6 %collective-permute-done.3 = f32[160,128]{1,0:T(8,128)S(1)} collective-permute-done((f32[160,128]{1,0:T(8,128)S(1)}, f32[160,128]{1,0:T(8,128)S(1)}, u32[]{:S(2)}, u32[]{:S(2)}) %collective-permute-start.3) | collective-permute-done | bytes 81952 | tf_op jit(solution)/shard_map/ppermute | solution.py:17
  15.3 3.7 %collective-permute-start.6 = (f32[168,128]{1,0:T(8,128)S(1)}, f32[168,128]{1,0:T(8,128)S(1)}, u32[]{:S(2)}, u32[]{:S(2)}) collective-permute-start(f32[168,128]{1,0:T(8,128)S(1)} %pad_maximum_fusion.2), channel_id=1, source_target_pairs={{0,24},{2,26},{4,28},{6,30},{8,16},{10,18},{12,20},{14,22},{16,8},... | collective-permute-start | bytes 258056 | tf_op jit(solution)/shard_map/ppermute | solution.py:17
  19.0 0.8 %collective-permute-start.7 = (f32[160,128]{1,0:T(8,128)S(1)}, f32[160,128]{1,0:T(8,128)S(1)}, u32[]{:S(2)}, u32[]{:S(2)}) collective-permute-start(f32[160,128]{1,0:T(8,128)S(1)} %slice_add_fusion.2), channel_id=1, source_target_pairs={{0,16},{2,18},{4,20},{6,22},{8,24},{10,26},{12,28},{14,30},{16,0},... | collective-permute-start | bytes 245768 | tf_op jit(solution)/shard_map/ppermute | solution.py:17
  19.8 2.5 %collective-permute-done.6 = f32[168,128]{1,0:T(8,128)S(1)} collective-permute-done((f32[168,128]{1,0:T(8,128)S(1)}, f32[168,128]{1,0:T(8,128)S(1)}, u32[]{:S(2)}, u32[]{:S(2)}) %collective-permute-start.6) | collective-permute-done | bytes 86048 | tf_op jit(solution)/shard_map/ppermute | solution.py:17
  22.3 3.1 %collective-permute-done.5 = f32[168,128]{1,0:T(8,128)S(1)} collective-permute-done((f32[168,128]{1,0:T(8,128)S(1)}, f32[168,128]{1,0:T(8,128)S(1)}, u32[]{:S(2)}, u32[]{:S(2)}) %collective-permute-start.5) | collective-permute-done | bytes 86048 | tf_op jit(solution)/shard_map/ppermute | solution.py:17
  25.6 1.6 %collective-permute-start.8 = (f32[168,128]{1,0:T(8,128)S(1)}, f32[168,128]{1,0:T(8,128)S(1)}, u32[]{:S(2)}, u32[]{:S(2)}) collective-permute-start(f32[168,128]{1,0:T(8,128)S(1)} %pad_maximum_fusion.3), channel_id=1, source_target_pairs={{0,2},{2,0},{4,6},{6,4},{8,10},{10,8},{12,14},{14,12},{16,18},{18,... | collective-permute-start | bytes 258056 | tf_op jit(solution)/shard_map/ppermute | solution.py:17
  27.2 1.9 %collective-permute-start.10 = (f32[168,128]{1,0:T(8,128)S(1)}, f32[168,128]{1,0:T(8,128)S(1)}, u32[]{:S(2)}, u32[]{:S(2)}) collective-permute-start(f32[168,128]{1,0:T(8,128)S(1)} %pad_maximum_fusion.3), channel_id=1, source_target_pairs={{0,6},{2,4},{4,2},{6,0},{8,14},{10,12},{12,10},{14,8},{16,22},{18,... | collective-permute-start | bytes 258056 | tf_op jit(solution)/shard_map/ppermute | solution.py:17
  29.2 1.9 %collective-permute-done.8 = f32[168,128]{1,0:T(8,128)S(1)} collective-permute-done((f32[168,128]{1,0:T(8,128)S(1)}, f32[168,128]{1,0:T(8,128)S(1)}, u32[]{:S(2)}, u32[]{:S(2)}) %collective-permute-start.8) | collective-permute-done | bytes 86048 | tf_op jit(solution)/shard_map/ppermute | solution.py:17
  31.0 2.5 %collective-permute-done.9 = f32[168,128]{1,0:T(8,128)S(1)} collective-permute-done((f32[168,128]{1,0:T(8,128)S(1)}, f32[168,128]{1,0:T(8,128)S(1)}, u32[]{:S(2)}, u32[]{:S(2)}) %collective-permute-start.9) | collective-permute-done | bytes 86048 | tf_op jit(solution)/shard_map/ppermute | solution.py:17
  33.7 1.6 %collective-permute-done.11.refs_3_ = f32[648,128]{1,0:T(8,128)S(1)} collective-permute-done((f32[648,128]{1,0:T(8,128)S(1)}, f32[648,128]{1,0:T(8,128)S(1)}, u32[]{:S(2)}, u32[]{:S(2)}) %collective-permute-start.11) | collective-permute-done | bytes 331808 | tf_op jit(solution)/shard_map/ppermute | solution.py:17
  35.3 0.7 %collective-permute-start.12 = (f32[8,128]{1,0:T(8,128)S(1)}, f32[8,128]{1,0:T(8,128)S(1)}, u32[]{:S(2)}, u32[]{:S(2)}) collective-permute-start(f32[8,128]{1,0:T(8,128)S(1)} %slice_add_fusion.5), channel_id=1, source_target_pairs={{0,8},{2,10},{4,12},{6,14},{8,0},{10,2},{12,4},{14,6},{16,24},{18,... | collective-permute-start | bytes 12296 | tf_op jit(solution)/shard_map/ppermute | solution.py:17
  36.0 14.6 %factor.1 = (f32[512,512]{1,0:T(8,128)S(1)}, f32[512,512]{1,0:T(8,128)S(1)}) custom-call(s32[1]{0:T(128)} %bitcast.1.side_ref.refs_0_, s32[1]{0:T(128)} %bitcast.9.refs_1_, f32[648,128]{1,0:T(8,128)S(1)} %get-tuple-element.26.refs_2_, f32[648,128]{1,0:T(8,128)S(1)} %collective-permute-done.11.refs_3_), custom_call_target="tpu_custom_call" | custom-call | flops 2147483648 | bytes 2097152 | tf_op jit(solution)/shard_map/factor/pallas_call | solution.py:326
  50.6 2.6 %collective-permute-start.13 = (f32[8,128]{1,0:T(8,128)S(1)}, f32[8,128]{1,0:T(8,128)S(1)}, u32[]{:S(2)}, u32[]{:S(2)}) collective-permute-start(f32[8,128]{1,0:T(8,128)S(1)} %add.76), channel_id=1, source_target_pairs={{0,16},{2,18},{4,20},{6,22},{8,24},{10,26},{12,28},{14,30},{16,0},... | collective-permute-start | bytes 12296 | tf_op jit(solution)/shard_map/ppermute | solution.py:17
  53.2 2.1 %modes.1 = bf16[768,512]{1,0:T(8,128)(2,1)} custom-call(f32[512,512]{1,0:T(8,128)S(1)} %get-tuple-element.17.inverse_ref.refs_0_, bf16[768,512]{1,0:T(8,128)(2,1)S(1)} %bitcast.23), custom_call_target="tpu_custom_call" | custom-call | flops 805306368 | bytes 1048576 | tf_op jit(solution)/shard_map/modes/pallas_call | solution.py:353
  55.3 2.8 %finish.1 = (f32[1,768]{1,0:T(1,128)}, f32[513,513]{1,0:T(8,128)}) custom-call(f32[512,512]{1,0:T(8,128)S(1)} %get-tuple-element.17.inverse_ref.refs_0_, f32[512,512]{1,0:T(8,128)S(1)} %get-tuple-element.18.refs_1_, f32[8,128]{1,0:T(8,128)S(1)} %add.77.refs_2_, f32[6,128]{1,0:T(8,128)S(1)} %get-tuple-element.20.refs_3_, bf16[768,512]{1,0:T(8,128)(2,1)S(1)} %bitcast.24), custom_call_target="tpu_custom_call" | custom-call | flops 16777216 | bytes 2097152 | tf_op jit(solution)/shard_map/finish/pallas_call | solution.py:408
  (38 shorter events, 1.4 us)
Async XLA Ops:
  0.6 3.7 %copy-start = (bf16[3,1,2,128,512]{4,3,2,1,0:T(8,128)(2,1)S(1)}, bf16[3,1,2,128,512]{4,3,2,1,0:T(8,128)(2,1)}, u32[]{:S(2)}) copy-start(bf16[3,1,2,128,512]{4,3,2,1,0:T(8,128)(2,1)} %param.4) | copy-start | bytes 2359300
  0.6 1.2 %copy-start.1 = (bf16[3,8,16,1024]{3,2,1,0:T(8,128)(2,1)S(1)}, bf16[3,8,16,1024]{3,2,1,0:T(8,128)(2,1)}, u32[]{:S(2)}) copy-start(bf16[3,8,16,1024]{3,2,1,0:T(8,128)(2,1)} %param.3) | copy-start | bytes 2359300
  1.9 0.7 %copy-start.2 = (bf16[3,17]{1,0:T(4,128)(2,1)S(1)}, bf16[3,17]{1,0:T(4,128)(2,1)}, u32[]{:S(2)}) copy-start(bf16[3,17]{1,0:T(4,128)(2,1)} %refs_0_.1) | copy-start | bytes 310
  3.8 1.6 %collective-permute-start = (f32[24,128]{1,0:T(8,128)S(1)}, f32[24,128]{1,0:T(8,128)S(1)}, u32[]{:S(2)}, u32[]{:S(2)}) collective-permute-start(f32[24,128]{1,0:T(8,128)S(1)} %slice_select_fusion), channel_id=1, source_target_pairs={{0,1},{1,0},{2,3},{3,2},{4,5},{5,4},{6,7},{7,6},{8,9},{9,8},{10,11... | collective-permute-start | bytes 36872 | tf_op jit(solution)/shard_map/ppermute | solution.py:17
  4.7 1.7 %collective-permute-start.1 = (f32[640,128]{1,0:T(8,128)S(1)}, f32[640,128]{1,0:T(8,128)S(1)}, u32[]{:S(2)}, u32[]{:S(2)}) collective-permute-start(f32[640,128]{1,0:T(8,128)S(1)} %gram.3), channel_id=1, source_target_pairs={{0,1},{1,0},{2,3},{3,2},{4,5},{5,4},{6,7},{7,6},{8,9},{9,8},{10,11... | collective-permute-start | bytes 983048 | tf_op jit(solution)/shard_map/ppermute | solution.py:17
  6.5 7.0 %collective-permute-start.4 = (f32[168,128]{1,0:T(8,128)S(1)}, f32[168,128]{1,0:T(8,128)S(1)}, u32[]{:S(2)}, u32[]{:S(2)}) collective-permute-start(f32[168,128]{1,0:T(8,128)S(1)} %pad_maximum_fusion.1), channel_id=1, source_target_pairs={{0,6},{2,4},{4,2},{6,0},{8,14},{10,12},{12,10},{14,8},{16,22},{18,... | collective-permute-start | bytes 258056 | tf_op jit(solution)/shard_map/ppermute | solution.py:17
  10.1 5.2 %collective-permute-start.2 = (f32[168,128]{1,0:T(8,128)S(1)}, f32[168,128]{1,0:T(8,128)S(1)}, u32[]{:S(2)}, u32[]{:S(2)}) collective-permute-start(f32[168,128]{1,0:T(8,128)S(1)} %pad_maximum_fusion), channel_id=1, source_target_pairs={{0,2},{2,0},{4,6},{6,4},{8,10},{10,8},{12,14},{14,12},{16,18},{18,... | collective-permute-start | bytes 258056 | tf_op jit(solution)/shard_map/ppermute | solution.py:17
  10.7 4.4 %collective-permute-start.3 = (f32[160,128]{1,0:T(8,128)S(1)}, f32[160,128]{1,0:T(8,128)S(1)}, u32[]{:S(2)}, u32[]{:S(2)}) collective-permute-start(f32[160,128]{1,0:T(8,128)S(1)} %get-tuple-element.32), channel_id=1, source_target_pairs={{0,4},{2,6},{4,0},{6,2},{8,12},{10,14},{12,8},{14,10},{16,20},{18,... | collective-permute-start | bytes 245768 | tf_op jit(solution)/shard_map/ppermute | solution.py:17
  15.3 6.9 %collective-permute-start.6 = (f32[168,128]{1,0:T(8,128)S(1)}, f32[168,128]{1,0:T(8,128)S(1)}, u32[]{:S(2)}, u32[]{:S(2)}) collective-permute-start(f32[168,128]{1,0:T(8,128)S(1)} %pad_maximum_fusion.2), channel_id=1, source_target_pairs={{0,24},{2,26},{4,28},{6,30},{8,16},{10,18},{12,20},{14,22},{16,8},... | collective-permute-start | bytes 258056 | tf_op jit(solution)/shard_map/ppermute | solution.py:17
  19.0 6.3 %collective-permute-start.5 = (f32[168,128]{1,0:T(8,128)S(1)}, f32[168,128]{1,0:T(8,128)S(1)}, u32[]{:S(2)}, u32[]{:S(2)}) collective-permute-start(f32[168,128]{1,0:T(8,128)S(1)} %pad_maximum_fusion.2), channel_id=1, source_target_pairs={{0,8},{2,10},{4,12},{6,14},{8,0},{10,2},{12,4},{14,6},{16,24},{18,... | collective-permute-start | bytes 258056 | tf_op jit(solution)/shard_map/ppermute | solution.py:17
  19.0 6.5 %collective-permute-start.7 = (f32[160,128]{1,0:T(8,128)S(1)}, f32[160,128]{1,0:T(8,128)S(1)}, u32[]{:S(2)}, u32[]{:S(2)}) collective-permute-start(f32[160,128]{1,0:T(8,128)S(1)} %slice_add_fusion.2), channel_id=1, source_target_pairs={{0,16},{2,18},{4,20},{6,22},{8,24},{10,26},{12,28},{14,30},{16,0},... | collective-permute-start | bytes 245768 | tf_op jit(solution)/shard_map/ppermute | solution.py:17
  25.6 5.4 %collective-permute-start.8 = (f32[168,128]{1,0:T(8,128)S(1)}, f32[168,128]{1,0:T(8,128)S(1)}, u32[]{:S(2)}, u32[]{:S(2)}) collective-permute-start(f32[168,128]{1,0:T(8,128)S(1)} %pad_maximum_fusion.3), channel_id=1, source_target_pairs={{0,2},{2,0},{4,6},{6,4},{8,10},{10,8},{12,14},{14,12},{16,18},{18,... | collective-permute-start | bytes 258056 | tf_op jit(solution)/shard_map/ppermute | solution.py:17
  27.2 6.4 %collective-permute-start.10 = (f32[168,128]{1,0:T(8,128)S(1)}, f32[168,128]{1,0:T(8,128)S(1)}, u32[]{:S(2)}, u32[]{:S(2)}) collective-permute-start(f32[168,128]{1,0:T(8,128)S(1)} %pad_maximum_fusion.3), channel_id=1, source_target_pairs={{0,6},{2,4},{4,2},{6,0},{8,14},{10,12},{12,10},{14,8},{16,22},{18,... | collective-permute-start | bytes 258056 | tf_op jit(solution)/shard_map/ppermute | solution.py:17
  29.1 4.5 %collective-permute-start.9 = (f32[168,128]{1,0:T(8,128)S(1)}, f32[168,128]{1,0:T(8,128)S(1)}, u32[]{:S(2)}, u32[]{:S(2)}) collective-permute-start(f32[168,128]{1,0:T(8,128)S(1)} %pad_maximum_fusion.3), channel_id=1, source_target_pairs={{0,4},{2,6},{4,0},{6,2},{8,12},{10,14},{12,8},{14,10},{16,20},{18,... | collective-permute-start | bytes 258056 | tf_op jit(solution)/shard_map/ppermute | solution.py:17
  33.6 1.7 %collective-permute-start.11 = (f32[648,128]{1,0:T(8,128)S(1)}, f32[648,128]{1,0:T(8,128)S(1)}, u32[]{:S(2)}, u32[]{:S(2)}) collective-permute-start(f32[648,128]{1,0:T(8,128)S(1)} %get-tuple-element.26.refs_2_), channel_id=1, source_target_pairs={{0,1},{1,0},{2,3},{3,2},{4,5},{5,4},{6,7},{7,6},{8,9},{9,8},{10,11... | collective-permute-start | bytes 995336 | tf_op jit(solution)/shard_map/ppermute | solution.py:17
  35.3 15.3 %collective-permute-start.12 = (f32[8,128]{1,0:T(8,128)S(1)}, f32[8,128]{1,0:T(8,128)S(1)}, u32[]{:S(2)}, u32[]{:S(2)}) collective-permute-start(f32[8,128]{1,0:T(8,128)S(1)} %slice_add_fusion.5), channel_id=1, source_target_pairs={{0,8},{2,10},{4,12},{6,14},{8,0},{10,2},{12,4},{14,6},{16,24},{18,... | collective-permute-start | bytes 12296 | tf_op jit(solution)/shard_map/ppermute | solution.py:17
  50.6 4.6 %collective-permute-start.13 = (f32[8,128]{1,0:T(8,128)S(1)}, f32[8,128]{1,0:T(8,128)S(1)}, u32[]{:S(2)}, u32[]{:S(2)}) collective-permute-start(f32[8,128]{1,0:T(8,128)S(1)} %add.76), channel_id=1, source_target_pairs={{0,16},{2,18},{4,20},{6,22},{8,24},{10,26},{12,28},{14,30},{16,0},... | collective-permute-start | bytes 12296 | tf_op jit(solution)/shard_map/ppermute | solution.py:17

commit v4 on v3

--- a/solution.py
+++ b/solution.py
@@ -37,32 +37,45 @@
     )
 
 
-def upper_blocks(chunks):
-    return [(p, c) for p in range(chunks) for c in range(p, chunks)]
+def packed_blocks(chunks):
+    whole = chunks - chunks // 4
+    blocks = [(p, c) for p in range(chunks) for c in range(p, chunks) if p < c or p < whole]
+    guests = {i: (whole + i // 3, i % 3) for i in range(3 * (chunks // 4))}
+    return blocks, guests
 
 
 def gram_kernel(side_ref, rows_ref, out_ref):
-    blocks = upper_blocks(rows_ref.shape[1] // TILE)
-    half = len(blocks) // 2
+    blocks, guests = packed_blocks(rows_ref.shape[1] // TILE)
+    half, edge = out_ref.shape[0], TILE // 2
+    lane = lax.broadcasted_iota(jnp.int32, (edge, TILE), 1)
     for side in range(2):
 
         @pl.when(side_ref[0] == side)
         def _():
-            mine = blocks[half * side : half * (side + 1)]
-            for p in sorted({p for p, _ in mine}):
-                cols = [c for q, c in mine if q == p]
-                part = contract_rows(
-                    rows_ref[:, TILE * p : TILE * (p + 1)],
-                    rows_ref[:, TILE * cols[0] : TILE * (cols[-1] + 1)],
+            tops = range(half * side, half * (side + 1), edge)
+            panels = {}
+            for p in sorted({blocks[top // TILE][0] for top in tops}):
+                last = max(blocks[top // TILE][1] for top in tops if blocks[top // TILE][0] == p)
+                panels[p] = contract_rows(
+                    rows_ref[:, TILE * p : TILE * (p + 1)], rows_ref[:, TILE * p : TILE * (last + 1)]
                 )
-                for c in cols:
-                    at = TILE * mine.index((p, c))
-                    out_ref[at : at + TILE, :] = part[:, TILE * (c - cols[0]) : TILE * (c - cols[0] + 1)]
+            for top in tops:
+                p, c = blocks[top // TILE]
+                low = top % TILE
+                value = panels[p][low : low + edge, TILE * (c - p) : TILE * (c - p + 1)]
+                if p == c and low and p in guests:
+                    guest, quarter = guests[p]
+                    if guest not in panels:
+                        own = rows_ref[:, TILE * guest : TILE * (guest + 1)]
+                        panels[guest] = contract_rows(own, own)
+                    part = panels[guest][edge:, :TILE] if quarter == 2 else panels[guest][:edge, :TILE]
+                    value = jnp.where(lane < edge, pltpu.roll(part, edge, 1) if quarter else part, value)
+                out_ref[top - half * side : top - half * side + edge, :] = value
 
 
 def half_gram(side, rows):
     count, modes = rows.shape
-    height = TILE * len(upper_blocks(modes // TILE)) // 2
+    height = TILE * len(packed_blocks(modes // TILE)[0]) // 2
     return pl.pallas_call(
         gram_kernel,
         out_shape=jax.ShapeDtypeStruct((height, TILE), F32),
@@ -93,18 +106,24 @@
     return quotient, index - size * quotient
 
 
-def filter_kernel(taps_ref, cells_ref, out_ref, band, *, comps, cells_x, cells_y):
+def filter_kernel(
+    taps_hbm, cells_hbm, out_ref, taps_ref, band, cells, arrived, *, comps, cells_x, cells_y
+):
+    taps_copy = pltpu.make_async_copy(taps_hbm, taps_ref, arrived.at[0])
+    cells_copy = pltpu.make_async_copy(cells_hbm, cells, arrived.at[1])
+    taps_copy.start()
+    cells_copy.start()
     depth, points = band.shape
     height = out_ref.shape[0]
     z = lax.broadcasted_iota(jnp.int32, (TILE, points), 0)
     p = lax.broadcasted_iota(jnp.int32, (TILE, points), 1)
     lag = z - STRIDE * p + STRIDE
+    taps_copy.wait()
     pattern = weights(taps_ref, 2, jnp.where(lag < 0, lag + depth, lag))
     for block in range(depth // TILE):
         turned = pltpu.roll(pattern, TILE // STRIDE * block, 1) if block else pattern
         band[TILE * block : TILE * (block + 1), :] = turned.astype(BF16)
-    along_z = jnp.dot(cells_ref[...], band[...], preferred_element_type=F32)
-    count = cells_ref.shape[0]
+    count = cells.shape[0]
     per_y = cells_y // STRIDE
     out = lax.broadcasted_iota(jnp.int32, (height, count), 0)
     cell = lax.broadcasted_iota(jnp.int32, (height, count), 1)
@@ -117,6 +136,8 @@
     weight = weights(taps_ref, 0, x - STRIDE * (r - 1) + STRIDE)
     weight = weight * weights(taps_ref, 1, y - STRIDE * q + STRIDE)
     weight = jnp.where(cell_comp == comp, weight, 0.0)
+    cells_copy.wait()
+    along_z = jnp.dot(cells[...], band[...], preferred_element_type=F32)
     out_ref[...] = jnp.dot(weight, along_z, precision=HIGHEST, preferred_element_type=F32)
 
 
@@ -129,13 +150,19 @@
     return pl.pallas_call(
         lambda *refs: filter_kernel(*refs, comps=comps, cells_x=cells_x, cells_y=cells_y),
         out_shape=jax.ShapeDtypeStruct((height, points), F32),
-        scratch_shapes=[pltpu.VMEM((cells_z, points), BF16)],
+        in_specs=[pl.BlockSpec(memory_space=pltpu.HBM)] * 2,
+        scratch_shapes=[
+            pltpu.VMEM(taps.shape, BF16),
+            pltpu.VMEM((cells_z, points), BF16),
+            pltpu.VMEM(cells.shape, BF16),
+            pltpu.SemaphoreType.DMA((2,)),
+        ],
         cost_estimate=pl.CostEstimate(
             flops=4 * cells.size * points, bytes_accessed=2 * cells.size, transcendentals=0
         ),
         compiler_params=pltpu.CompilerParams(vmem_limit_bytes=4 << 20),
         name="filter",
-    )(taps, cells)
+    )(*(pltpu.with_memory_space_constraint(array, pltpu.HBM) for array in (taps, cells)))
 
 
 def padded_rows(rows):
@@ -311,8 +338,21 @@
         for step in range(4):
             at = pl.multiple_of(half * side + piece * (member_ref[0] ^ step), 8)
             blocks[pl.ds(at, piece), :] = part_ref[piece * step : piece * (step + 1), :] * (1.0 / total)
-    for at, (p, c) in enumerate(upper_blocks(chunks)):
+    places, guests = packed_blocks(chunks)
+    for at, (p, c) in enumerate(places):
         work[TILE * p : TILE * (p + 1), TILE * c : TILE * (c + 1)] = blocks[TILE * at : TILE * (at + 1), :]
+    edge = TILE // 2
+    lane = lax.broadcasted_iota(jnp.int32, (edge, TILE), 1)
+    corners = {}
+    for p, guest in guests.items():
+        at = TILE * places.index((p, p)) + edge
+        corners[guest] = blocks[at : at + edge, :]
+    for guest in sorted({guest for guest, _ in corners}):
+        top, cut = TILE * guest, slice(TILE * guest, TILE * (guest + 1))
+        work[top : top + edge, cut] = jnp.where(
+            lane < edge, corners[guest, 0], pltpu.roll(corners[guest, 1], edge, 1)
+        )
+        work[top + edge : top + TILE, cut] = jnp.where(lane < edge, 0.0, pltpu.roll(corners[guest, 2], edge, 1))
     scales = factor_blocks(work, scaled, factor_ref)
     for g, scale in enumerate(scales):
         where = slice(8 * g, 8 * g + 8)
@@ -321,7 +361,7 @@
 
 
 def factored(side, member, mine, other, modes, total):
-    height = TILE * len(upper_blocks(modes // TILE))
+    height = TILE * len(packed_blocks(modes // TILE)[0])
     smem, vmem = (pl.BlockSpec(memory_space=space) for space in (pltpu.SMEM, pltpu.VMEM))
     return pl.pallas_call(
         lambda *refs: factor_kernel(*refs, total=total),

time: 58.3 us -> 56.5 us (0.969)
  local copies, waits for them, and re-layouts: 1.93 us -> 0.05 us
  Pallas kernels: 21.8 us -> 22.8 us
    unnamed x9 -> x5, local copies, waits for them, and re-layouts: 1.9 us -> 0.02 us
    pallas_call x1, Pallas kernels: 1.25 us -> 2.1 us  [local_filter(): pl.pallas_call(lambda *refs: filter_kernel(*refs, comps=comps, cells_x=ce...]
  transfers between devices with their start and end apart: 14 -> 14, of which waited for: 9 -> 9; matrix products, arithmetic and copies ran while one was open for 0% -> 0% of each run, Pallas kernels for 31% -> 32%
where the time goes in v4:
time: 56.5 us; the launch traced here: 56.4 us
  Pallas kernels  22.8 us (40%)
  waiting for transfers between devices  16.5 us (29%)
  starting transfers between devices  16 us (28%)
  between operations  0.83 us (1%)
    ppermute x14, waiting for transfers between devices, swap(): lax.ppermute(block, axis, [(i, i ^ step) for i in range(lax.axis_size(axi...  16.5 us
    ppermute x14, starting transfers between devices, swap(): lax.ppermute(block, axis, [(i, i ^ step) for i in range(lax.axis_size(axi...  16 us
    pallas_call x1, Pallas kernels, factored(): pl.pallas_call(lambda *refs: factor_kernel(*refs, total=total), out_shape...  14.5 us
    pallas_call x1, Pallas kernels, finish(): pl.pallas_call(lambda *refs: finish_kernel(*refs, total=total), out_shape...  2.82 us
    pallas_call x1, Pallas kernels, local_filter(): pl.pallas_call(lambda *refs: filter_kernel(*refs, comps=comps, cells_x=ce...  2.1 us
    pallas_call x1, Pallas kernels, solved_modes(): pl.pallas_call(modes_kernel, out_shape=jax.ShapeDtypeStruct((count, modes...  2.07 us
  transfers between devices with their start and end apart: 14, of which 9 were waited for; matrix products, arithmetic and copies ran while one was open for 0% of the time, Pallas kernels for 32%

profile of v4, /device:TPU:0, one launch (start us, length us, event | category | flops | bytes accessed | tf_op | source)
XLA Modules:
  0.0 56.4 jit_solution(17657504278999750335)
XLA Ops:
  0.6 2.1 %filter.1 = f32[72,128]{1,0:T(8,128)S(1)} custom-call(bf16[3,17]{1,0:T(4,128)(2,1)} %refs_0_.1, bf16[384,1024]{1,0:T(8,128)(2,1)} %bitcast.27), custom_call_target="tpu_custom_call" | custom-call | flops 201326592 | bytes 786432 | tf_op jit(solution)/shard_map/filter/pallas_call | solution.py:150
  2.8 0.6 collective-permute-start
  3.3 0.5 gram.3
  3.9 0.6 %gram.2 = f32[576,128]{1,0:T(8,128)S(1)} custom-call(s32[1]{0:T(128)} %bitcast.1.side_ref.refs_0_, bf16[768,512]{1,0:T(8,128)(2,1)S(1)} %bitcast.21), custom_call_target="tpu_custom_call" | custom-call | flops 113246208 | bytes 294912 | tf_op jit(solution)/shard_map/gram/pallas_call | solution.py:79
  4.5 0.9 %collective-permute-done.1 = f32[576,128]{1,0:T(8,128)S(1)} collective-permute-done((f32[576,128]{1,0:T(8,128)S(1)}, f32[576,128]{1,0:T(8,128)S(1)}, u32[]{:S(2)}, u32[]{:S(2)}) %collective-permute-start.1) | collective-permute-done | bytes 294944 | tf_op jit(solution)/shard_map/ppermute | solution.py:17
  5.5 3.6 %collective-permute-start.4 = (f32[152,128]{1,0:T(8,128)S(1)}, f32[152,128]{1,0:T(8,128)S(1)}, u32[]{:S(2)}, u32[]{:S(2)}) collective-permute-start(f32[152,128]{1,0:T(8,128)S(1)} %pad_maximum_fusion.1), channel_id=1, source_target_pairs={{0,6},{2,4},{4,2},{6,0},{8,14},{10,12},{12,10},{14,8},{16,22},{18,... | collective-permute-start | bytes 233480 | tf_op jit(solution)/shard_map/ppermute | solution.py:17
  9.1 0.5 collective-permute-start.2
  9.8 2.5 %collective-permute-done.4 = f32[152,128]{1,0:T(8,128)S(1)} collective-permute-done((f32[152,128]{1,0:T(8,128)S(1)}, f32[152,128]{1,0:T(8,128)S(1)}, u32[]{:S(2)}, u32[]{:S(2)}) %collective-permute-start.4) | collective-permute-done | bytes 77856 | tf_op jit(solution)/shard_map/ppermute | solution.py:17
  12.3 1.7 %collective-permute-done.3 = f32[144,128]{1,0:T(8,128)S(1)} collective-permute-done((f32[144,128]{1,0:T(8,128)S(1)}, f32[144,128]{1,0:T(8,128)S(1)}, u32[]{:S(2)}, u32[]{:S(2)}) %collective-permute-start.3) | collective-permute-done | bytes 73760 | tf_op jit(solution)/shard_map/ppermute | solution.py:17
  14.0 3.7 %collective-permute-start.6 = (f32[152,128]{1,0:T(8,128)S(1)}, f32[152,128]{1,0:T(8,128)S(1)}, u32[]{:S(2)}, u32[]{:S(2)}) collective-permute-start(f32[152,128]{1,0:T(8,128)S(1)} %pad_maximum_fusion.2), channel_id=1, source_target_pairs={{0,24},{2,26},{4,28},{6,30},{8,16},{10,18},{12,20},{14,22},{16,8},... | collective-permute-start | bytes 233480 | tf_op jit(solution)/shard_map/ppermute | solution.py:17
  17.7 0.8 %collective-permute-start.7 = (f32[144,128]{1,0:T(8,128)S(1)}, f32[144,128]{1,0:T(8,128)S(1)}, u32[]{:S(2)}, u32[]{:S(2)}) collective-permute-start(f32[144,128]{1,0:T(8,128)S(1)} %slice_add_fusion.2), channel_id=1, source_target_pairs={{0,16},{2,18},{4,20},{6,22},{8,24},{10,26},{12,28},{14,30},{16,0},... | collective-permute-start | bytes 221192 | tf_op jit(solution)/shard_map/ppermute | solution.py:17
  18.5 2.3 %collective-permute-done.6 = f32[152,128]{1,0:T(8,128)S(1)} collective-permute-done((f32[152,128]{1,0:T(8,128)S(1)}, f32[152,128]{1,0:T(8,128)S(1)}, u32[]{:S(2)}, u32[]{:S(2)}) %collective-permute-start.6) | collective-permute-done | bytes 77856 | tf_op jit(solution)/shard_map/ppermute | solution.py:17
  20.7 2.9 %collective-permute-done.5 = f32[152,128]{1,0:T(8,128)S(1)} collective-permute-done((f32[152,128]{1,0:T(8,128)S(1)}, f32[152,128]{1,0:T(8,128)S(1)}, u32[]{:S(2)}, u32[]{:S(2)}) %collective-permute-start.5) | collective-permute-done | bytes 77856 | tf_op jit(solution)/shard_map/ppermute | solution.py:17
  23.9 1.5 %collective-permute-start.8 = (f32[152,128]{1,0:T(8,128)S(1)}, f32[152,128]{1,0:T(8,128)S(1)}, u32[]{:S(2)}, u32[]{:S(2)}) collective-permute-start(f32[152,128]{1,0:T(8,128)S(1)} %pad_maximum_fusion.3), channel_id=1, source_target_pairs={{0,2},{2,0},{4,6},{6,4},{8,10},{10,8},{12,14},{14,12},{16,18},{18,... | collective-permute-start | bytes 233480 | tf_op jit(solution)/shard_map/ppermute | solution.py:17
  25.4 1.5 %collective-permute-start.10 = (f32[152,128]{1,0:T(8,128)S(1)}, f32[152,128]{1,0:T(8,128)S(1)}, u32[]{:S(2)}, u32[]{:S(2)}) collective-permute-start(f32[152,128]{1,0:T(8,128)S(1)} %pad_maximum_fusion.3), channel_id=1, source_target_pairs={{0,6},{2,4},{4,2},{6,0},{8,14},{10,12},{12,10},{14,8},{16,22},{18,... | collective-permute-start | bytes 233480 | tf_op jit(solution)/shard_map/ppermute | solution.py:17
  26.9 0.6 %collective-permute-start.9 = (f32[152,128]{1,0:T(8,128)S(1)}, f32[152,128]{1,0:T(8,128)S(1)}, u32[]{:S(2)}, u32[]{:S(2)}) collective-permute-start(f32[152,128]{1,0:T(8,128)S(1)} %pad_maximum_fusion.3), channel_id=1, source_target_pairs={{0,4},{2,6},{4,0},{6,2},{8,12},{10,14},{12,8},{14,10},{16,20},{18,... | collective-permute-start | bytes 233480 | tf_op jit(solution)/shard_map/ppermute | solution.py:17
  27.4 1.7 %collective-permute-done.8 = f32[152,128]{1,0:T(8,128)S(1)} collective-permute-done((f32[152,128]{1,0:T(8,128)S(1)}, f32[152,128]{1,0:T(8,128)S(1)}, u32[]{:S(2)}, u32[]{:S(2)}) %collective-permute-start.8) | collective-permute-done | bytes 77856 | tf_op jit(solution)/shard_map/ppermute | solution.py:17
  29.1 2.6 %collective-permute-done.9 = f32[152,128]{1,0:T(8,128)S(1)} collective-permute-done((f32[152,128]{1,0:T(8,128)S(1)}, f32[152,128]{1,0:T(8,128)S(1)}, u32[]{:S(2)}, u32[]{:S(2)}) %collective-permute-start.9) | collective-permute-done | bytes 77856 | tf_op jit(solution)/shard_map/ppermute | solution.py:17
  31.8 1.6 %collective-permute-done.11.refs_3_ = f32[584,128]{1,0:T(8,128)S(1)} collective-permute-done((f32[584,128]{1,0:T(8,128)S(1)}, f32[584,128]{1,0:T(8,128)S(1)}, u32[]{:S(2)}, u32[]{:S(2)}) %collective-permute-start.11) | collective-permute-done | bytes 299040 | tf_op jit(solution)/shard_map/ppermute | solution.py:17
  33.4 1.0 %collective-permute-start.12 = (f32[8,128]{1,0:T(8,128)S(1)}, f32[8,128]{1,0:T(8,128)S(1)}, u32[]{:S(2)}, u32[]{:S(2)}) collective-permute-start(f32[8,128]{1,0:T(8,128)S(1)} %slice_add_fusion.5), channel_id=1, source_target_pairs={{0,8},{2,10},{4,12},{6,14},{8,0},{10,2},{12,4},{14,6},{16,24},{18,... | collective-permute-start | bytes 12296 | tf_op jit(solution)/shard_map/ppermute | solution.py:17
  34.4 14.5 %factor.1 = (f32[512,512]{1,0:T(8,128)S(1)}, f32[512,512]{1,0:T(8,128)S(1)}) custom-call(s32[1]{0:T(128)} %bitcast.1.side_ref.refs_0_, s32[1]{0:T(128)} %bitcast.9.refs_1_, f32[584,128]{1,0:T(8,128)S(1)} %get-tuple-element.26.refs_2_, f32[584,128]{1,0:T(8,128)S(1)} %collective-permute-done.11.refs_3_), custom_call_target="tpu_custom_call" | custom-call | flops 2147483648 | bytes 2097152 | tf_op jit(solution)/shard_map/factor/pallas_call | solution.py:366
  49.0 2.1 %collective-permute-start.13 = (f32[8,128]{1,0:T(8,128)S(1)}, f32[8,128]{1,0:T(8,128)S(1)}, u32[]{:S(2)}, u32[]{:S(2)}) collective-permute-start(f32[8,128]{1,0:T(8,128)S(1)} %add.76), channel_id=1, source_target_pairs={{0,16},{2,18},{4,20},{6,22},{8,24},{10,26},{12,28},{14,30},{16,0},... | collective-permute-start | bytes 12296 | tf_op jit(solution)/shard_map/ppermute | solution.py:17
  51.0 2.1 %modes.1 = bf16[768,512]{1,0:T(8,128)(2,1)} custom-call(f32[512,512]{1,0:T(8,128)S(1)} %get-tuple-element.17.inverse_ref.refs_0_, bf16[768,512]{1,0:T(8,128)(2,1)S(1)} %bitcast.23), custom_call_target="tpu_custom_call" | custom-call | flops 805306368 | bytes 1048576 | tf_op jit(solution)/shard_map/modes/pallas_call | solution.py:393
  53.5 2.8 %finish.1 = (f32[1,768]{1,0:T(1,128)}, f32[513,513]{1,0:T(8,128)}) custom-call(f32[512,512]{1,0:T(8,128)S(1)} %get-tuple-element.17.inverse_ref.refs_0_, f32[512,512]{1,0:T(8,128)S(1)} %get-tuple-element.18.refs_1_, f32[8,128]{1,0:T(8,128)S(1)} %add.77.refs_2_, f32[6,128]{1,0:T(8,128)S(1)} %get-tuple-element.20.refs_3_, bf16[768,512]{1,0:T(8,128)(2,1)S(1)} %bitcast.24), custom_call_target="tpu_custom_call" | custom-call | flops 16777216 | bytes 2097152 | tf_op jit(solution)/shard_map/finish/pallas_call | solution.py:448
  (34 shorter events, 1.1 us)
Async XLA Ops:
  0.6 2.7 %copy-start = (bf16[3,1,2,128,512]{4,3,2,1,0:T(8,128)(2,1)S(1)}, bf16[3,1,2,128,512]{4,3,2,1,0:T(8,128)(2,1)}, u32[]{:S(2)}) copy-start(bf16[3,1,2,128,512]{4,3,2,1,0:T(8,128)(2,1)} %param.4) | copy-start | bytes 2359300
  2.8 1.7 %collective-permute-start = (f32[24,128]{1,0:T(8,128)S(1)}, f32[24,128]{1,0:T(8,128)S(1)}, u32[]{:S(2)}, u32[]{:S(2)}) collective-permute-start(f32[24,128]{1,0:T(8,128)S(1)} %slice_select_fusion), channel_id=1, source_target_pairs={{0,1},{1,0},{2,3},{3,2},{4,5},{5,4},{6,7},{7,6},{8,9},{9,8},{10,11... | collective-permute-start | bytes 36872 | tf_op jit(solution)/shard_map/ppermute | solution.py:17
  3.8 1.6 %collective-permute-start.1 = (f32[576,128]{1,0:T(8,128)S(1)}, f32[576,128]{1,0:T(8,128)S(1)}, u32[]{:S(2)}, u32[]{:S(2)}) collective-permute-start(f32[576,128]{1,0:T(8,128)S(1)} %gram.3), channel_id=1, source_target_pairs={{0,1},{1,0},{2,3},{3,2},{4,5},{5,4},{6,7},{7,6},{8,9},{9,8},{10,11... | collective-permute-start | bytes 884744 | tf_op jit(solution)/shard_map/ppermute | solution.py:17
  5.5 6.7 %collective-permute-start.4 = (f32[152,128]{1,0:T(8,128)S(1)}, f32[152,128]{1,0:T(8,128)S(1)}, u32[]{:S(2)}, u32[]{:S(2)}) collective-permute-start(f32[152,128]{1,0:T(8,128)S(1)} %pad_maximum_fusion.1), channel_id=1, source_target_pairs={{0,6},{2,4},{4,2},{6,0},{8,14},{10,12},{12,10},{14,8},{16,22},{18,... | collective-permute-start | bytes 233480 | tf_op jit(solution)/shard_map/ppermute | solution.py:17
  9.1 4.9 %collective-permute-start.2 = (f32[152,128]{1,0:T(8,128)S(1)}, f32[152,128]{1,0:T(8,128)S(1)}, u32[]{:S(2)}, u32[]{:S(2)}) collective-permute-start(f32[152,128]{1,0:T(8,128)S(1)} %pad_maximum_fusion), channel_id=1, source_target_pairs={{0,2},{2,0},{4,6},{6,4},{8,10},{10,8},{12,14},{14,12},{16,18},{18,... | collective-permute-start | bytes 233480 | tf_op jit(solution)/shard_map/ppermute | solution.py:17
  9.6 4.4 %collective-permute-start.3 = (f32[144,128]{1,0:T(8,128)S(1)}, f32[144,128]{1,0:T(8,128)S(1)}, u32[]{:S(2)}, u32[]{:S(2)}) collective-permute-start(f32[144,128]{1,0:T(8,128)S(1)} %get-tuple-element.32), channel_id=1, source_target_pairs={{0,4},{2,6},{4,0},{6,2},{8,12},{10,14},{12,8},{14,10},{16,20},{18,... | collective-permute-start | bytes 221192 | tf_op jit(solution)/shard_map/ppermute | solution.py:17
  14.0 6.7 %collective-permute-start.6 = (f32[152,128]{1,0:T(8,128)S(1)}, f32[152,128]{1,0:T(8,128)S(1)}, u32[]{:S(2)}, u32[]{:S(2)}) collective-permute-start(f32[152,128]{1,0:T(8,128)S(1)} %pad_maximum_fusion.2), channel_id=1, source_target_pairs={{0,24},{2,26},{4,28},{6,30},{8,16},{10,18},{12,20},{14,22},{16,8},... | collective-permute-start | bytes 233480 | tf_op jit(solution)/shard_map/ppermute | solution.py:17
  17.7 5.9 %collective-permute-start.5 = (f32[152,128]{1,0:T(8,128)S(1)}, f32[152,128]{1,0:T(8,128)S(1)}, u32[]{:S(2)}, u32[]{:S(2)}) collective-permute-start(f32[152,128]{1,0:T(8,128)S(1)} %pad_maximum_fusion.2), channel_id=1, source_target_pairs={{0,8},{2,10},{4,12},{6,14},{8,0},{10,2},{12,4},{14,6},{16,24},{18,... | collective-permute-start | bytes 233480 | tf_op jit(solution)/shard_map/ppermute | solution.py:17
  17.7 6.1 %collective-permute-start.7 = (f32[144,128]{1,0:T(8,128)S(1)}, f32[144,128]{1,0:T(8,128)S(1)}, u32[]{:S(2)}, u32[]{:S(2)}) collective-permute-start(f32[144,128]{1,0:T(8,128)S(1)} %slice_add_fusion.2), channel_id=1, source_target_pairs={{0,16},{2,18},{4,20},{6,22},{8,24},{10,26},{12,28},{14,30},{16,0},... | collective-permute-start | bytes 221192 | tf_op jit(solution)/shard_map/ppermute | solution.py:17
  23.9 5.3 %collective-permute-start.8 = (f32[152,128]{1,0:T(8,128)S(1)}, f32[152,128]{1,0:T(8,128)S(1)}, u32[]{:S(2)}, u32[]{:S(2)}) collective-permute-start(f32[152,128]{1,0:T(8,128)S(1)} %pad_maximum_fusion.3), channel_id=1, source_target_pairs={{0,2},{2,0},{4,6},{6,4},{8,10},{10,8},{12,14},{14,12},{16,18},{18,... | collective-permute-start | bytes 233480 | tf_op jit(solution)/shard_map/ppermute | solution.py:17
  25.4 6.4 %collective-permute-start.10 = (f32[152,128]{1,0:T(8,128)S(1)}, f32[152,128]{1,0:T(8,128)S(1)}, u32[]{:S(2)}, u32[]{:S(2)}) collective-permute-start(f32[152,128]{1,0:T(8,128)S(1)} %pad_maximum_fusion.3), channel_id=1, source_target_pairs={{0,6},{2,4},{4,2},{6,0},{8,14},{10,12},{12,10},{14,8},{16,22},{18,... | collective-permute-start | bytes 233480 | tf_op jit(solution)/shard_map/ppermute | solution.py:17
  26.9 4.9 %collective-permute-start.9 = (f32[152,128]{1,0:T(8,128)S(1)}, f32[152,128]{1,0:T(8,128)S(1)}, u32[]{:S(2)}, u32[]{:S(2)}) collective-permute-start(f32[152,128]{1,0:T(8,128)S(1)} %pad_maximum_fusion.3), channel_id=1, source_target_pairs={{0,4},{2,6},{4,0},{6,2},{8,12},{10,14},{12,8},{14,10},{16,20},{18,... | collective-permute-start | bytes 233480 | tf_op jit(solution)/shard_map/ppermute | solution.py:17
  31.8 1.7 %collective-permute-start.11 = (f32[584,128]{1,0:T(8,128)S(1)}, f32[584,128]{1,0:T(8,128)S(1)}, u32[]{:S(2)}, u32[]{:S(2)}) collective-permute-start(f32[584,128]{1,0:T(8,128)S(1)} %get-tuple-element.26.refs_2_), channel_id=1, source_target_pairs={{0,1},{1,0},{2,3},{3,2},{4,5},{5,4},{6,7},{7,6},{8,9},{9,8},{10,11... | collective-permute-start | bytes 897032 | tf_op jit(solution)/shard_map/ppermute | solution.py:17
  33.4 15.5 %collective-permute-start.12 = (f32[8,128]{1,0:T(8,128)S(1)}, f32[8,128]{1,0:T(8,128)S(1)}, u32[]{:S(2)}, u32[]{:S(2)}) collective-permute-start(f32[8,128]{1,0:T(8,128)S(1)} %slice_add_fusion.5), channel_id=1, source_target_pairs={{0,8},{2,10},{4,12},{6,14},{8,0},{10,2},{12,4},{14,6},{16,24},{18,... | collective-permute-start | bytes 12296 | tf_op jit(solution)/shard_map/ppermute | solution.py:17
  49.0 4.6 %collective-permute-start.13 = (f32[8,128]{1,0:T(8,128)S(1)}, f32[8,128]{1,0:T(8,128)S(1)}, u32[]{:S(2)}, u32[]{:S(2)}) collective-permute-start(f32[8,128]{1,0:T(8,128)S(1)} %add.76), channel_id=1, source_target_pairs={{0,16},{2,18},{4,20},{6,22},{8,24},{10,26},{12,28},{14,30},{16,0},... | collective-permute-start | bytes 12296 | tf_op jit(solution)/shard_map/ppermute | solution.py:17

commit v5 on v4

--- a/solution.py
+++ b/solution.py
@@ -5,6 +5,7 @@
 from jax.experimental.pallas import tpu as pltpu
 from jax.sharding import PartitionSpec as P
 
+
 STRIDE = 8
 TILE = 128
 PIVOTS = 32
@@ -15,6 +16,14 @@
 
 def swap(block, axis, step):
     return lax.ppermute(block, axis, [(i, i ^ step) for i in range(lax.axis_size(axis))])
+
+
+def swap_by_side(block, steps):
+    wide = lax.axis_size("gy")
+    pairs = [
+        (i * wide + j, (i ^ steps[j & 1]) * wide + j) for i in range(lax.axis_size("gx")) for j in range(wide)
+    ]
+    return lax.ppermute(block, ("gx", "gy"), pairs)
 
 
 def bit_groups(size):
@@ -106,9 +115,7 @@
     return quotient, index - size * quotient
 
 
-def filter_kernel(
-    taps_hbm, cells_hbm, out_ref, taps_ref, band, cells, arrived, *, comps, cells_x, cells_y
-):
+def filter_kernel(taps_hbm, cells_hbm, out_ref, taps_ref, band, cells, arrived, *, cells_x, cells_y):
     taps_copy = pltpu.make_async_copy(taps_hbm, taps_ref, arrived.at[0])
     cells_copy = pltpu.make_async_copy(cells_hbm, cells, arrived.at[1])
     taps_copy.start()
@@ -148,7 +155,7 @@
     height = 9 * padded_rows(comps * cells_y // STRIDE)
     cells = snapshot.reshape(-1, cells_z)
     return pl.pallas_call(
-        lambda *refs: filter_kernel(*refs, comps=comps, cells_x=cells_x, cells_y=cells_y),
+        lambda *refs: filter_kernel(*refs, cells_x=cells_x, cells_y=cells_y),
         out_shape=jax.ShapeDtypeStruct((height, points), F32),
         in_specs=[pl.BlockSpec(memory_space=pltpu.HBM)] * 2,
         scratch_shapes=[
@@ -232,15 +239,16 @@
     return jnp.concatenate([a, b, a, b, c, a])
 
 
-def factor_blocks(work, scaled, upper):
+def factor_blocks(work, scaled, upper, panels, after):
     modes = work.shape[0]
     chunks = modes // TILE
     groups = PIVOTS // 8
     lane = lax.broadcasted_iota(jnp.int32, (8, TILE), 1)
     row = lax.broadcasted_iota(jnp.int32, (8, TILE), 0)
-    scale_blocks = []
-    for p in range(chunks):
+    for p in panels:
         base = p * TILE
+        shift = panels[0] * TILE
+        scale_blocks = []
         for j in range(TILE // PIVOTS):
             first = PIVOTS * j
             top = base + first
@@ -282,16 +290,17 @@
             inside = (lane >= first) & (lane < first + PIVOTS)
             for g in range(groups):
                 where = slice(top + 8 * g, top + 8 * g + 8)
+                line = slice(top - shift + 8 * g, top - shift + 8 * g + 8)
                 for c in range(chunks):
                     cut = slice(TILE * c, TILE * (c + 1))
                     if c < p:
-                        upper[where, cut] = jnp.zeros((8, TILE), F32)
+                        upper[line, cut] = jnp.zeros((8, TILE), F32)
                     elif c == p:
-                        upper[where, cut] = jnp.where(
+                        upper[line, cut] = jnp.where(
                             lane >= first + 8 * g + row, rows[g][c] * scale[g], 0.0
                         )
                     else:
-                        upper[where, cut] = rows[g][c] * scale[g]
+                        upper[line, cut] = rows[g][c] * scale[g]
                     if c >= p:
                         scaled[first + 8 * g : first + 8 * g + 8, cut] = rows[g][c] * inverse[g]
                     work[where, cut] = jnp.where(inside, unit[g], rows[g][c]) if c == p else rows[g][c]
@@ -325,18 +334,23 @@
             work[below, own] = -inverse_part[:, base:]
             gram_part = contract_rows(part, right[:, TILE * i :])
             work[below, TILE * i :] = work[below, TILE * i :] - gram_part
-    return scale_blocks
-
-
-def factor_kernel(side_ref, member_ref, mine_ref, other_ref, inverse_ref, factor_ref, scaled, blocks, *, total):
-    work = inverse_ref
+        for g, scale in enumerate(scale_blocks):
+            where = slice(base + 8 * g, base + 8 * g + 8)
+            for c in range(p + 1):
+                cut = slice(TILE * c, TILE * (c + 1))
+                work[where, cut] = work[where, cut] * scale
+        after(p)
+
+
+def early_kernel(side_ref, member_ref, beside_ref, mine_ref, other_ref, work, upper, scaled, blocks, *, total):
     modes = work.shape[0]
     chunks = modes // TILE
     half = blocks.shape[0] // 2
     piece = half // 4
-    for part_ref, side in ((mine_ref, side_ref[0]), (other_ref, 1 - side_ref[0])):
+    sides = ((mine_ref, side_ref[0], member_ref[0]), (other_ref, 1 - side_ref[0], beside_ref[0]))
+    for part_ref, side, member in sides:
         for step in range(4):
-            at = pl.multiple_of(half * side + piece * (member_ref[0] ^ step), 8)
+            at = pl.multiple_of(half * side + piece * (member ^ step), 8)
             blocks[pl.ds(at, piece), :] = part_ref[piece * step : piece * (step + 1), :] * (1.0 / total)
     places, guests = packed_blocks(chunks)
     for at, (p, c) in enumerate(places):
@@ -353,110 +367,139 @@
             lane < edge, corners[guest, 0], pltpu.roll(corners[guest, 1], edge, 1)
         )
         work[top + edge : top + TILE, cut] = jnp.where(lane < edge, 0.0, pltpu.roll(corners[guest, 2], edge, 1))
-    scales = factor_blocks(work, scaled, factor_ref)
-    for g, scale in enumerate(scales):
-        where = slice(8 * g, 8 * g + 8)
-        for c in range(8 * g // TILE + 1):
-            work[where, TILE * c : TILE * (c + 1)] = work[where, TILE * c : TILE * (c + 1)] * scale
-
-
-def factored(side, member, mine, other, modes, total):
+    factor_blocks(work, scaled, upper, range(chunks // 2), lambda p: None)
+
+
+def early_panels(side, member, beside, mine, other, modes, total):
     height = TILE * len(packed_blocks(modes // TILE)[0])
     smem, vmem = (pl.BlockSpec(memory_space=space) for space in (pltpu.SMEM, pltpu.VMEM))
     return pl.pallas_call(
-        lambda *refs: factor_kernel(*refs, total=total),
-        out_shape=(jax.ShapeDtypeStruct((modes, modes), F32),) * 2,
-        in_specs=[smem, smem, vmem, vmem],
+        lambda *refs: early_kernel(*refs, total=total),
+        out_shape=(
+            jax.ShapeDtypeStruct((modes, modes), F32),
+            jax.ShapeDtypeStruct((modes // TILE // 2 * TILE, modes), F32),
+        ),
+        in_specs=[smem, smem, smem, vmem, vmem],
         scratch_shapes=[pltpu.VMEM((TILE, modes), F32), pltpu.VMEM((height, TILE), F32)],
         cost_estimate=pl.CostEstimate(
             flops=16 * modes**3, bytes_accessed=8 * modes * modes, transcendentals=modes
         ),
-        compiler_params=pltpu.CompilerParams(vmem_limit_bytes=10 << 20),
-        name="factor",
-    )(side.reshape(1), member.reshape(1), mine, other)
-
-
-def modes_kernel(inverse_ref, rows_ref, modes_ref):
-    for p in range(inverse_ref.shape[0] // TILE):
+        compiler_params=pltpu.CompilerParams(vmem_limit_bytes=8 << 20),
+        name="early",
+    )(side.reshape(1), member.reshape(1), beside.reshape(1), mine, other)
+
+
+def late_kernel(
+    early_ref, early_upper_ref, rows_ref, inverse_ref, modes_hbm, factor_hbm, scaled, upper, solved, sent
+):
+    modes = inverse_ref.shape[0]
+    chunks = modes // TILE
+    above = early_upper_ref.shape[0]
+    copies = [pltpu.make_async_copy(early_upper_ref, factor_hbm.at[:above, :modes], sent.at[chunks])]
+    copies[0].start()
+    inverse_ref[...] = early_ref[...]
+
+    def solve(p):
         own = slice(TILE * p, TILE * (p + 1))
         width = TILE * (p + 1)
         known = inverse_ref[own, :width]
         first = known.astype(BF16)
         second = (known - first.astype(F32)).astype(BF16)
         left = rows_ref[:, :width]
-        solved = contract_lanes(left, first) + contract_lanes(left, second)
-        modes_ref[:, own] = solved.astype(BF16)
-
-
-def solved_modes(inverse, rows):
+        solved[p] = (contract_lanes(left, first) + contract_lanes(left, second)).astype(BF16)
+        copy = pltpu.make_async_copy(solved.at[p], modes_hbm.at[:, own], sent.at[p])
+        copy.start()
+        copies.append(copy)
+
+    for p in range(chunks // 2):
+        solve(p)
+    factor_blocks(inverse_ref, scaled, upper, range(chunks // 2, chunks), solve)
+    upper[modes - above : modes - above + 1, :] = jnp.zeros((1, modes), F32)
+    copy = pltpu.make_async_copy(upper, factor_hbm.at[above:, :modes], sent.at[chunks + 1])
+    copy.start()
+    for copy in copies + [copy]:
+        copy.wait()
+
+
+def late_panels(early, early_upper, rows):
     count, modes = rows.shape
+    chunks = modes // TILE
+    vmem, hbm = (pl.BlockSpec(memory_space=space) for space in (pltpu.VMEM, pltpu.HBM))
     return pl.pallas_call(
-        modes_kernel,
-        out_shape=jax.ShapeDtypeStruct((count, modes), BF16),
+        late_kernel,
+        out_shape=(
+            jax.ShapeDtypeStruct((modes, modes), F32),
+            jax.ShapeDtypeStruct((count, modes), BF16),
+            jax.ShapeDtypeStruct((modes + 1, modes + 1), F32),
+        ),
+        out_specs=(vmem, hbm, hbm),
+        scratch_shapes=[
+            pltpu.VMEM((TILE, modes), F32),
+            pltpu.VMEM((modes + 1 - early_upper.shape[0], modes), F32),
+            pltpu.VMEM((chunks, count, TILE), BF16),
+            pltpu.SemaphoreType.DMA((chunks + 2,)),
+        ],
         cost_estimate=pl.CostEstimate(
-            flops=4 * count * modes * modes, bytes_accessed=4 * modes * modes, transcendentals=0
-        ),
-        compiler_params=pltpu.CompilerParams(vmem_limit_bytes=8 << 20),
-        name="modes",
-    )(inverse, rows)
-
-
-def finish_kernel(inverse_ref, upper_ref, sums_ref, fresh_ref, rows_ref, mode_ref, factor_ref, *, total):
+            flops=16 * modes**3, bytes_accessed=8 * modes * modes, transcendentals=modes
+        ),
+        compiler_params=pltpu.CompilerParams(vmem_limit_bytes=10 << 20),
+        name="late",
+    )(early, early_upper, rows)
+
+
+def finish_kernel(inverse_ref, sums_ref, fresh_ref, rows_ref, _, mode_ref, column_ref, *, total):
     modes = inverse_ref.shape[0]
     chunks = modes // TILE
     sums = sums_ref[...] * (1.0 / total)
     cross = [sums[c : c + 1, :] for c in range(chunks)]
     square = sums[chunks : chunks + 1, :]
-    projected = []
+    norm = jnp.zeros((1, TILE), F32)
+    back = [jnp.zeros((1, TILE), F32)] * chunks
     for p in range(chunks):
         own = slice(TILE * p, TILE * (p + 1))
-        width = TILE * (p + 1)
-        known = inverse_ref[own, :width]
-        line = jnp.concatenate(cross[: p + 1], axis=1)
-        projected.append(contract_lanes(jnp.broadcast_to(line, (8, width)), known, HIGHEST))
-        column = sum(known[:, TILE * c : TILE * (c + 1)] * cross[c] for c in range(p + 1))
-        factor_ref[own, :modes] = upper_ref[own, :]
-        factor_ref[own, modes : modes + 1] = jnp.sum(column, axis=1, keepdims=True)
-    norm = sum(jnp.sum(part * part, axis=1, keepdims=True) for part in projected)
-    last = jnp.sqrt(square[:, :1] - norm[:1, :])
-    back = []
-    for c in range(chunks):
-        own = slice(TILE * c, TILE * (c + 1))
-        part = jnp.zeros((8, TILE), F32)
-        for p in range(c, chunks):
-            part = part + jnp.dot(
-                projected[p],
-                inverse_ref[TILE * p : TILE * (p + 1), own],
-                precision=HIGHEST,
-                preferred_element_type=F32,
-            )
-        back.append(part)
+        known = [inverse_ref[own, TILE * c : TILE * (c + 1)] for c in range(p + 1)]
+        column = sum(known[c] * cross[c] for c in range(p + 1))
+        column = jnp.broadcast_to(jnp.sum(column, axis=1, keepdims=True), (TILE, TILE))
+        column_ref[own, :] = column
+        norm = norm + jnp.sum(column * column, axis=0, keepdims=True)
+        for c in range(p + 1):
+            back[c] = back[c] + jnp.sum(known[c] * column, axis=0, keepdims=True)
+    last = jnp.sqrt(square - norm)
     share = jnp.concatenate(back, axis=1)
     first = share.astype(BF16)
     second = (share - first.astype(F32)).astype(BF16)
+    both = jnp.concatenate([jnp.broadcast_to(part, (16, modes)) for part in (first, second)])
     points = fresh_ref.shape[1]
     for i in range(fresh_ref.shape[0]):
         left = rows_ref[points * i : points * (i + 1), :]
-        covered = contract_lanes(first, left) + contract_lanes(second, left)
-        mode_ref[:, points * i : points * (i + 1)] = (fresh_ref[i : i + 1, :] - covered[:1, :]) / last
-    factor_ref[modes : modes + 1, :modes] = jnp.zeros((1, modes), F32)
-    factor_ref[modes : modes + 1, modes : modes + 1] = last
-
-
-def finish(inverse, upper, sums, fresh, rows, total):
+        covered = contract_lanes(both, left)
+        covered = covered[:1, :] + covered[16:17, :]
+        mode_ref[:, points * i : points * (i + 1)] = (fresh_ref[i : i + 1, :] - covered) / last
+    column_ref[modes : modes + 1, :] = last
+
+
+def finish(inverse, sums, fresh, rows, factor, total):
     count, modes = rows.shape
+    vmem, hbm = (pl.BlockSpec(memory_space=space) for space in (pltpu.VMEM, pltpu.HBM))
     return pl.pallas_call(
         lambda *refs: finish_kernel(*refs, total=total),
+        grid=(1,),
         out_shape=(
             jax.ShapeDtypeStruct((1, count), F32),
             jax.ShapeDtypeStruct((modes + 1, modes + 1), F32),
         ),
+        in_specs=[vmem, vmem, vmem, vmem, hbm],
+        out_specs=(
+            pl.BlockSpec((1, count), lambda i: (0, 0)),
+            pl.BlockSpec((modes + 1, TILE), lambda i: (0, modes // TILE)),
+        ),
+        input_output_aliases={4: 1},
         cost_estimate=pl.CostEstimate(
-            flops=64 * modes * modes, bytes_accessed=8 * modes * modes, transcendentals=0
+            flops=64 * modes * modes, bytes_accessed=4 * modes * modes, transcendentals=0
         ),
         compiler_params=pltpu.CompilerParams(vmem_limit_bytes=8 << 20),
         name="finish",
-    )(inverse, upper, sums, fresh, rows)
+    )(inverse, sums, fresh, rows, factor)
 
 
 def local(snapshot, basis, taps):
@@ -465,9 +508,12 @@
     total = rows.shape[0] * lax.axis_size("gx") * lax.axis_size("gy")
     side = lax.axis_index("gy") & 1
     place = lax.axis_index("gx")
-    member = place & 3
+    inner, group = place & 3, (place >> 2) & 3
     slabs = lax.axis_size("gx")
-    first, *others = bit_groups(slabs)
+    near_steps, far_steps, *others = bit_groups(slabs)
+    even = side == 0
+    member, beside = jnp.where(even, inner, group), jnp.where(even, group, inner)
+    ways = (tuple(zip(near_steps, far_steps)), tuple(zip(far_steps, near_steps)))
 
     parts = local_filter(taps, snapshot)
     side, parts = lax.optimization_barrier((side, parts))
@@ -487,25 +533,36 @@
         return lax.dynamic_index_in_dim(quarters, index, 0, keepdims=False)
 
     before, own, after = parts[:height], parts[height : 2 * height], parts[2 * height :]
-    odd = (member & 1) == 1
-    riders = {1: jnp.where(odd, before, after), 3: jnp.where(odd, after, before)}
-    got = {}
-    for step in first:
-        block = quarter_of(member ^ step)
-        got[step] = swap(jnp.concatenate([block, riders[step]]) if step in riders else block, "gx", step)
-    quarter = sum([got[step][:piece] for step in first], quarter_of(member))
-    near, far = got[1][piece:], got[3][piece:]
-
+    odd = (inner & 1) == 1
+    outer = (inner == 0) | (inner == 3)
+    by_one, by_three = jnp.where(odd, before, after), jnp.where(odd, after, before)
+    over = jnp.where(inner == 0, before, after)
+    wanted = jnp.where((inner == 0) == even, group - 1, group + 1) & 3
+    next_group = (group ^ wanted) == 1
+
+    def exchanged(blocks, riders, way):
+        return [
+            swap_by_side(block if rider is None else jnp.concatenate([block, rider]), steps)
+            for block, rider, steps in zip(blocks, riders, way)
+        ]
+
+    got = exchanged(
+        [quarter_of(member ^ step) for step in (1, 2, 3)],
+        (jnp.where(even, by_one, over), None, jnp.where(even, by_three, over)),
+        ways[0],
+    )
+    quarter = sum([block[:piece] for block in got], quarter_of(member))
+    one, three = got[0][piece:], got[2][piece:]
+
+    crossed = jnp.where(outer, jnp.where(next_group, one, three), by_three)
+    riders = (jnp.where(even, three, by_one), None, jnp.where(even, three, crossed))
+    got = exchanged([quarter] * 3, riders, ways[1])
+    quarter = sum([block[:piece] for block in got], quarter)
     if slabs == 16:
-        got = {}
-        for step in others[0]:
-            block = jnp.concatenate([quarter, far]) if step != 8 else quarter
-            got[step] = swap(block, "gx", step)
-        quarter = sum([block[:piece] for block in got.values()], quarter)
-        group = place >> 2
-        wanted = jnp.where(member == 0, group - 1, group + 1) & 3
-        outer = jnp.where((group ^ wanted) == 1, got[4][piece:], got[12][piece:])
-        far = jnp.where((member == 0) | (member == 3), outer, far)
+        last_one, last_three = got[0][piece:], got[2][piece:]
+        near = jnp.where(even, one, last_one)
+        passed = jnp.where(outer, jnp.where(next_group, last_one, last_three), three)
+        far = jnp.where(even, passed, last_three)
     else:
         for steps in others:
             quarter = sum([swap(quarter, "gx", step) for step in steps], quarter)
@@ -515,29 +572,29 @@
 
     fresh, cross = local_cross(own, near, far, rows)
     block = jnp.concatenate([quarter, cross])
-    gathered = [block] + [swap(block, "gx", step) for step in first]
+    gathered = [block] + exchanged([block] * 3, (None,) * 3, ways[0])
     sums = sum([got[piece:] for got in gathered[1:]], block[piece:])
-    mine = jnp.concatenate([got[:piece] for got in gathered] + [sums])
+    mine = jnp.concatenate([got[:piece] for got in gathered])
     other = swap(mine, "gy", 1)
-    sums = mine[4 * piece :] + other[4 * piece :]
+    sums = sums + swap_by_side(sums, ways[1][0])
+    for steps in others:
+        sums = sum([swap(sums, "gx", step) for step in steps], sums)
     bit = 2
     while bit < lax.axis_size("gy"):
         sums = sums + swap(sums, "gy", bit)
         bit *= 2
-    bit = 4
-    while 2 * bit < slabs:
-        sums = sums + swap(sums, "gx", bit)
-        bit *= 2
-    inverse, upper = factored(side, member, mine, other, modes, total)
-    sums, inverse = lax.optimization_barrier((sums, inverse))
-    if bit < slabs:
-        sums = sums + swap(sums, "gx", bit)
-    new_modes = solved_modes(inverse, rows)
-    new_mode, factor = finish(inverse, upper, sums, fresh, rows, total)
+    hopped = swap_by_side(sums, ways[1][1])
+    sums = sums + hopped
+    early, early_upper = early_panels(side, member, beside, mine, other, modes, total)
+    sums, early = lax.optimization_barrier((sums, early))
+    sums = sums + swap(sums, "gy", 1)
+    inverse, new_modes, factor = late_panels(early, early_upper, rows)
+    new_mode, factor = finish(inverse, sums, fresh, rows, factor, total)
     return (new_modes.reshape(basis.shape), new_mode.reshape(basis.shape[:-1]), factor)
 
 
 def solution(mesh):
     in_specs = (P(None, "gx", "gy", None), P(None, "gx", "gy", None, None), P())
     out_specs = (P(None, "gx", "gy", None, None), P(None, "gx", "gy", None), P())
+
     return jax.shard_map(local, mesh=mesh, in_specs=in_specs, out_specs=out_specs, check_vma=False)

time: 56.5 us -> 56.6 us (level)
  Pallas kernels: 22.8 us -> 21 us
  waiting for transfers between devices: 16.5 us -> 17.7 us
  starting transfers between devices: 16 us -> 16.7 us
    ppermute x0 -> x11, waiting for transfers between devices: none -> 16.8 us  [swap_by_side(): return lax.ppermute(block, ('gx', 'gy'), pairs)]
    ppermute x0 -> x11, starting transfers between devices: none -> 16 us  [swap_by_side(): return lax.ppermute(block, ('gx', 'gy'), pairs)]
    ppermute x14 -> x4, waiting for transfers between devices: 16.5 us -> 0.91 us  [swap(): lax.ppermute(block, axis, [(i, i ^ step) for i in range(lax.axis_size(axi...]
    ppermute x14 -> x4, starting transfers between devices: 16 us -> 0.76 us  [swap(): lax.ppermute(block, axis, [(i, i ^ step) for i in range(lax.axis_size(axi...]
    pallas_call x4, Pallas kernels: 21.5 us -> 19.7 us  [the longest x1 8.96 us: late_panels(): pl.pallas_call(late_kernel, out_shape=(jax.ShapeDtypeStruct((modes, modes...]
  transfers between devices with their start and end apart: 14 -> 15, of which waited for: 9 -> 10; matrix products, arithmetic and copies ran while one was open for 0% -> 0% of each run, Pallas kernels for 32% -> 18%
where the time goes in v5:
time: 56.6 us; the launch traced here: 56.5 us
  Pallas kernels  21 us (37%)
  waiting for transfers between devices  17.7 us (31%)
  starting transfers between devices  16.7 us (30%)
  between operations  0.85 us (2%)
    ppermute x11, waiting for transfers between devices, swap_by_side(): return lax.ppermute(block, ('gx', 'gy'), pairs)  16.8 us
    ppermute x11, starting transfers between devices, swap_by_side(): return lax.ppermute(block, ('gx', 'gy'), pairs)  16 us
    pallas_call x1, Pallas kernels, late_panels(): pl.pallas_call(late_kernel, out_shape=(jax.ShapeDtypeStruct((modes, modes...  8.96 us
    pallas_call x1, Pallas kernels, early_panels(): pl.pallas_call(lambda *refs: early_kernel(*refs, total=total), out_shape=...  7.55 us
    pallas_call x1, Pallas kernels, local_filter(): pl.pallas_call(lambda *refs: filter_kernel(*refs, cells_x=cells_x, cells_...  2.1 us
  transfers between devices with their start and end apart: 15, of which 10 were waited for; matrix products, arithmetic and copies ran while one was open for 0% of the time, Pallas kernels for 18%

profile of v5, /device:TPU:0, one launch (start us, length us, event | category | flops | bytes accessed | tf_op | source)
XLA Modules:
  0.0 56.5 jit_solution(15245185033381135815)
XLA Ops:
  0.6 2.1 %filter.1 = f32[72,128]{1,0:T(8,128)S(1)} custom-call(bf16[3,17]{1,0:T(4,128)(2,1)} %refs_0_.1, bf16[384,1024]{1,0:T(8,128)(2,1)} %bitcast.28), custom_call_target="tpu_custom_call" | custom-call | flops 201326592 | bytes 786432 | tf_op jit(solution)/shard_map/filter/pallas_call | solution.py:157
  2.8 0.6 collective-permute-start
  3.9 0.6 %gram.2 = f32[576,128]{1,0:T(8,128)S(1)} custom-call(s32[1]{0:T(128)} %bitcast.1.side_ref.refs_0_, bf16[768,512]{1,0:T(8,128)(2,1)S(1)} %bitcast.22), custom_call_target="tpu_custom_call" | custom-call | flops 113246208 | bytes 294912 | tf_op jit(solution)/shard_map/gram/pallas_call | solution.py:88
  4.5 0.9 %collective-permute-done.1 = f32[576,128]{1,0:T(8,128)S(1)} collective-permute-done((f32[576,128]{1,0:T(8,128)S(1)}, f32[576,128]{1,0:T(8,128)S(1)}, u32[]{:S(2)}, u32[]{:S(2)}) %collective-permute-start.1) | collective-permute-done | bytes 294944 | tf_op jit(solution)/shard_map/ppermute | solution.py:18
  5.5 3.6 %collective-permute-start.4 = (f32[152,128]{1,0:T(8,128)S(1)}, f32[152,128]{1,0:T(8,128)S(1)}, u32[]{:S(2)}, u32[]{:S(2)}) collective-permute-start(f32[152,128]{1,0:T(8,128)S(1)} %pad_maximum_fusion.2), channel_id=1, source_target_pairs={{0,6},{1,25},{2,4},{3,27},{4,2},{5,29},{6,0},{7,31},{8,14},{9,17},... | collective-permute-start | bytes 233480 | tf_op jit(solution)/shard_map/ppermute | solution.py:26
  9.8 4.2 %collective-permute-done.3 = f32[144,128]{1,0:T(8,128)S(1)} collective-permute-done((f32[144,128]{1,0:T(8,128)S(1)}, f32[144,128]{1,0:T(8,128)S(1)}, u32[]{:S(2)}, u32[]{:S(2)}) %collective-permute-start.3) | collective-permute-done | bytes 73760 | tf_op jit(solution)/shard_map/ppermute | solution.py:26
  14.1 3.7 %collective-permute-start.6 = (f32[152,128]{1,0:T(8,128)S(1)}, f32[152,128]{1,0:T(8,128)S(1)}, u32[]{:S(2)}, u32[]{:S(2)}) collective-permute-start(f32[152,128]{1,0:T(8,128)S(1)} %get-tuple-element.39), channel_id=1, source_target_pairs={{0,24},{1,7},{2,26},{3,5},{4,28},{5,3},{6,30},{7,1},{8,16},{9,15},... | collective-permute-start | bytes 233480 | tf_op jit(solution)/shard_map/ppermute | solution.py:26
  17.7 0.8 %collective-permute-start.7 = (f32[144,128]{1,0:T(8,128)S(1)}, f32[144,128]{1,0:T(8,128)S(1)}, u32[]{:S(2)}, u32[]{:S(2)}) collective-permute-start(f32[144,128]{1,0:T(8,128)S(1)} %slice_add_fusion.2), channel_id=1, source_target_pairs={{0,16},{1,5},{2,18},{3,7},{4,20},{5,1},{6,22},{7,3},{8,24},{9,13},... | collective-permute-start | bytes 221192 | tf_op jit(solution)/shard_map/ppermute | solution.py:26
  18.5 1.9 %collective-permute-done.6 = f32[152,128]{1,0:T(8,128)S(1)} collective-permute-done((f32[152,128]{1,0:T(8,128)S(1)}, f32[152,128]{1,0:T(8,128)S(1)}, u32[]{:S(2)}, u32[]{:S(2)}) %collective-permute-start.6) | collective-permute-done | bytes 77856 | tf_op jit(solution)/shard_map/ppermute | solution.py:26
  20.4 1.8 %collective-permute-done.5 = f32[152,128]{1,0:T(8,128)S(1)} collective-permute-done((f32[152,128]{1,0:T(8,128)S(1)}, f32[152,128]{1,0:T(8,128)S(1)}, u32[]{:S(2)}, u32[]{:S(2)}) %collective-permute-start.5) | collective-permute-done | bytes 77856 | tf_op jit(solution)/shard_map/ppermute | solution.py:26
  22.4 0.6 %collective-permute-done.7 = f32[144,128]{1,0:T(8,128)S(1)} collective-permute-done((f32[144,128]{1,0:T(8,128)S(1)}, f32[144,128]{1,0:T(8,128)S(1)}, u32[]{:S(2)}, u32[]{:S(2)}) %collective-permute-start.7) | collective-permute-done | bytes 73760 | tf_op jit(solution)/shard_map/ppermute | solution.py:26
  23.0 1.5 %collective-permute-start.10 = (f32[152,128]{1,0:T(8,128)S(1)}, f32[152,128]{1,0:T(8,128)S(1)}, u32[]{:S(2)}, u32[]{:S(2)}) collective-permute-start(f32[152,128]{1,0:T(8,128)S(1)} %pad_maximum_fusion.5), channel_id=1, source_target_pairs={{0,6},{1,25},{2,4},{3,27},{4,2},{5,29},{6,0},{7,31},{8,14},{9,17},... | collective-permute-start | bytes 233480 | tf_op jit(solution)/shard_map/ppermute | solution.py:26
  24.5 1.5 %collective-permute-start.9 = (f32[152,128]{1,0:T(8,128)S(1)}, f32[152,128]{1,0:T(8,128)S(1)}, u32[]{:S(2)}, u32[]{:S(2)}) collective-permute-start(f32[152,128]{1,0:T(8,128)S(1)} %pad_maximum_fusion.5), channel_id=1, source_target_pairs={{0,4},{1,17},{2,6},{3,19},{4,0},{5,21},{6,2},{7,23},{8,12},{9,25},... | collective-permute-start | bytes 233480 | tf_op jit(solution)/shard_map/ppermute | solution.py:26
  26.0 0.5 collective-permute-start.8
  26.6 1.8 %collective-permute-done.10 = f32[152,128]{1,0:T(8,128)S(1)} collective-permute-done((f32[152,128]{1,0:T(8,128)S(1)}, f32[152,128]{1,0:T(8,128)S(1)}, u32[]{:S(2)}, u32[]{:S(2)}) %collective-permute-start.10) | collective-permute-done | bytes 77856 | tf_op jit(solution)/shard_map/ppermute | solution.py:26
  28.4 0.8 %collective-permute-done.9 = f32[152,128]{1,0:T(8,128)S(1)} collective-permute-done((f32[152,128]{1,0:T(8,128)S(1)}, f32[152,128]{1,0:T(8,128)S(1)}, u32[]{:S(2)}, u32[]{:S(2)}) %collective-permute-start.9) | collective-permute-done | bytes 77856 | tf_op jit(solution)/shard_map/ppermute | solution.py:26
  29.2 1.2 %collective-permute-done.8 = f32[152,128]{1,0:T(8,128)S(1)} collective-permute-done((f32[152,128]{1,0:T(8,128)S(1)}, f32[152,128]{1,0:T(8,128)S(1)}, u32[]{:S(2)}, u32[]{:S(2)}) %collective-permute-start.8) | collective-permute-done | bytes 77856 | tf_op jit(solution)/shard_map/ppermute | solution.py:26
  30.6 2.1 %collective-permute-start.11 = (f32[8,128]{1,0:T(8,128)S(1)}, f32[8,128]{1,0:T(8,128)S(1)}, u32[]{:S(2)}, u32[]{:S(2)}) collective-permute-start(f32[8,128]{1,0:T(8,128)S(1)} %slice_add_fusion.5), channel_id=1, source_target_pairs={{0,8},{1,3},{2,10},{3,1},{4,12},{5,7},{6,14},{7,5},{8,0},{9,11},{1... | collective-permute-start | bytes 12296 | tf_op jit(solution)/shard_map/ppermute | solution.py:26
  32.7 1.6 %collective-permute-done.11 = f32[8,128]{1,0:T(8,128)S(1)} collective-permute-done((f32[8,128]{1,0:T(8,128)S(1)}, f32[8,128]{1,0:T(8,128)S(1)}, u32[]{:S(2)}, u32[]{:S(2)}) %collective-permute-start.11) | collective-permute-done | bytes 4128 | tf_op jit(solution)/shard_map/ppermute | solution.py:26
  34.2 1.7 %collective-permute-start.12 = (f32[8,128]{1,0:T(8,128)S(1)}, f32[8,128]{1,0:T(8,128)S(1)}, u32[]{:S(2)}, u32[]{:S(2)}) collective-permute-start(f32[8,128]{1,0:T(8,128)S(1)} %add.75), channel_id=1, source_target_pairs={{0,16},{1,5},{2,18},{3,7},{4,20},{5,1},{6,22},{7,3},{8,24},{9,13},... | collective-permute-start | bytes 12296 | tf_op jit(solution)/shard_map/ppermute | solution.py:26
  35.9 2.8 %collective-permute-done.12 = f32[8,128]{1,0:T(8,128)S(1)} collective-permute-done((f32[8,128]{1,0:T(8,128)S(1)}, f32[8,128]{1,0:T(8,128)S(1)}, u32[]{:S(2)}, u32[]{:S(2)}) %collective-permute-start.12) | collective-permute-done | bytes 4128 | tf_op jit(solution)/shard_map/ppermute | solution.py:26
  38.8 7.5 %early.1 = (f32[512,512]{1,0:T(8,128)S(1)}, f32[256,512]{1,0:T(8,128)S(1)}) custom-call(s32[1]{0:T(128)} %bitcast.1.side_ref.refs_0_, s32[1]{0:T(128)} %bitcast.9.refs_1_, s32[1]{0:T(128)} %bitcast.10.refs_2_, f32[576,128]{1,0:T(8,128)S(1)} %pad_maximum_fusion.refs_3_, f32[576,128]{1,0:T(8,128)S(1)} %collective-permute-done.13.refs_4_), custom_call_target="tpu_custom_call" | custom-call | flops 2147483648 | bytes 2097152 | tf_op jit(solution)/shard_map/early/pallas_call | solution.py:376
  46.4 9.0 %late.1 = (f32[512,512]{1,0:T(8,128)S(1)}, bf16[768,512]{1,0:T(8,128)(2,1)}, f32[513,513]{1,0:T(8,128)}) custom-call(f32[512,512]{1,0:T(8,128)S(1)} %get-tuple-element.20.early_ref, f32[256,512]{1,0:T(8,128)S(1)} %get-tuple-element.21.early_upper_ref, bf16[768,512]{1,0:T(8,128)(2,1)S(1)} %bitcast.24), custom_call_target="tpu_custom_call" | custom-call | flops 2147483648 | bytes 2097152 | tf_op jit(solution)/shard_map/late/pallas_call | solution.py:428
  55.4 1.1 %finish.1 = (f32[1,768]{1,0:T(1,128)}, f32[513,513]{1,0:T(8,128)}) custom-call(f32[512,512]{1,0:T(8,128)S(1)} %get-tuple-element.23.refs_0_, f32[8,128]{1,0:T(8,128)S(1)} %add.77.refs_1_, f32[6,128]{1,0:T(8,128)S(1)} %get-tuple-element.25.refs_2_, bf16[768,512]{1,0:T(8,128)(2,1)S(1)} %bitcast.25, ...), custom_call_target="tpu_custom_call", output_to_operand_aliasing={{1}: (4, {})} | custom-call | flops 16777216 | bytes 1048576 | tf_op jit(solution)/shard_map/finish/pallas_call | solution.py:484
  (36 shorter events, 1.8 us)
Async XLA Ops:
  0.6 2.7 %copy-start = (bf16[3,1,2,128,512]{4,3,2,1,0:T(8,128)(2,1)S(1)}, bf16[3,1,2,128,512]{4,3,2,1,0:T(8,128)(2,1)}, u32[]{:S(2)}) copy-start(bf16[3,1,2,128,512]{4,3,2,1,0:T(8,128)(2,1)} %param.4) | copy-start | bytes 2359300
  2.8 1.7 %collective-permute-start = (f32[24,128]{1,0:T(8,128)S(1)}, f32[24,128]{1,0:T(8,128)S(1)}, u32[]{:S(2)}, u32[]{:S(2)}) collective-permute-start(f32[24,128]{1,0:T(8,128)S(1)} %slice_select_fusion), channel_id=1, source_target_pairs={{0,1},{1,0},{2,3},{3,2},{4,5},{5,4},{6,7},{7,6},{8,9},{9,8},{10,11... | collective-permute-start | bytes 36872 | tf_op jit(solution)/shard_map/ppermute | solution.py:18
  3.8 1.6 %collective-permute-start.1 = (f32[576,128]{1,0:T(8,128)S(1)}, f32[576,128]{1,0:T(8,128)S(1)}, u32[]{:S(2)}, u32[]{:S(2)}) collective-permute-start(f32[576,128]{1,0:T(8,128)S(1)} %gram.3), channel_id=1, source_target_pairs={{0,1},{1,0},{2,3},{3,2},{4,5},{5,4},{6,7},{7,6},{8,9},{9,8},{10,11... | collective-permute-start | bytes 884744 | tf_op jit(solution)/shard_map/ppermute | solution.py:18
  5.5 8.5 %collective-permute-start.4 = (f32[152,128]{1,0:T(8,128)S(1)}, f32[152,128]{1,0:T(8,128)S(1)}, u32[]{:S(2)}, u32[]{:S(2)}) collective-permute-start(f32[152,128]{1,0:T(8,128)S(1)} %pad_maximum_fusion.2), channel_id=1, source_target_pairs={{0,6},{1,25},{2,4},{3,27},{4,2},{5,29},{6,0},{7,31},{8,14},{9,17},... | collective-permute-start | bytes 233480 | tf_op jit(solution)/shard_map/ppermute | solution.py:26
  9.1 4.9 %collective-permute-start.2 = (f32[152,128]{1,0:T(8,128)S(1)}, f32[152,128]{1,0:T(8,128)S(1)}, u32[]{:S(2)}, u32[]{:S(2)}) collective-permute-start(f32[152,128]{1,0:T(8,128)S(1)} %pad_maximum_fusion.1), channel_id=1, source_target_pairs={{0,2},{1,9},{2,0},{3,11},{4,6},{5,13},{6,4},{7,15},{8,10},{9,1},{1... | collective-permute-start | bytes 233480 | tf_op jit(solution)/shard_map/ppermute | solution.py:26
  9.6 4.4 %collective-permute-start.3 = (f32[144,128]{1,0:T(8,128)S(1)}, f32[144,128]{1,0:T(8,128)S(1)}, u32[]{:S(2)}, u32[]{:S(2)}) collective-permute-start(f32[144,128]{1,0:T(8,128)S(1)} %get-tuple-element.34), channel_id=1, source_target_pairs={{0,4},{1,17},{2,6},{3,19},{4,0},{5,21},{6,2},{7,23},{8,12},{9,25},... | collective-permute-start | bytes 221192 | tf_op jit(solution)/shard_map/ppermute | solution.py:26
  14.1 6.3 %collective-permute-start.6 = (f32[152,128]{1,0:T(8,128)S(1)}, f32[152,128]{1,0:T(8,128)S(1)}, u32[]{:S(2)}, u32[]{:S(2)}) collective-permute-start(f32[152,128]{1,0:T(8,128)S(1)} %get-tuple-element.39), channel_id=1, source_target_pairs={{0,24},{1,7},{2,26},{3,5},{4,28},{5,3},{6,30},{7,1},{8,16},{9,15},... | collective-permute-start | bytes 233480 | tf_op jit(solution)/shard_map/ppermute | solution.py:26
  17.7 4.4 %collective-permute-start.5 = (f32[152,128]{1,0:T(8,128)S(1)}, f32[152,128]{1,0:T(8,128)S(1)}, u32[]{:S(2)}, u32[]{:S(2)}) collective-permute-start(f32[152,128]{1,0:T(8,128)S(1)} %get-tuple-element.40), channel_id=1, source_target_pairs={{0,8},{1,3},{2,10},{3,1},{4,12},{5,7},{6,14},{7,5},{8,0},{9,11},{1... | collective-permute-start | bytes 233480 | tf_op jit(solution)/shard_map/ppermute | solution.py:26
  17.7 5.3 %collective-permute-start.7 = (f32[144,128]{1,0:T(8,128)S(1)}, f32[144,128]{1,0:T(8,128)S(1)}, u32[]{:S(2)}, u32[]{:S(2)}) collective-permute-start(f32[144,128]{1,0:T(8,128)S(1)} %slice_add_fusion.2), channel_id=1, source_target_pairs={{0,16},{1,5},{2,18},{3,7},{4,20},{5,1},{6,22},{7,3},{8,24},{9,13},... | collective-permute-start | bytes 221192 | tf_op jit(solution)/shard_map/ppermute | solution.py:26
  23.0 5.4 %collective-permute-start.10 = (f32[152,128]{1,0:T(8,128)S(1)}, f32[152,128]{1,0:T(8,128)S(1)}, u32[]{:S(2)}, u32[]{:S(2)}) collective-permute-start(f32[152,128]{1,0:T(8,128)S(1)} %pad_maximum_fusion.5), channel_id=1, source_target_pairs={{0,6},{1,25},{2,4},{3,27},{4,2},{5,29},{6,0},{7,31},{8,14},{9,17},... | collective-permute-start | bytes 233480 | tf_op jit(solution)/shard_map/ppermute | solution.py:26
  24.5 4.7 %collective-permute-start.9 = (f32[152,128]{1,0:T(8,128)S(1)}, f32[152,128]{1,0:T(8,128)S(1)}, u32[]{:S(2)}, u32[]{:S(2)}) collective-permute-start(f32[152,128]{1,0:T(8,128)S(1)} %pad_maximum_fusion.5), channel_id=1, source_target_pairs={{0,4},{1,17},{2,6},{3,19},{4,0},{5,21},{6,2},{7,23},{8,12},{9,25},... | collective-permute-start | bytes 233480 | tf_op jit(solution)/shard_map/ppermute | solution.py:26
  26.0 4.4 %collective-permute-start.8 = (f32[152,128]{1,0:T(8,128)S(1)}, f32[152,128]{1,0:T(8,128)S(1)}, u32[]{:S(2)}, u32[]{:S(2)}) collective-permute-start(f32[152,128]{1,0:T(8,128)S(1)} %pad_maximum_fusion.5), channel_id=1, source_target_pairs={{0,2},{1,9},{2,0},{3,11},{4,6},{5,13},{6,4},{7,15},{8,10},{9,1},{1... | collective-permute-start | bytes 233480 | tf_op jit(solution)/shard_map/ppermute | solution.py:26
  30.5 8.3 %collective-permute-start.13 = (f32[576,128]{1,0:T(8,128)S(1)}, f32[576,128]{1,0:T(8,128)S(1)}, u32[]{:S(2)}, u32[]{:S(2)}) collective-permute-start(f32[576,128]{1,0:T(8,128)S(1)} %pad_maximum_fusion.refs_3_), channel_id=1, source_target_pairs={{0,1},{1,0},{2,3},{3,2},{4,5},{5,4},{6,7},{7,6},{8,9},{9,8},{10,11... | collective-permute-start | bytes 884744 | tf_op jit(solution)/shard_map/ppermute | solution.py:18
  30.6 3.7 %collective-permute-start.11 = (f32[8,128]{1,0:T(8,128)S(1)}, f32[8,128]{1,0:T(8,128)S(1)}, u32[]{:S(2)}, u32[]{:S(2)}) collective-permute-start(f32[8,128]{1,0:T(8,128)S(1)} %slice_add_fusion.5), channel_id=1, source_target_pairs={{0,8},{1,3},{2,10},{3,1},{4,12},{5,7},{6,14},{7,5},{8,0},{9,11},{1... | collective-permute-start | bytes 12296 | tf_op jit(solution)/shard_map/ppermute | solution.py:26
  34.2 4.5 %collective-permute-start.12 = (f32[8,128]{1,0:T(8,128)S(1)}, f32[8,128]{1,0:T(8,128)S(1)}, u32[]{:S(2)}, u32[]{:S(2)}) collective-permute-start(f32[8,128]{1,0:T(8,128)S(1)} %add.75), channel_id=1, source_target_pairs={{0,16},{1,5},{2,18},{3,7},{4,20},{5,1},{6,22},{7,3},{8,24},{9,13},... | collective-permute-start | bytes 12296 | tf_op jit(solution)/shard_map/ppermute | solution.py:26
  46.3 9.1 %collective-permute-start.14 = (f32[8,128]{1,0:T(8,128)S(1)}, f32[8,128]{1,0:T(8,128)S(1)}, u32[]{:S(2)}, u32[]{:S(2)}) collective-permute-start(f32[8,128]{1,0:T(8,128)S(1)} %add.76), channel_id=1, source_target_pairs={{0,1},{1,0},{2,3},{3,2},{4,5},{5,4},{6,7},{7,6},{8,9},{9,8},{10,11... | collective-permute-start | bytes 12296 | tf_op jit(solution)/shard_map/ppermute | solution.py:18
